TPU v7x, 32 devices: a whole 2x2x4 slice. The times are simulated.
32 devices in a mesh: gx: 2 (over x), gy: 4 (over z), gz: 4 (over y, core).
Axes of the slice: x: 2, y: 2, z: 4, core: 2. Of those that a mesh axis runs over, the one named last changes fastest.
Arguments:
- density: float32 [4, 32, 96, 256], P('gz', 'gy', None, 'gx'), may hold values from 0.2 to 1
- bone: int32 [4, 32, 96, 256], P('gz', 'gy', None, 'gx'), may hold values 0 or 1
- fixed: int32 [4, 32, 96, 256], P('gz', 'gy', None, 'gx'), may hold values 0 or 1
- load: float32 [3, 4, 32, 96, 256], P(None, 'gz', 'gy', None, 'gx'), may hold values from -6 to 6
Outputs:
- density_new: float32 [4, 32, 96, 256], P('gz', 'gy', None, 'gx')
- displacement: float32 [3, 4, 32, 96, 256], P(None, 'gz', 'gy', None, 'gx')
All inputs are finite; a program needn't handle non-finite values. No bound on the sum of `bone` or of `fixed` on one device may be relied on, other than what follows from the above.
Results may differ from a plain program's by a relative error of at most 0.00024.
Values sent between devices are 32-bit elements; how exact they have to be, the bound alone decides.
No kernel may reach another device: no remote copies, remote signals or barrier semaphores. Data moves between devices by JAX's collectives and lax.ppermute only.
A program may use at most 64 MiB of HBM per device.

v0:
```python
import math

import jax
import jax.numpy as jnp
import numpy as np
from jax import lax
from jax.sharding import PartitionSpec as P

RAD = 24
ITERS = 2


MARROW = 0.1
REMODEL = 0.25
FLOOR = 0.2
CEILING = 1.0
EPSILON = 1e-06


def shifted(value, axis, steps):
    count = lax.axis_size(axis)
    initial, last = (max(0, -steps), min(count, count - steps))
    return lax.ppermute(value, axis, [(source, source + steps) for source in range(initial, last)])


def from_behind(block, axis, distance):
    devices = range(lax.axis_size(axis))
    route = [((i - distance) % len(devices), i) for i in devices]
    return lax.ppermute(block, axis, route)


def extended(block, sides, width):
    for axis, dim in sides:
        count = lax.axis_size(axis)
        forward = [(i, i + 1) for i in range(count - 1)]
        backward = [(target, source) for source, target in forward]
        low = lax.ppermute(
            lax.slice_in_dim(block, block.shape[dim] - width, None, axis=dim), axis, forward
        )
        high = lax.ppermute(lax.slice_in_dim(block, 0, width, axis=dim), axis, backward)
        block = jnp.concatenate([low, block, high], axis=dim)
    return block


def element_stiffness():
    poisson = 0.3
    lame = poisson / ((1.0 + poisson) * (1.0 - 2.0 * poisson))
    shear = 0.5 / (1.0 + poisson)
    elastic = np.zeros((6, 6))
    elastic[:3, :3] = lame
    for index in range(3):
        elastic[index, index] += 2.0 * shear
        elastic[index + 3, index + 3] = shear
    points = [0.5 - 0.5 / math.sqrt(3.0), 0.5 + 0.5 / math.sqrt(3.0)]
    matrix = np.zeros((24, 24))
    for point_z in points:
        for point_y in points:
            for point_x in points:
                strain = np.zeros((6, 24))
                for corner_z in range(2):
                    for corner_y in range(2):
                        for corner_x in range(2):
                            node = 4 * corner_z + 2 * corner_y + corner_x
                            shape_x = point_x if corner_x else 1.0 - point_x
                            shape_y = point_y if corner_y else 1.0 - point_y
                            shape_z = point_z if corner_z else 1.0 - point_z
                            slope_x = 1.0 if corner_x else -1.0
                            slope_y = 1.0 if corner_y else -1.0
                            slope_z = 1.0 if corner_z else -1.0
                            along_x = slope_x * shape_y * shape_z
                            along_y = shape_x * slope_y * shape_z
                            along_z = shape_x * shape_y * slope_z
                            strain[0, node] = along_x
                            strain[1, 8 + node] = along_y
                            strain[2, 16 + node] = along_z
                            strain[3, node] = along_y
                            strain[3, 8 + node] = along_x
                            strain[4, 8 + node] = along_z
                            strain[4, 16 + node] = along_y
                            strain[5, node] = along_z
                            strain[5, 16 + node] = along_x
                matrix = matrix + strain.T @ elastic @ strain / 8.0
    return matrix


def corners():
    return [
        (corner_z, corner_y, corner_x)
        for corner_z in range(2)
        for corner_y in range(2)
        for corner_x in range(2)
    ]


def corner_values(nodes, depth, height, width):
    values = []
    for component in range(3):
        for cz, cy, cx in corners():
            values.append(nodes[component, cz : cz + depth, cy : cy + height, cx : cx + width])
    return values


def element_rows(values, table):
    products = []
    for row in range(24):
        total = values[0] * float(table[row, 0])
        for column in range(1, 24):
            total = total + values[column] * float(table[row, column])
        products.append(total)
    return products


def lean_forces(nodes, moduli, table):
    depth, height, width = moduli.shape
    products = element_rows(corner_values(nodes, depth, height, width), table)
    components = []
    for component in range(3):
        total = jnp.zeros((depth + 1, height + 1, width + 1), jnp.float32)
        for node, (cz, cy, cx) in enumerate(corners()):
            term = moduli * products[component * 8 + node]
            total = total + jnp.pad(term, ((cz, 1 - cz), (cy, 1 - cy), (cx, 1 - cx)))
        components.append(total)
    return jnp.stack(components, axis=0)


def lean_energy(nodes, moduli, table):
    depth, height, width = moduli.shape
    values = corner_values(nodes, depth, height, width)
    products = element_rows(values, table)
    total = values[0] * products[0]
    for row in range(1, 24):
        total = total + values[row] * products[row]
    return 0.5 * moduli * total


def stiffness_diagonal(moduli_ext, stiffness, depth, height, width):
    main = jnp.diagonal(stiffness).reshape(3, 8)
    total = jnp.zeros((3, depth, height, width), jnp.float32)
    for node, (cz, cy, cx) in enumerate(corners()):
        piece = moduli_ext[
            1 - cz : 1 - cz + depth, 1 - cy : 1 - cy + height, 1 - cx : 1 - cx + width
        ]
        total = total + main[:, node][:, None, None, None] * piece[None]
    return total


def banded(length_in, length_out, radius):
    offsets = jnp.arange(2 * radius + 1).astype(jnp.float32) - radius
    normal = jnp.sum(jnp.exp(-jnp.abs(offsets) / (0.5 * radius)))
    inputs = jnp.arange(length_in)[:, None]
    outputs = jnp.arange(length_out)[None, :]
    distance = (inputs - (length_in - length_out) // 2 - outputs).astype(jnp.float32)
    weight = jnp.exp(-jnp.abs(distance) / (0.5 * radius)) / normal
    return jnp.where(jnp.abs(distance) <= radius, weight, 0.0)


def smooth(values, axis, length_out):
    matrix = banded(values.shape[axis], length_out, RAD)
    if axis == 2:
        return jnp.einsum("zyi,io->zyo", values, matrix, precision=lax.Precision.HIGHEST)
    if axis == 1:
        return jnp.einsum("zix,io->zox", values, matrix, precision=lax.Precision.HIGHEST)
    return jnp.einsum("iyx,io->oyx", values, matrix, precision=lax.Precision.HIGHEST)


def upper_nodes(field):
    column = shifted(field[:, :, :, :1], "gx", -1)
    wide = jnp.concatenate([field, column], axis=3)
    inner = from_behind(wide[:, :1], "gy", -1)
    outer = shifted(inner, "gz", -1)
    position = lax.axis_index("gy")
    upper = jnp.where(position == lax.axis_size("gy") - 1, outer, inner)
    return jnp.concatenate([wide, upper], axis=1)


def fold_upper(values):
    depth = values.shape[1] - 1
    width = values.shape[3] - 1
    inner = from_behind(values[:, depth:], "gy", 1)
    outer = shifted(inner, "gz", 1)
    position = lax.axis_index("gy")
    carried = jnp.where(position == 0, outer, inner)
    values = jnp.concatenate([values[:, :1] + carried, values[:, 1:depth]], axis=1)
    column = shifted(values[:, :, :, width:], "gx", 1)
    return jnp.concatenate([values[:, :, :, :1] + column, values[:, :, :, 1:width]], axis=3)


def node_forces(field, modulus, table):
    height = field.shape[2]
    nodes = jnp.pad(upper_nodes(field), ((0, 0), (0, 0), (0, 1), (0, 0)))
    forces = lean_forces(nodes, modulus, table)
    return fold_upper(forces[:, :, :height])


def local_energy(solution, modulus, table):
    nodes = jnp.pad(upper_nodes(solution), ((0, 0), (0, 0), (0, 1), (0, 0)))
    return lean_energy(nodes, modulus, table)


def inner_sum(values):
    return lax.psum(jnp.sum(values), ("gx", "gy", "gz"))


def to_bricks(values):
    return lax.all_to_all(values, "gy", split_axis=2, concat_axis=1, tiled=True)


def to_slabs(values):
    return lax.all_to_all(values, "gy", split_axis=1, concat_axis=2, tiled=True)


def on_device(density, bone, fixed, load):
    table = element_stiffness()
    stiffness = jnp.asarray(table, jnp.float32)
    local_density = density[0]
    bone_share = bone[0].astype(jnp.float32)
    free_nodes = 1.0 - fixed[0].astype(jnp.float32)
    modulus = bone_share * local_density * local_density + (1.0 - bone_share) * MARROW
    depth, height, width = local_density.shape
    moduli_ext = jnp.pad(modulus, ((1, 1), (1, 0), (1, 1)))
    diagonal_part = stiffness_diagonal(moduli_ext, stiffness, depth + 1, height, width + 1)
    precondition = free_nodes / fold_upper(diagonal_part)
    residual = free_nodes * load[:, 0]
    solution = jnp.zeros_like(residual)
    search = precondition * residual
    gamma = inner_sum(residual * search)
    for count in range(ITERS):
        image = free_nodes * node_forces(free_nodes * search, modulus, table)
        alpha = gamma / lax.psum(jnp.sum(search * image), ("gx", "gy", "gz"))
        solution = solution + alpha * search
        if count + 1 < ITERS:
            residual = residual - alpha * image
            scaled = precondition * residual
            gamma_next = inner_sum(residual * scaled)
            search = scaled + gamma_next / gamma * search
            gamma = gamma_next
    energy = local_energy(solution, modulus, table)
    specific = energy / local_density
    sideways = extended(specific, (("gx", 2),), RAD)
    planar = smooth(smooth(sideways, 2, width), 1, height)
    brick = to_bricks(planar[None])[0]
    deep = extended(brick, (("gz", 0),), RAD)
    stimulus = smooth(deep, 0, brick.shape[0])
    total = lax.psum(jnp.sum(stimulus), ("gx", "gy", "gz"))
    cells = stimulus.size * lax.axis_size("gx") * lax.axis_size("gy") * lax.axis_size("gz")
    mean = total / cells
    returned = to_slabs(stimulus[None])[0]
    updated = local_density + REMODEL * bone_share * (returned / (mean + EPSILON) - 1.0)
    updated = jnp.clip(updated, FLOOR, CEILING)
    return (updated[None], solution[:, None])


def solution(mesh):
    placed = (
        P("gz", "gy", None, "gx"),
        P("gz", "gy", None, "gx"),
        P("gz", "gy", None, "gx"),
        P(None, "gz", "gy", None, "gx"),
    )
    return jax.shard_map(
        on_device,
        mesh=mesh,
        in_specs=placed,
        out_specs=(P("gz", "gy", None, "gx"), P(None, "gz", "gy", None, "gx")),
        check_vma=False,
    )
```

profile of v0, /device:TPU:0, one launch (start us, length us, event | category | flops | bytes accessed | tf_op | source)
XLA Modules:
  0.0 470.6 jit_solution(395824094293059541)
XLA Ops:
  3.4 2.3 pad_slice_fusion.25
  6.8 2.8 multiply_add_fusion
  9.7 3.1 collective-permute-start
  13.2 3.2 copy.83
  16.3 3.7 collective-permute-done
  23.4 3.5 collective-permute-start.2
  31.3 4.3 collective-permute-done.3
  37.4 5.4 %collective-permute-done.4 = f32[3,1,96,129]{2,3,1,0:T(8,128)S(1)} collective-permute-done((f32[3,1,96,129]{2,3,1,0:T(8,128)S(1)}, f32[3,1,96,129]{2,3,1,0:T(8,128)S(1)}, u32[]{:S(2)}, u32[]{:S(2)}) %collective-permute-start.4) | collective-permute-done | bytes 148640 | tf_op jit(solution)/shard_map/ppermute | solution.py:29
  44.0 2.3 collective-permute-done.5
  46.5 2.6 fusion.232
  59.9 2.3 fusion.225
  93.3 7.6 %collective-permute-done.6 = f32[3,1,96,129]{2,3,1,0:T(8,128)S(1)} collective-permute-done((f32[3,1,96,129]{2,3,1,0:T(8,128)S(1)}, f32[3,1,96,129]{2,3,1,0:T(8,128)S(1)}, u32[]{:S(2)}, u32[]{:S(2)}) %collective-permute-start.6) | collective-permute-done | bytes 148640 | tf_op jit(solution)/shard_map/ppermute | solution.py:29
  100.9 7.6 %collective-permute-start.7 = (f32[3,1,96,129]{2,3,1,0:T(8,128)S(1)}, f32[3,1,96,129]{2,3,1,0:T(8,128)S(1)}, u32[]{:S(2)}, u32[]{:S(2)}) collective-permute-start(f32[3,1,96,129]{2,3,1,0:T(8,128)S(1)} %collective-permute-done.6), channel_id=1, source_target_pairs={{0,1},{1,2},{2,3},{4,5},{5,6},{6,7},{8,9},{9,10},{10,11},{12,13},{... | collective-permute-start | bytes 445832 | tf_op jit(solution)/shard_map/ppermute | solution.py:23
  114.6 42.5 %all-reduce.52 = (f32[]{:T(128)}, f32[]{:T(128)}) all-reduce(f32[]{:T(128)} %get-tuple-element.11, f32[]{:T(128)} %get-tuple-element.10), channel_id=1, replica_groups=mesh['gx'=2,'gy'=4,'gz'=4] {'gx','gy','gz'}, use_global_device_ids=true, to_apply=%region_2.3 | all-reduce | flops 2 | bytes 16 | tf_op jit(solution)/shard_map/psum | solution.py:201
  158.5 4.5 multiply_reduce_fusion
  163.0 41.2 %psum.37 = f32[]{:T(128)} all-reduce(f32[]{:T(128)} %get-tuple-element.26), channel_id=1, replica_groups=mesh['gx'=2,'gy'=4,'gz'=4] {'gx','gy','gz'}, use_global_device_ids=true, to_apply=%region_6.7 | all-reduce | flops 1 | bytes 8 | tf_op jit(solution)/shard_map/psum | solution.py:201
  209.1 4.3 collective-permute-done.9
  215.2 4.1 collective-permute-done.10
  222.8 2.8 fusion.138
  268.5 7.6 %collective-permute-done.12 = f32[3,1,96,129]{2,3,1,0:T(8,128)S(1)} collective-permute-done((f32[3,1,96,129]{2,3,1,0:T(8,128)S(1)}, f32[3,1,96,129]{2,3,1,0:T(8,128)S(1)}, u32[]{:S(2)}, u32[]{:S(2)}) %collective-permute-start.12) | collective-permute-done | bytes 148640 | tf_op jit(solution)/shard_map/ppermute | solution.py:29
  276.1 5.4 %collective-permute-start.13 = (f32[3,1,96,129]{2,3,1,0:T(8,128)S(1)}, f32[3,1,96,129]{2,3,1,0:T(8,128)S(1)}, u32[]{:S(2)}, u32[]{:S(2)}) collective-permute-start(f32[3,1,96,129]{2,3,1,0:T(8,128)S(1)} %collective-permute-done.12), channel_id=1, source_target_pairs={{0,1},{1,2},{2,3},{4,5},{5,6},{6,7},{8,9},{9,10},{10,11},{12,13},{... | collective-permute-start | bytes 445832 | tf_op jit(solution)/shard_map/ppermute | solution.py:23
  287.2 42.4 %psum.38 = f32[]{:T(128)} all-reduce(f32[]{:T(128)} %fusion.3), channel_id=1, replica_groups=mesh['gx'=2,'gy'=4,'gz'=4] {'gx','gy','gz'}, use_global_device_ids=true, to_apply=%region_8.9 | all-reduce | flops 1 | bytes 8 | tf_op jit(solution)/shard_map/psum | solution.py:229
  334.4 4.3 collective-permute-done.15
  340.8 4.4 collective-permute-done.16
  349.6 28.1 %bitcast_divide_fusion = f32[8,96,128]{1,2,0:T(8,128)S(1)} fusion(f32[1,8,96,128]{2,3,1,0:T(8,128)S(1)} %copy-done.10, f32[3,9,96,129]{2,3,1,0:T(8,128)S(1)} %pad_maximum_fusion.2, f32[3,8,96,1]{2,3,1,0:T(1,128)S(1)} %collective-permute-done.15, f32[3,8,96,128]{2,3,1,0:T(8,128)S(1)} %multiply_add_fusion.1, f32[8,96,128]{1,2,0:T(8,128)S(1)} %fusion.35), kind=kLoop, calls=%fused_computation.584 | loop fusion | flops 91521024 | bytes 9625600 | tf_op jit(solution)/shard_map/div | solution.py:238
  381.6 4.3 collective-permute-done.19
  385.9 2.3 fusion.17
  389.6 15.8 %all_to_all.24 = f32[1,8,96,128]{3,1,0,2:T(8,128)S(1)} all-to-all(f32[1,8,96,128]{3,1,0,2:T(8,128)S(1)} %copy.84), channel_id=1, replica_groups=mesh['gx'=2,'gy'=4,'gz'=4] {'gy'}, dimensions={2} | all-to-all | bytes 786432 | tf_op jit(solution)/shard_map/all_to_all | solution.py:205
  405.5 3.5 collective-permute-start.20
  415.4 3.5 all-to-all-start.1
  422.9 2.9 copy.95
  425.8 42.7 %psum.39 = f32[]{:T(128)} all-reduce(f32[]{:T(128)} %get-tuple-element.50), channel_id=1, replica_groups=mesh['gx'=2,'gy'=4,'gz'=4] {'gx','gy','gz'}, use_global_device_ids=true, to_apply=%region_10.11 | all-reduce | flops 1 | bytes 8 | tf_op jit(solution)/shard_map/psum | solution.py:244
  (180 shorter events, 147.2 us)
Async XLA Ops:
  9.7 10.3 %collective-permute-start = (f32[3,1,96,129]{2,3,1,0:T(8,128)S(1)}, f32[3,1,96,129]{2,3,1,0:T(8,128)S(1)}, u32[]{:S(2)}, u32[]{:S(2)}) collective-permute-start(f32[3,1,96,129]{2,3,1,0:T(8,128)S(1)} %slice.546), channel_id=1, source_target_pairs={{12,0},{0,4},{4,8},{8,12},{13,1},{1,5},{5,9},{9,13},{14,2},{2,6},{... | collective-permute-start | bytes 445832 | tf_op jit(solution)/shard_map/ppermute | solution.py:29
  12.9 15.4 %copy-start.4 = (f32[3,7,96,129]{2,3,1,0:T(8,128)}, f32[3,7,96,129]{2,3,1,0:T(8,128)S(1)}, u32[]{:S(2)}) copy-start(f32[3,7,96,129]{2,3,1,0:T(8,128)S(1)} %slice.547) | copy-start | bytes 3120772
  20.0 2.4 collective-permute-start.1
  23.3 5.0 %copy-start.13 = (f32[3,1,96,129]{2,3,1,0:T(8,128)}, f32[3,1,96,129]{2,3,1,0:T(8,128)S(1)}, u32[]{:S(2)}) copy-start(f32[3,1,96,129]{2,3,1,0:T(8,128)S(1)} %slice_add_fusion) | copy-start | bytes 445828
  23.4 5.0 %copy-start = (f32[3,1,8,96,128]{3,4,2,0,1:T(8,128)S(1)}, f32[3,1,8,96,128]{3,4,2,0,1:T(8,128)}, u32[]{:S(2)}) copy-start(f32[3,1,8,96,128]{3,4,2,0,1:T(8,128)} %copy.83) | copy-start | bytes 3538948
  23.4 4.9 %collective-permute-start.2 = (f32[3,8,96,1]{2,3,1,0:T(1,128)S(1)}, f32[3,8,96,1]{2,3,1,0:T(1,128)S(1)}, u32[]{:S(2)}, u32[]{:S(2)}) collective-permute-start(f32[3,8,96,1]{2,3,1,0:T(1,128)S(1)} %pad_maximum_fusion.9), channel_id=1, source_target_pairs={{0,16},{1,17},{2,18},{3,19},{4,20},{5,21},{6,22},{7,23},{8,24},{9,... | collective-permute-start | bytes 27656 | tf_op jit(solution)/shard_map/ppermute | solution.py:23
  30.0 5.6 %collective-permute-start.3 = (f32[3,8,96,1]{2,3,1,0:T(1,128)S(1)}, f32[3,8,96,1]{2,3,1,0:T(1,128)S(1)}, u32[]{:S(2)}, u32[]{:S(2)}) collective-permute-start(f32[3,8,96,1]{2,3,1,0:T(1,128)S(1)} %slice.549), channel_id=1, source_target_pairs={{16,0},{17,1},{18,2},{19,3},{20,4},{21,5},{22,6},{23,7},{24,8},{25... | collective-permute-start | bytes 27656 | tf_op jit(solution)/shard_map/ppermute | solution.py:23
  35.6 7.2 %collective-permute-start.4 = (f32[3,1,96,129]{2,3,1,0:T(8,128)S(1)}, f32[3,1,96,129]{2,3,1,0:T(8,128)S(1)}, u32[]{:S(2)}, u32[]{:S(2)}) collective-permute-start(f32[3,1,96,129]{2,3,1,0:T(8,128)S(1)} %fusion.238), channel_id=1, source_target_pairs={{4,0},{8,4},{12,8},{0,12},{5,1},{9,5},{13,9},{1,13},{6,2},{10,6},{... | collective-permute-start | bytes 445832 | tf_op jit(solution)/shard_map/ppermute | solution.py:29
  42.7 3.6 collective-permute-start.5
  93.2 7.7 %collective-permute-start.6 = (f32[3,1,96,129]{2,3,1,0:T(8,128)S(1)}, f32[3,1,96,129]{2,3,1,0:T(8,128)S(1)}, u32[]{:S(2)}, u32[]{:S(2)}) collective-permute-start(f32[3,1,96,129]{2,3,1,0:T(8,128)S(1)} %pad_maximum_fusion.8), channel_id=1, source_target_pairs={{12,0},{0,4},{4,8},{8,12},{13,1},{1,5},{5,9},{9,13},{14,2},{2,6},{... | collective-permute-start | bytes 445832 | tf_op jit(solution)/shard_map/ppermute | solution.py:29
  100.9 8.7 %collective-permute-start.7 = (f32[3,1,96,129]{2,3,1,0:T(8,128)S(1)}, f32[3,1,96,129]{2,3,1,0:T(8,128)S(1)}, u32[]{:S(2)}, u32[]{:S(2)}) collective-permute-start(f32[3,1,96,129]{2,3,1,0:T(8,128)S(1)} %collective-permute-done.6), channel_id=1, source_target_pairs={{0,1},{1,2},{2,3},{4,5},{5,6},{6,7},{8,9},{9,10},{10,11},{12,13},{... | collective-permute-start | bytes 445832 | tf_op jit(solution)/shard_map/ppermute | solution.py:23
  109.8 3.3 copy-start.1
  109.8 3.3 collective-permute-start.8
  113.1 45.4 %copy-start.18 = (f32[3,8,96,1]{2,3,1,0:T(1,128)}, f32[3,8,96,1]{2,3,1,0:T(1,128)S(1)}, u32[]{:S(2)}) copy-start(f32[3,8,96,1]{2,3,1,0:T(1,128)S(1)} %slice_add_fusion.2) | copy-start | bytes 27652
  207.8 5.6 %collective-permute-start.9 = (f32[3,8,96,1]{2,3,1,0:T(1,128)S(1)}, f32[3,8,96,1]{2,3,1,0:T(1,128)S(1)}, u32[]{:S(2)}, u32[]{:S(2)}) collective-permute-start(f32[3,8,96,1]{2,3,1,0:T(1,128)S(1)} %slice.568), channel_id=1, source_target_pairs={{16,0},{17,1},{18,2},{19,3},{20,4},{21,5},{22,6},{23,7},{24,8},{25... | collective-permute-start | bytes 27656 | tf_op jit(solution)/shard_map/ppermute | solution.py:23
  213.4 5.9 %collective-permute-start.10 = (f32[3,1,96,129]{2,3,1,0:T(8,128)S(1)}, f32[3,1,96,129]{2,3,1,0:T(8,128)S(1)}, u32[]{:S(2)}, u32[]{:S(2)}) collective-permute-start(f32[3,1,96,129]{2,3,1,0:T(8,128)S(1)} %fusion.237), channel_id=1, source_target_pairs={{4,0},{8,4},{12,8},{0,12},{5,1},{9,5},{13,9},{1,13},{6,2},{10,6},{... | collective-permute-start | bytes 445832 | tf_op jit(solution)/shard_map/ppermute | solution.py:29
  219.2 3.3 collective-permute-start.11
  268.4 7.7 %collective-permute-start.12 = (f32[3,1,96,129]{2,3,1,0:T(8,128)S(1)}, f32[3,1,96,129]{2,3,1,0:T(8,128)S(1)}, u32[]{:S(2)}, u32[]{:S(2)}) collective-permute-start(f32[3,1,96,129]{2,3,1,0:T(8,128)S(1)} %pad_maximum_fusion.7), channel_id=1, source_target_pairs={{12,0},{0,4},{4,8},{8,12},{13,1},{1,5},{5,9},{9,13},{14,2},{2,6},{... | collective-permute-start | bytes 445832 | tf_op jit(solution)/shard_map/ppermute | solution.py:29
  276.1 6.4 %collective-permute-start.13 = (f32[3,1,96,129]{2,3,1,0:T(8,128)S(1)}, f32[3,1,96,129]{2,3,1,0:T(8,128)S(1)}, u32[]{:S(2)}, u32[]{:S(2)}) collective-permute-start(f32[3,1,96,129]{2,3,1,0:T(8,128)S(1)} %collective-permute-done.12), channel_id=1, source_target_pairs={{0,1},{1,2},{2,3},{4,5},{5,6},{6,7},{8,9},{9,10},{10,11},{12,13},{... | collective-permute-start | bytes 445832 | tf_op jit(solution)/shard_map/ppermute | solution.py:23
  282.7 3.4 copy-start.3
  282.7 3.4 copy-start.5
  282.7 3.3 collective-permute-start.14
  333.1 5.6 %collective-permute-start.15 = (f32[3,8,96,1]{2,3,1,0:T(1,128)S(1)}, f32[3,8,96,1]{2,3,1,0:T(1,128)S(1)}, u32[]{:S(2)}, u32[]{:S(2)}) collective-permute-start(f32[3,8,96,1]{2,3,1,0:T(1,128)S(1)} %slice.587), channel_id=1, source_target_pairs={{16,0},{17,1},{18,2},{19,3},{20,4},{21,5},{22,6},{23,7},{24,8},{25... | collective-permute-start | bytes 27656 | tf_op jit(solution)/shard_map/ppermute | solution.py:23
  338.7 6.5 %collective-permute-start.16 = (f32[3,1,96,129]{2,3,1,0:T(8,128)S(1)}, f32[3,1,96,129]{2,3,1,0:T(8,128)S(1)}, u32[]{:S(2)}, u32[]{:S(2)}) collective-permute-start(f32[3,1,96,129]{2,3,1,0:T(8,128)S(1)} %fusion.236), channel_id=1, source_target_pairs={{4,0},{8,4},{12,8},{0,12},{5,1},{9,5},{13,9},{1,13},{6,2},{10,6},{... | collective-permute-start | bytes 445832 | tf_op jit(solution)/shard_map/ppermute | solution.py:29
  345.2 3.3 collective-permute-start.17
  377.7 3.8 collective-permute-start.18
  379.4 6.5 %collective-permute-start.19 = (f32[8,96,24]{1,2,0:T(8,128)S(1)}, f32[8,96,24]{1,2,0:T(8,128)S(1)}, u32[]{:S(2)}, u32[]{:S(2)}) collective-permute-start(f32[8,96,24]{1,2,0:T(8,128)S(1)} %get-tuple-element.37), channel_id=1, source_target_pairs={{16,0},{17,1},{18,2},{19,3},{20,4},{21,5},{22,6},{23,7},{24,8},{25... | collective-permute-start | bytes 221192 | tf_op jit(solution)/shard_map/ppermute | solution.py:40
  405.5 13.4 %copy-start.14 = (f32[3,1,96,129]{2,3,1,0:T(8,128)S(1)}, f32[3,1,96,129]{2,3,1,0:T(8,128)}, u32[]{:S(2)}) copy-start(f32[3,1,96,129]{2,3,1,0:T(8,128)} %copy-done.13) | copy-start | bytes 445828
  405.5 5.0 %collective-permute-start.20 = (f32[24,24,128]{2,0,1:T(8,128)S(1)}, f32[24,24,128]{2,0,1:T(8,128)S(1)}, u32[]{:S(2)}, u32[]{:S(2)}) collective-permute-start(f32[24,24,128]{2,0,1:T(8,128)S(1)} %get-tuple-element.46), channel_id=1, source_target_pairs={{0,1},{1,2},{2,3},{4,5},{5,6},{6,7},{8,9},{9,10},{10,11},{12,13},{... | collective-permute-start | bytes 884744 | tf_op jit(solution)/shard_map/ppermute | solution.py:37
  409.0 3.5 collective-permute-start.21
  415.4 53.7 %all-to-all-start.1 = ((f32[1,32,24,128]{3,2,0,1:T(8,128)}), f32[1,32,24,128]{3,2,0,1:T(8,128)S(1)}, u32[]{:S(2)}, u32[]{:S(2)}) async-start(f32[1,32,24,128]{3,2,0,1:T(8,128)} %copy.86), calls=%async_computation.1 | async-start | bytes 786432 | tf_op jit(solution)/shard_map/all_to_all | solution.py:209
  425.8 43.6 %copy-start.16 = (s32[1,8,96,128]{2,3,1,0:T(8,128)S(1)}, s32[1,8,96,128]{2,3,1,0:T(8,128)}, u32[]{:S(2)}) copy-start(s32[1,8,96,128]{2,3,1,0:T(8,128)} %copy-done.15) | copy-start | bytes 1179652
  (11 other events, 24.9 us)
where the time goes:
time: 476 us; the launch traced here: 471 us
  blocking collectives  185 us (39%)
  other arithmetic  143 us (30%)
  waiting for transfers between devices  63.9 us (13%)
  starting transfers between devices  49.6 us (10%)
  local copies, waits for them, and re-layouts  17.6 us (4%)
  between operations  6.32 us (1%)
  matrix products  5.38 us (1%)
    mul x48, other arithmetic, lean_forces(): term = moduli * products[component * 8 + node]  88.2 us
    psum x2, blocking collectives, inner_sum(): return lax.psum(jnp.sum(values), ('gx', 'gy', 'gz'))  83.7 us
    psum x1, blocking collectives, on_device(): total = lax.psum(jnp.sum(stimulus), ('gx', 'gy', 'gz'))  42.7 us
    psum x1, blocking collectives, on_device(): alpha = gamma / lax.psum(jnp.sum(search * image), ('gx', 'gy', 'gz'))  42.4 us
    ppermute x6, waiting for transfers between devices, from_behind(): return lax.ppermute(block, axis, route)  32.6 us
    ppermute x12, starting transfers between devices, shifted(): lax.ppermute(value, axis, [(source, source + steps) for source in range(i...  29.3 us
    div x1, other arithmetic, on_device(): specific = energy / local_density  28.1 us
    ppermute x12, waiting for transfers between devices, shifted(): lax.ppermute(value, axis, [(source, source + steps) for source in range(i...  24.1 us
  transfers between devices with their start and end apart: 23, of which 20 were waited for; matrix products, arithmetic and copies ran while one was open for 3% of the time, Pallas kernels for 0%

commit v1 on v0

--- a/solution.py
+++ b/solution.py
@@ -197,8 +197,22 @@
     return lean_energy(nodes, modulus, table)
 
 
+def total_over_mesh(value):
+    for axis in ("gx", "gy", "gz"):
+        count = lax.axis_size(axis)
+        if count & (count - 1):
+            value = lax.psum(value, axis)
+            continue
+        step = 1
+        while step < count:
+            other = lax.ppermute(value, axis, [(i, i ^ step) for i in range(count)])
+            value = value + other
+            step *= 2
+    return value
+
+
 def inner_sum(values):
-    return lax.psum(jnp.sum(values), ("gx", "gy", "gz"))
+    return total_over_mesh(jnp.full((8, 128), jnp.sum(values)))[0, 0]
 
 
 def to_bricks(values):
@@ -226,7 +240,7 @@
     gamma = inner_sum(residual * search)
     for count in range(ITERS):
         image = free_nodes * node_forces(free_nodes * search, modulus, table)
-        alpha = gamma / lax.psum(jnp.sum(search * image), ("gx", "gy", "gz"))
+        alpha = gamma / inner_sum(search * image)
         solution = solution + alpha * search
         if count + 1 < ITERS:
             residual = residual - alpha * image
@@ -241,7 +255,7 @@
     brick = to_bricks(planar[None])[0]
     deep = extended(brick, (("gz", 0),), RAD)
     stimulus = smooth(deep, 0, brick.shape[0])
-    total = lax.psum(jnp.sum(stimulus), ("gx", "gy", "gz"))
+    total = inner_sum(stimulus)
     cells = stimulus.size * lax.axis_size("gx") * lax.axis_size("gy") * lax.axis_size("gz")
     mean = total / cells
     returned = to_slabs(stimulus[None])[0]

time: 476 us -> 382 us (0.80)
  blocking collectives: 185 us -> 16.6 us
  waiting for transfers between devices: 63.9 us -> 105 us
  starting transfers between devices: 49.6 us -> 76 us
  local copies, waits for them, and re-layouts: 17.6 us -> 23.9 us
    psum x4 -> x0, blocking collectives: 169 us -> none  [the longest x2 83.7 us: inner_sum(): return lax.psum(jnp.sum(values), ('gx', 'gy', 'gz'))]
    ppermute x0 -> x25, waiting for transfers between devices: none -> 42.1 us  [total_over_mesh(): other = lax.ppermute(value, axis, [(i, i ^ step) for i in range(count)])]
    ppermute x0 -> x25, starting transfers between devices: none -> 27.7 us  [total_over_mesh(): other = lax.ppermute(value, axis, [(i, i ^ step) for i in range(count)])]
    add x0 -> x25, other arithmetic: none -> 6.14 us  [total_over_mesh(): value = value + other]
    unnamed x46 -> x42, local copies, waits for them, and re-layouts: 10.9 us -> 10.8 us
  transfers between devices with their start and end apart: 23 -> 48, of which waited for: 20 -> 40; matrix products, arithmetic and copies ran while one was open for 3% -> 5% of each run, Pallas kernels for 0% -> 0%
where the time goes in v1:
time: 382 us; the launch traced here: 376 us
  other arithmetic  142 us (37%)
  waiting for transfers between devices  105 us (27%)
  starting transfers between devices  76 us (20%)
  local copies, waits for them, and re-layouts  23.9 us (6%)
  blocking collectives  16.6 us (4%)
  between operations  6.55 us (2%)
  matrix products  5.34 us (1%)
    mul x48, other arithmetic, lean_forces(): term = moduli * products[component * 8 + node]  88.2 us
    ppermute x25, waiting for transfers between devices, total_over_mesh(): other = lax.ppermute(value, axis, [(i, i ^ step) for i in range(count)])  42.1 us
    ppermute x6, waiting for transfers between devices, from_behind(): return lax.ppermute(block, axis, route)  32 us
    div x1, other arithmetic, on_device(): specific = energy / local_density  28.1 us
    ppermute x12, starting transfers between devices, shifted(): lax.ppermute(value, axis, [(source, source + steps) for source in range(i...  27.7 us
    ppermute x25, starting transfers between devices, total_over_mesh(): other = lax.ppermute(value, axis, [(i, i ^ step) for i in range(count)])  27.7 us
    ppermute x12, waiting for transfers between devices, shifted(): lax.ppermute(value, axis, [(source, source + steps) for source in range(i...  24.1 us
    all_to_all x1, blocking collectives, to_bricks(): return lax.all_to_all(values, 'gy', split_axis=2, concat_axis=1, tiled=True)  16.6 us
  transfers between devices with their start and end apart: 48, of which 40 were waited for; matrix products, arithmetic and copies ran while one was open for 5% of the time, Pallas kernels for 0%

profile of v1, /device:TPU:0, one launch (start us, length us, event | category | flops | bytes accessed | tf_op | source)
XLA Modules:
  0.0 376.2 jit_solution(12671448150828264604)
XLA Ops:
  6.9 2.8 multiply_add_fusion
  10.4 3.1 collective-permute-start
  13.8 3.2 copy.83
  17.0 3.9 %collective-permute-done = f32[3,1,96,129]{2,3,1,0:T(8,128)S(1)} collective-permute-done((f32[3,1,96,129]{2,3,1,0:T(8,128)}, f32[3,1,96,129]{2,3,1,0:T(8,128)S(1)}, u32[]{:S(2)}, u32[]{:S(2)}) %collective-permute-start) | collective-permute-done | bytes 148640 | tf_op jit(solution)/shard_map/ppermute | solution.py:29
  24.2 3.5 collective-permute-start.2
  32.2 4.3 %collective-permute-done.8 = f32[3,8,96,1]{2,3,1,0:T(1,128)S(1)} collective-permute-done((f32[3,8,96,1]{2,3,1,0:T(1,128)S(1)}, f32[3,8,96,1]{2,3,1,0:T(1,128)S(1)}, u32[]{:S(2)}, u32[]{:S(2)}) %collective-permute-start.8) | collective-permute-done | bytes 9248 | tf_op jit(solution)/shard_map/ppermute | solution.py:23
  38.3 5.4 %collective-permute-done.9 = f32[3,1,96,129]{2,3,1,0:T(8,128)S(1)} collective-permute-done((f32[3,1,96,129]{2,3,1,0:T(8,128)S(1)}, f32[3,1,96,129]{2,3,1,0:T(8,128)S(1)}, u32[]{:S(2)}, u32[]{:S(2)}) %collective-permute-start.9) | collective-permute-done | bytes 148640 | tf_op jit(solution)/shard_map/ppermute | solution.py:29
  94.2 7.6 %collective-permute-done.11 = f32[3,1,96,129]{2,3,1,0:T(8,128)S(1)} collective-permute-done((f32[3,1,96,129]{2,3,1,0:T(8,128)S(1)}, f32[3,1,96,129]{2,3,1,0:T(8,128)S(1)}, u32[]{:S(2)}, u32[]{:S(2)}) %collective-permute-start.11) | collective-permute-done | bytes 148640 | tf_op jit(solution)/shard_map/ppermute | solution.py:29
  101.8 7.6 %collective-permute-start.12 = (f32[3,1,96,129]{2,3,1,0:T(8,128)S(1)}, f32[3,1,96,129]{2,3,1,0:T(8,128)S(1)}, u32[]{:S(2)}, u32[]{:S(2)}) collective-permute-start(f32[3,1,96,129]{2,3,1,0:T(8,128)S(1)} %collective-permute-done.11), channel_id=1, source_target_pairs={{0,1},{1,2},{2,3},{4,5},{5,6},{6,7},{8,9},{9,10},{10,11},{12,13},{... | collective-permute-start | bytes 445832 | tf_op jit(solution)/shard_map/ppermute | solution.py:23
  132.1 5.1 %collective-permute-start.18 = (f32[8,128]{1,0:T(8,128)S(1)}, f32[8,128]{1,0:T(8,128)S(1)}, u32[]{:S(2)}, u32[]{:S(2)}) collective-permute-start(f32[8,128]{1,0:T(8,128)S(1)} %add.6201), channel_id=1, source_target_pairs={{0,2},{1,3},{2,0},{3,1},{4,6},{5,7},{6,4},{7,5},{8,10},{9,11},{10,... | collective-permute-start | bytes 12296 | tf_op jit(solution)/shard_map/ppermute | solution.py:208
  145.3 2.9 collective-permute-done.19
  149.4 3.1 collective-permute-done.20
  154.3 3.4 collective-permute-done.21
  166.0 4.3 %collective-permute-done.24 = f32[3,8,96,1]{2,3,1,0:T(1,128)S(1)} collective-permute-done((f32[3,8,96,1]{2,3,1,0:T(1,128)S(1)}, f32[3,8,96,1]{2,3,1,0:T(1,128)S(1)}, u32[]{:S(2)}, u32[]{:S(2)}) %collective-permute-start.24) | collective-permute-done | bytes 9248 | tf_op jit(solution)/shard_map/ppermute | solution.py:23
  172.1 4.1 %collective-permute-done.25 = f32[3,1,96,129]{2,3,1,0:T(8,128)S(1)} collective-permute-done((f32[3,1,96,129]{2,3,1,0:T(8,128)S(1)}, f32[3,1,96,129]{2,3,1,0:T(8,128)S(1)}, u32[]{:S(2)}, u32[]{:S(2)}) %collective-permute-start.25) | collective-permute-done | bytes 148640 | tf_op jit(solution)/shard_map/ppermute | solution.py:29
  179.7 2.8 fusion.138
  225.9 7.1 %collective-permute-done.27 = f32[3,1,96,129]{2,3,1,0:T(8,128)S(1)} collective-permute-done((f32[3,1,96,129]{2,3,1,0:T(8,128)S(1)}, f32[3,1,96,129]{2,3,1,0:T(8,128)S(1)}, u32[]{:S(2)}, u32[]{:S(2)}) %collective-permute-start.27) | collective-permute-done | bytes 148640 | tf_op jit(solution)/shard_map/ppermute | solution.py:29
  233.0 4.0 %collective-permute-start.28 = (f32[3,1,96,129]{2,3,1,0:T(8,128)S(1)}, f32[3,1,96,129]{2,3,1,0:T(8,128)S(1)}, u32[]{:S(2)}, u32[]{:S(2)}) collective-permute-start(f32[3,1,96,129]{2,3,1,0:T(8,128)S(1)} %collective-permute-done.27), channel_id=1, source_target_pairs={{0,1},{1,2},{2,3},{4,5},{5,6},{6,7},{8,9},{9,10},{10,11},{12,13},{... | collective-permute-start | bytes 445832 | tf_op jit(solution)/shard_map/ppermute | solution.py:23
  247.9 3.6 collective-permute-done.31
  252.5 4.2 %collective-permute-done.32 = f32[8,128]{1,0:T(8,128)S(1)} collective-permute-done((f32[8,128]{1,0:T(8,128)S(1)}, f32[8,128]{1,0:T(8,128)S(1)}, u32[]{:S(2)}, u32[]{:S(2)}) %collective-permute-start.32) | collective-permute-done | bytes 4128 | tf_op jit(solution)/shard_map/ppermute | solution.py:208
  257.9 5.0 %collective-permute-start.34 = (f32[8,128]{1,0:T(8,128)S(1)}, f32[8,128]{1,0:T(8,128)S(1)}, u32[]{:S(2)}, u32[]{:S(2)}) collective-permute-start(f32[8,128]{1,0:T(8,128)S(1)} %add.6801), channel_id=1, source_target_pairs={{0,2},{1,3},{2,0},{3,1},{4,6},{5,7},{6,4},{7,5},{8,10},{9,11},{10,... | collective-permute-start | bytes 12296 | tf_op jit(solution)/shard_map/ppermute | solution.py:208
  267.9 4.3 %collective-permute-done.35 = f32[3,8,96,1]{2,3,1,0:T(1,128)S(1)} collective-permute-done((f32[3,8,96,1]{2,3,1,0:T(1,128)S(1)}, f32[3,8,96,1]{2,3,1,0:T(1,128)S(1)}, u32[]{:S(2)}, u32[]{:S(2)}) %collective-permute-start.35) | collective-permute-done | bytes 9248 | tf_op jit(solution)/shard_map/ppermute | solution.py:23
  274.1 4.1 %collective-permute-done.36 = f32[3,1,96,129]{2,3,1,0:T(8,128)S(1)} collective-permute-done((f32[3,1,96,129]{2,3,1,0:T(8,128)S(1)}, f32[3,1,96,129]{2,3,1,0:T(8,128)S(1)}, u32[]{:S(2)}, u32[]{:S(2)}) %collective-permute-start.36) | collective-permute-done | bytes 148640 | tf_op jit(solution)/shard_map/ppermute | solution.py:29
  282.5 28.1 %bitcast_divide_fusion = f32[8,96,128]{1,2,0:T(8,128)S(1)} fusion(f32[1,8,96,128]{2,3,1,0:T(8,128)S(1)} %copy-done.8, f32[3,9,96,129]{2,3,1,0:T(8,128)S(1)} %pad_maximum_fusion.2, f32[3,8,96,1]{2,3,1,0:T(1,128)S(1)} %collective-permute-done.35, f32[3,8,96,128]{2,3,1,0:T(8,128)S(1)} %multiply_add_fusion.1, f32[8,96,128]{1,2,0:T(8,128)S(1)} %fusion.35), kind=kLoop, calls=%fused_computation.584 | loop fusion | flops 91521024 | bytes 9625600 | tf_op jit(solution)/shard_map/div | solution.py:252
  314.5 4.3 %collective-permute-done.39 = f32[8,96,24]{1,2,0:T(8,128)S(1)} collective-permute-done((f32[8,96,24]{1,2,0:T(8,128)S(1)}, f32[8,96,24]{1,2,0:T(8,128)S(1)}, u32[]{:S(2)}, u32[]{:S(2)}) %collective-permute-start.39) | collective-permute-done | bytes 73760 | tf_op jit(solution)/shard_map/ppermute | solution.py:40
  322.5 16.6 %all_to_all.24 = f32[1,8,96,128]{3,1,0,2:T(8,128)S(1)} all-to-all(f32[1,8,96,128]{3,1,0,2:T(8,128)S(1)} %copy.84), channel_id=1, replica_groups=mesh['gx'=2,'gy'=4,'gz'=4] {'gy'}, dimensions={2} | all-to-all | bytes 786432 | tf_op jit(solution)/shard_map/all_to_all | solution.py:219
  339.2 3.0 collective-permute-start.40
  348.3 3.6 collective-permute-done.42
  352.8 3.4 collective-permute-done.43
  357.9 4.2 %all-to-all-start.1 = ((f32[1,32,24,128]{3,2,0,1:T(8,128)}), f32[1,32,24,128]{3,2,0,1:T(8,128)S(1)}, u32[]{:S(2)}, u32[]{:S(2)}) async-start(f32[1,32,24,128]{3,2,0,1:T(8,128)} %copy.86), calls=%async_computation.1 | async-start | bytes 786432 | tf_op jit(solution)/shard_map/all_to_all | solution.py:223
  365.5 2.8 collective-permute-start.46
  370.5 2.9 copy.95
  (257 shorter events, 201.6 us)
Async XLA Ops:
  10.4 10.4 %collective-permute-start = (f32[3,1,96,129]{2,3,1,0:T(8,128)}, f32[3,1,96,129]{2,3,1,0:T(8,128)S(1)}, u32[]{:S(2)}, u32[]{:S(2)}) collective-permute-start(f32[3,1,96,129]{2,3,1,0:T(8,128)} %slice.566), channel_id=1, source_target_pairs={{12,0},{0,4},{4,8},{8,12},{13,1},{1,5},{5,9},{9,13},{14,2},{2,6},{... | collective-permute-start | bytes 445832 | tf_op jit(solution)/shard_map/ppermute | solution.py:29
  24.2 4.9 %collective-permute-start.2 = (f32[3,8,96,1]{2,3,1,0:T(1,128)S(1)}, f32[3,8,96,1]{2,3,1,0:T(1,128)S(1)}, u32[]{:S(2)}, u32[]{:S(2)}) collective-permute-start(f32[3,8,96,1]{2,3,1,0:T(1,128)S(1)} %pad_maximum_fusion.9), channel_id=1, source_target_pairs={{0,16},{1,17},{2,18},{3,19},{4,20},{5,21},{6,22},{7,23},{8,24},{9,... | collective-permute-start | bytes 27656 | tf_op jit(solution)/shard_map/ppermute | solution.py:23
  30.9 5.6 %collective-permute-start.8 = (f32[3,8,96,1]{2,3,1,0:T(1,128)S(1)}, f32[3,8,96,1]{2,3,1,0:T(1,128)S(1)}, u32[]{:S(2)}, u32[]{:S(2)}) collective-permute-start(f32[3,8,96,1]{2,3,1,0:T(1,128)S(1)} %slice.569), channel_id=1, source_target_pairs={{16,0},{17,1},{18,2},{19,3},{20,4},{21,5},{22,6},{23,7},{24,8},{25... | collective-permute-start | bytes 27656 | tf_op jit(solution)/shard_map/ppermute | solution.py:23
  36.5 7.2 %collective-permute-start.9 = (f32[3,1,96,129]{2,3,1,0:T(8,128)S(1)}, f32[3,1,96,129]{2,3,1,0:T(8,128)S(1)}, u32[]{:S(2)}, u32[]{:S(2)}) collective-permute-start(f32[3,1,96,129]{2,3,1,0:T(8,128)S(1)} %fusion.238), channel_id=1, source_target_pairs={{4,0},{8,4},{12,8},{0,12},{5,1},{9,5},{13,9},{1,13},{6,2},{10,6},{... | collective-permute-start | bytes 445832 | tf_op jit(solution)/shard_map/ppermute | solution.py:29
  94.1 7.7 %collective-permute-start.11 = (f32[3,1,96,129]{2,3,1,0:T(8,128)S(1)}, f32[3,1,96,129]{2,3,1,0:T(8,128)S(1)}, u32[]{:S(2)}, u32[]{:S(2)}) collective-permute-start(f32[3,1,96,129]{2,3,1,0:T(8,128)S(1)} %pad_maximum_fusion.8), channel_id=1, source_target_pairs={{12,0},{0,4},{4,8},{8,12},{13,1},{1,5},{5,9},{9,13},{14,2},{2,6},{... | collective-permute-start | bytes 445832 | tf_op jit(solution)/shard_map/ppermute | solution.py:29
  101.8 8.7 %collective-permute-start.12 = (f32[3,1,96,129]{2,3,1,0:T(8,128)S(1)}, f32[3,1,96,129]{2,3,1,0:T(8,128)S(1)}, u32[]{:S(2)}, u32[]{:S(2)}) collective-permute-start(f32[3,1,96,129]{2,3,1,0:T(8,128)S(1)} %collective-permute-done.11), channel_id=1, source_target_pairs={{0,1},{1,2},{2,3},{4,5},{5,6},{6,7},{8,9},{9,10},{10,11},{12,13},{... | collective-permute-start | bytes 445832 | tf_op jit(solution)/shard_map/ppermute | solution.py:23
  116.1 3.9 %collective-permute-start.14 = (f32[8,128]{1,0:T(8,128)S(1)}, f32[8,128]{1,0:T(8,128)S(1)}, u32[]{:S(2)}, u32[]{:S(2)}) collective-permute-start(f32[8,128]{1,0:T(8,128)S(1)} %broadcast_in_dim.32), channel_id=1, source_target_pairs={{0,16},{16,0},{1,17},{17,1},{2,18},{18,2},{3,19},{19,3},{4,20},{20... | collective-permute-start | bytes 12296 | tf_op jit(solution)/shard_map/ppermute | solution.py:208
  119.0 3.7 collective-permute-start.3
  120.7 3.7 collective-permute-start.15
  123.2 3.7 collective-permute-start.4
  125.1 4.6 %collective-permute-start.16 = (f32[8,128]{1,0:T(8,128)S(1)}, f32[8,128]{1,0:T(8,128)S(1)}, u32[]{:S(2)}, u32[]{:S(2)}) collective-permute-start(f32[8,128]{1,0:T(8,128)S(1)} %fusion.301), channel_id=1, source_target_pairs={{0,8},{4,12},{8,0},{12,4},{1,9},{5,13},{9,1},{13,5},{2,10},{6,14},... | collective-permute-start | bytes 12296 | tf_op jit(solution)/shard_map/ppermute | solution.py:208
  127.5 4.6 %collective-permute-start.5 = (f32[8,128]{1,0:T(8,128)S(1)}, f32[8,128]{1,0:T(8,128)S(1)}, u32[]{:S(2)}, u32[]{:S(2)}) collective-permute-start(f32[8,128]{1,0:T(8,128)S(1)} %fusion.302), channel_id=1, source_target_pairs={{0,8},{4,12},{8,0},{12,4},{1,9},{5,13},{9,1},{13,5},{2,10},{6,14},... | collective-permute-start | bytes 12296 | tf_op jit(solution)/shard_map/ppermute | solution.py:208
  132.0 5.1 %collective-permute-start.6 = (f32[8,128]{1,0:T(8,128)S(1)}, f32[8,128]{1,0:T(8,128)S(1)}, u32[]{:S(2)}, u32[]{:S(2)}) collective-permute-start(f32[8,128]{1,0:T(8,128)S(1)} %add.5606), channel_id=1, source_target_pairs={{0,1},{1,0},{2,3},{3,2},{4,5},{5,4},{6,7},{7,6},{8,9},{9,8},{10,11... | collective-permute-start | bytes 12296 | tf_op jit(solution)/shard_map/ppermute | solution.py:208
  132.1 6.7 %collective-permute-start.18 = (f32[8,128]{1,0:T(8,128)S(1)}, f32[8,128]{1,0:T(8,128)S(1)}, u32[]{:S(2)}, u32[]{:S(2)}) collective-permute-start(f32[8,128]{1,0:T(8,128)S(1)} %add.6201), channel_id=1, source_target_pairs={{0,2},{1,3},{2,0},{3,1},{4,6},{5,7},{6,4},{7,5},{8,10},{9,11},{10,... | collective-permute-start | bytes 12296 | tf_op jit(solution)/shard_map/ppermute | solution.py:208
  153.1 4.6 %collective-permute-start.21 = (f32[8,128]{1,0:T(8,128)S(1)}, f32[8,128]{1,0:T(8,128)S(1)}, u32[]{:S(2)}, u32[]{:S(2)}) collective-permute-start(f32[8,128]{1,0:T(8,128)S(1)} %fusion.300), channel_id=1, source_target_pairs={{0,8},{4,12},{8,0},{12,4},{1,9},{5,13},{9,1},{13,5},{2,10},{6,14},... | collective-permute-start | bytes 12296 | tf_op jit(solution)/shard_map/ppermute | solution.py:208
  164.7 5.6 %collective-permute-start.24 = (f32[3,8,96,1]{2,3,1,0:T(1,128)S(1)}, f32[3,8,96,1]{2,3,1,0:T(1,128)S(1)}, u32[]{:S(2)}, u32[]{:S(2)}) collective-permute-start(f32[3,8,96,1]{2,3,1,0:T(1,128)S(1)} %slice.588), channel_id=1, source_target_pairs={{16,0},{17,1},{18,2},{19,3},{20,4},{21,5},{22,6},{23,7},{24,8},{25... | collective-permute-start | bytes 27656 | tf_op jit(solution)/shard_map/ppermute | solution.py:23
  170.3 5.9 %collective-permute-start.25 = (f32[3,1,96,129]{2,3,1,0:T(8,128)S(1)}, f32[3,1,96,129]{2,3,1,0:T(8,128)S(1)}, u32[]{:S(2)}, u32[]{:S(2)}) collective-permute-start(f32[3,1,96,129]{2,3,1,0:T(8,128)S(1)} %fusion.237), channel_id=1, source_target_pairs={{4,0},{8,4},{12,8},{0,12},{5,1},{9,5},{13,9},{1,13},{6,2},{10,6},{... | collective-permute-start | bytes 445832 | tf_op jit(solution)/shard_map/ppermute | solution.py:29
  225.3 7.7 %collective-permute-start.27 = (f32[3,1,96,129]{2,3,1,0:T(8,128)S(1)}, f32[3,1,96,129]{2,3,1,0:T(8,128)S(1)}, u32[]{:S(2)}, u32[]{:S(2)}) collective-permute-start(f32[3,1,96,129]{2,3,1,0:T(8,128)S(1)} %pad_maximum_fusion.7), channel_id=1, source_target_pairs={{12,0},{0,4},{4,8},{8,12},{13,1},{1,5},{5,9},{9,13},{14,2},{2,6},{... | collective-permute-start | bytes 445832 | tf_op jit(solution)/shard_map/ppermute | solution.py:29
  233.0 5.0 %collective-permute-start.28 = (f32[3,1,96,129]{2,3,1,0:T(8,128)S(1)}, f32[3,1,96,129]{2,3,1,0:T(8,128)S(1)}, u32[]{:S(2)}, u32[]{:S(2)}) collective-permute-start(f32[3,1,96,129]{2,3,1,0:T(8,128)S(1)} %collective-permute-done.27), channel_id=1, source_target_pairs={{0,1},{1,2},{2,3},{4,5},{5,6},{6,7},{8,9},{9,10},{10,11},{12,13},{... | collective-permute-start | bytes 445832 | tf_op jit(solution)/shard_map/ppermute | solution.py:23
  243.2 3.9 %collective-permute-start.30 = (f32[8,128]{1,0:T(8,128)S(1)}, f32[8,128]{1,0:T(8,128)S(1)}, u32[]{:S(2)}, u32[]{:S(2)}) collective-permute-start(f32[8,128]{1,0:T(8,128)S(1)} %broadcast_in_dim.35), channel_id=1, source_target_pairs={{0,16},{16,0},{1,17},{17,1},{2,18},{18,2},{3,19},{19,3},{4,20},{20... | collective-permute-start | bytes 12296 | tf_op jit(solution)/shard_map/ppermute | solution.py:208
  247.8 3.7 collective-permute-start.31
  252.1 4.6 %collective-permute-start.32 = (f32[8,128]{1,0:T(8,128)S(1)}, f32[8,128]{1,0:T(8,128)S(1)}, u32[]{:S(2)}, u32[]{:S(2)}) collective-permute-start(f32[8,128]{1,0:T(8,128)S(1)} %fusion.299), channel_id=1, source_target_pairs={{0,8},{4,12},{8,0},{12,4},{1,9},{5,13},{9,1},{13,5},{2,10},{6,14},... | collective-permute-start | bytes 12296 | tf_op jit(solution)/shard_map/ppermute | solution.py:208
  257.9 6.6 %collective-permute-start.34 = (f32[8,128]{1,0:T(8,128)S(1)}, f32[8,128]{1,0:T(8,128)S(1)}, u32[]{:S(2)}, u32[]{:S(2)}) collective-permute-start(f32[8,128]{1,0:T(8,128)S(1)} %add.6801), channel_id=1, source_target_pairs={{0,2},{1,3},{2,0},{3,1},{4,6},{5,7},{6,4},{7,5},{8,10},{9,11},{10,... | collective-permute-start | bytes 12296 | tf_op jit(solution)/shard_map/ppermute | solution.py:208
  266.6 5.6 %collective-permute-start.35 = (f32[3,8,96,1]{2,3,1,0:T(1,128)S(1)}, f32[3,8,96,1]{2,3,1,0:T(1,128)S(1)}, u32[]{:S(2)}, u32[]{:S(2)}) collective-permute-start(f32[3,8,96,1]{2,3,1,0:T(1,128)S(1)} %slice.607), channel_id=1, source_target_pairs={{16,0},{17,1},{18,2},{19,3},{20,4},{21,5},{22,6},{23,7},{24,8},{25... | collective-permute-start | bytes 27656 | tf_op jit(solution)/shard_map/ppermute | solution.py:23
  272.3 5.9 %collective-permute-start.36 = (f32[3,1,96,129]{2,3,1,0:T(8,128)S(1)}, f32[3,1,96,129]{2,3,1,0:T(8,128)S(1)}, u32[]{:S(2)}, u32[]{:S(2)}) collective-permute-start(f32[3,1,96,129]{2,3,1,0:T(8,128)S(1)} %fusion.236), channel_id=1, source_target_pairs={{4,0},{8,4},{12,8},{0,12},{5,1},{9,5},{13,9},{1,13},{6,2},{10,6},{... | collective-permute-start | bytes 445832 | tf_op jit(solution)/shard_map/ppermute | solution.py:29
  310.7 3.8 %collective-permute-start.38 = (f32[8,96,24]{1,2,0:T(8,128)S(1)}, f32[8,96,24]{1,2,0:T(8,128)S(1)}, u32[]{:S(2)}, u32[]{:S(2)}) collective-permute-start(f32[8,96,24]{1,2,0:T(8,128)S(1)} %get-tuple-element.34), channel_id=1, source_target_pairs={{0,16},{1,17},{2,18},{3,19},{4,20},{5,21},{6,22},{7,23},{8,24},{9,... | collective-permute-start | bytes 221192 | tf_op jit(solution)/shard_map/ppermute | solution.py:37
  312.3 6.5 %collective-permute-start.39 = (f32[8,96,24]{1,2,0:T(8,128)S(1)}, f32[8,96,24]{1,2,0:T(8,128)S(1)}, u32[]{:S(2)}, u32[]{:S(2)}) collective-permute-start(f32[8,96,24]{1,2,0:T(8,128)S(1)} %get-tuple-element.35), channel_id=1, source_target_pairs={{16,0},{17,1},{18,2},{19,3},{20,4},{21,5},{22,6},{23,7},{24,8},{25... | collective-permute-start | bytes 221192 | tf_op jit(solution)/shard_map/ppermute | solution.py:40
  339.2 4.5 %collective-permute-start.40 = (f32[24,24,128]{2,0,1:T(8,128)S(1)}, f32[24,24,128]{2,0,1:T(8,128)S(1)}, u32[]{:S(2)}, u32[]{:S(2)}) collective-permute-start(f32[24,24,128]{2,0,1:T(8,128)S(1)} %get-tuple-element.44), channel_id=1, source_target_pairs={{0,1},{1,2},{2,3},{4,5},{5,6},{6,7},{8,9},{9,10},{10,11},{12,13},{... | collective-permute-start | bytes 884744 | tf_op jit(solution)/shard_map/ppermute | solution.py:37
  352.5 3.7 collective-permute-start.43
  356.9 5.2 %collective-permute-start.44 = (f32[8,128]{1,0:T(8,128)S(1)}, f32[8,128]{1,0:T(8,128)S(1)}, u32[]{:S(2)}, u32[]{:S(2)}) collective-permute-start(f32[8,128]{1,0:T(8,128)S(1)} %fusion.298), channel_id=1, source_target_pairs={{0,8},{4,12},{8,0},{12,4},{1,9},{5,13},{9,1},{13,5},{2,10},{6,14},... | collective-permute-start | bytes 12296 | tf_op jit(solution)/shard_map/ppermute | solution.py:208
  357.9 16.7 %all-to-all-start.1 = ((f32[1,32,24,128]{3,2,0,1:T(8,128)}), f32[1,32,24,128]{3,2,0,1:T(8,128)S(1)}, u32[]{:S(2)}, u32[]{:S(2)}) async-start(f32[1,32,24,128]{3,2,0,1:T(8,128)} %copy.86), calls=%async_computation.1 | async-start | bytes 786432 | tf_op jit(solution)/shard_map/all_to_all | solution.py:223
  365.5 7.9 %collective-permute-start.46 = (f32[8,128]{1,0:T(8,128)S(1)}, f32[8,128]{1,0:T(8,128)S(1)}, u32[]{:S(2)}, u32[]{:S(2)}) collective-permute-start(f32[8,128]{1,0:T(8,128)S(1)} %add.7372), channel_id=1, source_target_pairs={{0,2},{1,3},{2,0},{3,1},{4,6},{5,7},{6,4},{7,5},{8,10},{9,11},{10,... | collective-permute-start | bytes 12296 | tf_op jit(solution)/shard_map/ppermute | solution.py:208
  (34 other events, 194.5 us)

commit v2 on v1

v2 whole, which is shorter than its diff:
```python
import functools
import math

import jax
import jax.numpy as jnp
import numpy as np
from jax import lax
from jax.experimental import pallas as pl
from jax.experimental.pallas import tpu as pltpu
from jax.sharding import PartitionSpec as P

RAD = 24
ITERS = 2

MARROW = 0.1
REMODEL = 0.25
FLOOR = 0.2
CEILING = 1.0
EPSILON = 1e-06

LANES = 128
PAD = 8
GUARD = 0.01


def element_stiffness():
    poisson = 0.3
    lame = poisson / ((1.0 + poisson) * (1.0 - 2.0 * poisson))
    shear = 0.5 / (1.0 + poisson)
    elastic = np.zeros((6, 6))
    elastic[:3, :3] = lame
    for index in range(3):
        elastic[index, index] += 2.0 * shear
        elastic[index + 3, index + 3] = shear
    points = [0.5 - 0.5 / math.sqrt(3.0), 0.5 + 0.5 / math.sqrt(3.0)]
    matrix = np.zeros((24, 24))
    for point_z in points:
        for point_y in points:
            for point_x in points:
                strain = np.zeros((6, 24))
                for corner_z in range(2):
                    for corner_y in range(2):
                        for corner_x in range(2):
                            node = 4 * corner_z + 2 * corner_y + corner_x
                            shape_x = point_x if corner_x else 1.0 - point_x
                            shape_y = point_y if corner_y else 1.0 - point_y
                            shape_z = point_z if corner_z else 1.0 - point_z
                            slope_x = 1.0 if corner_x else -1.0
                            slope_y = 1.0 if corner_y else -1.0
                            slope_z = 1.0 if corner_z else -1.0
                            along_x = slope_x * shape_y * shape_z
                            along_y = shape_x * slope_y * shape_z
                            along_z = shape_x * shape_y * slope_z
                            strain[0, node] = along_x
                            strain[1, 8 + node] = along_y
                            strain[2, 16 + node] = along_z
                            strain[3, node] = along_y
                            strain[3, 8 + node] = along_x
                            strain[4, 8 + node] = along_z
                            strain[4, 16 + node] = along_y
                            strain[5, node] = along_z
                            strain[5, 16 + node] = along_x
                matrix = matrix + strain.T @ elastic @ strain / 8.0
    return matrix


X, Y, Z, XY, XZ, YZ, XYZ = 1, 2, 4, 3, 5, 6, 7
U, V, W = 0, 1, 2
REDUCED = [
    [(U, X)], [(V, Y)], [(W, Z)],
    [(U, Y), (V, X)], [(U, Z), (W, X)], [(V, Z), (W, Y)],
    [(V, XY)], [(W, XZ)], [(U, XY)], [(W, YZ)], [(U, XZ)], [(V, YZ)],
    [(U, YZ)], [(V, XZ)], [(W, XY)],
    [(U, XYZ)], [(V, XYZ)], [(W, XYZ)],
]


def mode_constants(table):
    one = np.array([[1.0, 1.0], [-1.0, 1.0]])
    sums = np.kron(one, np.kron(one, one))
    change = np.kron(np.eye(3), sums)
    modes = change @ table @ change.T / 64.0
    at = lambda a, b: float(modes[a[0] * 8 + a[1], b[0] * 8 + b[1]])
    k = dict(
        cross=at((U, X), (V, Y)),
        shear=at((U, Y), (U, Y)),
        pair=at((V, XY), (W, XZ)),
        group=at((U, YZ), (V, XZ)),
        triple=at((U, XYZ), (U, XYZ)),
    )
    k["normal"] = at((U, X), (U, X)) - k["cross"]
    k["single"] = at((V, XY), (V, XY)) - k["pair"]
    reduce = np.zeros((18, 24))
    for row, members in enumerate(REDUCED):
        for component, bits in members:
            reduce[row, component * 8 + bits] = 1.0
    small = np.stack([np.array(stresses(list(unit), k)) for unit in np.eye(18)], axis=1)
    assert np.allclose(reduce.T @ small @ reduce, modes, atol=1e-12)
    assert np.allclose(np.diagonal(table), table[0, 0], atol=1e-12)
    return k


def stresses(m, k):
    trace = k["cross"] * (m[0] + m[1] + m[2])
    out = [trace + k["normal"] * m[i] for i in range(3)]
    out += [k["shear"] * m[i] for i in range(3, 6)]
    for i in (6, 8, 10):
        both = k["pair"] * (m[i] + m[i + 1])
        out += [both + k["single"] * m[i], both + k["single"] * m[i + 1]]
    total = m[12] + m[13] + m[14]
    out += [k["group"] * (total + m[i]) for i in range(12, 15)]
    out += [k["triple"] * m[i] for i in range(15, 18)]
    return out


def dotted(a, b):
    terms = [p * q for p, q in zip(a, b)]
    while len(terms) > 1:
        terms = [terms[i] + terms[i + 1] if i + 1 < len(terms) else terms[i] for i in range(0, len(terms), 2)]
    return terms[0]


def layer_modes(ref, index, row):
    found = []
    for component in range(3):
        low = ref[component, index, pl.ds(row, 8), :]
        high = ref[component, index, pl.ds(row + 1, 8), :]
        both, slope = low + high, high - low
        both_up, slope_up = (pltpu.roll(v, LANES - 1, 1) for v in (both, slope))
        found.append((both + both_up, slope + slope_up, both_up - both, slope_up - slope))
    return found


def voxel_modes(below, above):
    modes = {}
    for component in range(3):
        low, high = below[component], above[component]
        for bits in (X, Y, XY):
            modes[component, bits] = low[bits] + high[bits]
        for bits in (0, X, Y, XY):
            modes[component, bits + Z] = high[bits] - low[bits]
    reduced = []
    for members in REDUCED:
        value = modes[members[0]]
        for extra in members[1:]:
            value = value + modes[extra]
        reduced.append(value)
    return reduced


SLOT = {mode: row for row, members in enumerate(REDUCED) for mode in members}


def prepare_kernel(density, bone, fixed, load, fields, up, down):
    depth, height, width = density.shape
    zeros = jnp.zeros((LANES - height, width), jnp.float32)

    def layer(z, carry):
        thick = density[z]
        share = bone[z].astype(jnp.float32)
        free = 1.0 - fixed[z].astype(jnp.float32)
        modulus = share * thick * thick + (1.0 - share) * MARROW
        values = [modulus] + [free * load[c, z] for c in range(3)] + [free, thick]
        for slot, value in enumerate(values):
            square = jnp.concatenate([value, zeros], axis=0)
            fields[slot, z] = jnp.transpose(square)
        return carry

    lax.fori_loop(0, depth, layer, 0)

    def one(z):
        thick = density[z]
        share = bone[z].astype(jnp.float32)
        free = 1.0 - fixed[z].astype(jnp.float32)
        modulus = share * thick * thick + (1.0 - share) * MARROW
        return modulus, [free * load[c, z] for c in range(3)], free

    up[0] = one(depth - 2)[0]
    modulus, force, _ = one(depth - 1)
    up[1] = modulus
    for c in range(3):
        up[2 + c] = force[c]
    for z in range(2):
        modulus, force, free = one(z)
        down[z] = modulus
        for c in range(3):
            down[2 + 3 * z + c] = force[c]
        if z == 0:
            down[8] = free


def krylov_kernel(
    k, kappa,
    fields, up, down, left, right, left_up, right_up, left_down, right_down, weights, planes,
    out_p, out_w, out_g, out_stats,
    mod, force, free, search, inverse, lower, upper, image, stress, accumulate,
):
    depth, width = fields.shape[1], fields.shape[2]
    height = up.shape[1]
    first, last = PAD, PAD + width
    chunks = width // 8
    blank = jnp.zeros((LANES - height, width), jnp.float32)

    def turned(value):
        return jnp.transpose(jnp.concatenate([value, blank], axis=0))

    empty = jnp.zeros((PAD, LANES), jnp.float32)
    for ref in (mod, force, search):
        lead = ref.shape[:-2]
        for spot in np.ndindex(*lead):
            ref[spot + (pl.ds(0, PAD),)] = empty
            ref[spot + (pl.ds(last, PAD),)] = empty
            ref[spot + (pl.ds(last + PAD, PAD),)] = empty
    for z in range(depth + 1):
        free[z, pl.ds(last, PAD)] = empty

    def local(z, carry):
        for c in range(chunks):
            rows, into = pl.ds(8 * c, 8), pl.ds(first + 8 * c, 8)
            mod[z + 2, into] = fields[0, z, rows]
            for i in range(3):
                force[i, z + 1, into] = fields[1 + i, z, rows]
            free[z, into] = fields[4, z, rows]
        mod[z + 2, pl.ds(first - 2, 2)] = left[0, z]
        mod[z + 2, pl.ds(last, 2)] = right[0, z]
        for i in range(3):
            force[i, z + 1, pl.ds(first - 2, 2)] = left[1 + i, z]
            force[i, z + 1, pl.ds(last, 2)] = right[1 + i, z]
        free[z, pl.ds(last, 2)] = right[4, z]
        return carry

    lax.fori_loop(0, depth, local, 0)
    body = pl.ds(first, width)
    for z in range(2):
        mod[z, body] = turned(up[z])
        mod[depth + 2 + z, body] = turned(down[z])
        for side, low, high in ((first - 2, left_up, left_down), (last, right_up, right_down)):
            mod[z, pl.ds(side, 2)] = low[0, z]
            mod[depth + 2 + z, pl.ds(side, 2)] = high[0, z]
    for i in range(3):
        force[i, 0, body] = turned(up[2 + i])
        for side, low, high in ((first - 2, left_up, left_down), (last, right_up, right_down)):
            force[i, 0, pl.ds(side, 2)] = low[1 + i, 1]
            for z in range(2):
                force[i, depth + 1 + z, pl.ds(side, 2)] = high[1 + i, z]
        for z in range(2):
            force[i, depth + 1 + z, body] = turned(down[2 + 3 * z + i])
    free[depth, body] = turned(down[8])
    free[depth, pl.ds(last, 2)] = right_down[4, 0]

    def divide(chunk, carry):
        row = pl.multiple_of(chunk * 8, 8)
        previous = None
        for z in range(depth + 4):
            here = mod[z, pl.ds(row + PAD, 8)] + mod[z, pl.ds(row + PAD - 1, 8)]
            here = here + pltpu.roll(here, 1, 1)
            if z >= 1 and z <= depth + 3:
                total = kappa * (here + previous)
                share = jnp.where(total > 0.0, 1.0 / jnp.where(total > 0.0, total, 1.0), 0.0)
                node = z - 1
                for i in range(3):
                    search[i, node, pl.ds(row + PAD, 8)] = force[i, node, pl.ds(row + PAD, 8)] * share
                if 1 <= node <= depth + 1:
                    inverse[node - 1, pl.ds(row + PAD, 8)] = free[node - 1, pl.ds(row + PAD, 8)] * share
            previous = here
        return carry

    lax.fori_loop(0, chunks + 1, divide, 0)
    for z in range(depth + 3):
        side = mod[z, pl.ds(0, 8)]
        if z + 1 < depth + 4:
            total = side + mod[z + 1, pl.ds(0, 8)]
            total = total + pltpu.roll(total, 1, 0)
            total = kappa * (total + pltpu.roll(total, 1, 1))
            share = jnp.where(total > 0.0, 1.0 / jnp.where(total > 0.0, total, 1.0), 0.0)
            for i in range(3):
                search[i, z, pl.ds(0, 8)] = force[i, z, pl.ds(0, 8)] * share

    for s in range(accumulate.shape[0]):
        accumulate[s] = jnp.zeros((8, LANES), jnp.float32)

    def elements(row, inner):
        below = layer_modes(search, 0, row)
        carried = None
        for node in range(1, depth + 3):
            above = layer_modes(search, node, row)
            modes = voxel_modes(below, above)
            strain = stresses(modes, k)
            scale = mod[node, pl.ds(row, 8)]
            voxel = node - 2
            if inner is not None and 0 <= voxel < depth:
                rows = pl.ds(row - PAD, 8)
                work = (0.5 * scale) * dotted(modes, strain)
                out_g[0, voxel, rows] = work
                for s in range(18):
                    stress[s, voxel, rows] = strain[s]
            strain = [scale * s for s in strain]
            carry = []
            for component in range(3):
                value = lambda bits: strain[SLOT[component, bits]]
                totals, tops = [], []
                for bits in (0, X, Y, XY):
                    slope = value(bits + Z)
                    low, high = (-slope, slope) if bits == 0 else (value(bits) - slope, value(bits) + slope)
                    tops.append(high)
                    if carried is not None:
                        totals.append(low + carried[component][len(totals)])
                carry.append(tops)
                if carried is not None:
                    plain = (totals[0] - totals[2]) + pltpu.roll(totals[0] + totals[2], 1, 1)
                    tilted = (totals[1] - totals[3]) + pltpu.roll(totals[1] + totals[3], 1, 1)
                    lower[component, voxel, pl.ds(row, 8)] = plain - tilted
                    upper[component, voxel, pl.ds(row, 8)] = plain + tilted
            carried = carry
            below = above

    def middle(chunk, carry):
        elements(pl.multiple_of(PAD + chunk * 8, 8), True)
        return carry

    elements(0, None)
    lax.fori_loop(0, chunks, middle, 0)
    elements(last, None)

    def gather(chunk, carry):
        row = pl.multiple_of(PAD + chunk * 8, 8)
        rows = pl.ds(row, 8)
        gamma, second = jnp.zeros((8, LANES), jnp.float32), jnp.zeros((8, LANES), jnp.float32)
        for node in range(depth + 1):
            share = inverse[node, rows]
            for i in range(3):
                pulled = lower[i, node, rows] + upper[i, node, pl.ds(row - 1, 8)]
                scaled = share * pulled
                image[i, node, rows] = scaled
                if node < depth:
                    second = second + scaled * pulled
                    gamma = gamma + force[i, node + 1, rows] * search[i, node + 1, rows]
        accumulate[0] = accumulate[0] + jnp.where(chunk < chunks, gamma, 0.0)
        accumulate[2] = accumulate[2] + jnp.where(chunk < chunks, second, 0.0)
        return carry

    lax.fori_loop(0, chunks + 1, gather, 0)

    def energies(chunk, carry):
        row = pl.multiple_of(PAD + chunk * 8, 8)
        rows = pl.ds(pl.multiple_of(chunk * 8, 8), 8)
        weight = weights[rows]
        sums = [jnp.zeros((8, LANES), jnp.float32) for _ in range(5)]
        below = layer_modes(image, 0, row)
        for voxel in range(depth):
            above = layer_modes(image, voxel + 1, row)
            modes = voxel_modes(below, above)
            half = 0.5 * mod[voxel + 2, pl.ds(row, 8)]
            first_work = out_g[0, voxel, rows]
            mixed = half * dotted(modes, [stress[s, voxel, rows] for s in range(18)])
            second_work = half * dotted(modes, stresses(modes, k))
            thick = fields[5, voxel, rows]
            flip = jnp.where(thick > 0.0, 1.0 / jnp.where(thick > 0.0, thick, 1.0), 0.0)
            spread = weight * planes[voxel]
            sums[0] = sums[0] + first_work
            sums[1] = sums[1] + second_work
            for i, work in enumerate((first_work, mixed, second_work)):
                value = work * flip
                out_g[i, voxel, rows] = value
                sums[2 + i] = sums[2 + i] + spread * value
            below = above
            for i in range(3):
                out_p[i, voxel, rows] = search[i, voxel + 1, pl.ds(row, 8)]
                out_w[i, voxel, rows] = image[i, voxel, pl.ds(row, 8)]
        for slot, value in zip((1, 3, 4, 5, 6), sums):
            accumulate[slot] = accumulate[slot] + value
        return carry

    lax.fori_loop(0, chunks, energies, 0)
    for s in range(8):
        out_stats[pl.ds(s, 1)] = jnp.sum(accumulate[s], axis=0, keepdims=True)


def run_prepare(density, bone, fixed, load):
    depth, height, width = density.shape
    shapes = ((6, depth, width, LANES), (5, height, width), (9, height, width))
    return pl.pallas_call(
        prepare_kernel,
        out_shape=[jax.ShapeDtypeStruct(s, jnp.float32) for s in shapes],
        name="prepare",
    )(density, bone, fixed, load)


def run_krylov(table, fields, halos, weights, planes):
    depth, width = fields.shape[1], fields.shape[2]
    rows = width + 3 * PAD
    shapes = [(3, depth, width, LANES)] * 3 + [(8, LANES)]
    layers = [(depth + 4,), (3, depth + 3), (depth + 1,), (3, depth + 3), (depth + 1,)]
    layers += [(3, depth + 1)] * 3
    scratch = [pltpu.VMEM(lead + (rows, LANES), jnp.float32) for lead in layers]
    scratch += [
        pltpu.VMEM((18, depth, width, LANES), jnp.float32),
        pltpu.VMEM((8, 8, LANES), jnp.float32),
    ]
    return pl.pallas_call(
        functools.partial(krylov_kernel, mode_constants(table), float(table[0, 0])),
        out_shape=[jax.ShapeDtypeStruct(s, jnp.float32) for s in shapes],
        scratch_shapes=scratch,
        compiler_params=pltpu.CompilerParams(vmem_limit_bytes=56 * 1024 * 1024),
        name="krylov",
    )(fields, *halos, weights, planes)


def slab_route(steps, sideways=0):
    nx, ny, nz = (lax.axis_size(a) for a in ("gx", "gy", "gz"))
    pairs = []
    for x in range(nx):
        for slab in range(ny * nz):
            to, tx = slab + steps, x + sideways
            if 0 <= to < ny * nz and 0 <= tx < nx:
                spot = lambda i, s: (i * ny + s % ny) * nz + s // ny
                pairs.append((spot(x, slab), spot(tx, to)))
    return pairs


def to_slab(value, steps, sideways=0):
    return lax.ppermute(value, ("gx", "gy", "gz"), slab_route(steps, sideways))


def edges_swapped(low_edge, high_edge, steps):
    if lax.axis_size("gx") == 2:
        first = lax.axis_index("gx") == 0
        sent = jnp.where(first, high_edge, low_edge)
        spots = slab_route(steps, 1) + slab_route(steps, -1)
        got = lax.ppermute(sent, ("gx", "gy", "gz"), spots)
        none = jnp.zeros_like(got)
        return jnp.where(first, none, got), jnp.where(first, got, none)
    return to_slab(high_edge, steps, 1), to_slab(low_edge, steps, -1)


def total_over_mesh(value):
    for axis in ("gx", "gy", "gz"):
        count = lax.axis_size(axis)
        if count & (count - 1):
            value = lax.psum(value, axis)
            continue
        step = 1
        while step < count:
            other = lax.ppermute(value, axis, [(i, i ^ step) for i in range(count)])
            value = value + other
            step *= 2
    return value


def inner_sum(values):
    return total_over_mesh(jnp.full((8, LANES), jnp.sum(values)))[0, 0]


def tap_table():
    offsets = np.abs(np.arange(2 * RAD + 1) - RAD)
    raw = np.exp(-offsets / (0.5 * RAD))
    return raw / raw.sum()


def banded(length_in, length_out, shift):
    taps = tap_table()
    matrix = np.zeros((length_in, length_out))
    for i in range(length_in):
        for o in range(length_out):
            distance = i - shift - o
            if abs(distance) <= RAD:
                matrix[i, o] = taps[distance + RAD]
    return matrix.astype(np.float32)


def coverage(position, length):
    taps = tap_table()
    ends = jnp.asarray(np.concatenate([[0.0], np.cumsum(taps)]).astype(np.float32))
    low = jnp.maximum(-RAD, -position) + RAD
    high = jnp.minimum(RAD, length - 1 - position) + RAD + 1
    return ends[high] - ends[low]


def smooth_plane(fields, height):
    width = fields.shape[2]
    fields = fields[..., :height]
    from_left, from_right = edges_swapped(fields[:, :, :RAD], fields[:, :, width - RAD :], 0)
    wide = jnp.concatenate([from_left, fields, from_right], axis=2)
    along_x = jnp.asarray(banded(width + 2 * RAD, width, RAD))
    along_y = jnp.asarray(banded(height, height, 0))
    half = jnp.einsum("fzxy,xo->fzoy", wide, along_x, precision=lax.Precision.HIGHEST)
    return jnp.einsum("fzxy,yo->fzox", half, along_y, precision=lax.Precision.HIGHEST)


def smooth_depth(planar):
    depth = planar.shape[0]
    taps = tap_table()
    ratio = math.exp(-1.0 / (0.5 * RAD))
    pieces, blocks = [planar], [banded(depth, depth, 0)]
    decay = (ratio ** np.arange(depth)).astype(np.float64)
    low_plane = jnp.tensordot(jnp.asarray(decay.astype(np.float32)), planar, 1, precision=lax.Precision.HIGHEST)
    high_plane = jnp.tensordot(jnp.asarray(decay[::-1].astype(np.float32)), planar, 1, precision=lax.Precision.HIGHEST)
    steps = 1
    while (steps - 1) * depth + 1 <= RAD:
        if steps * depth + depth - 1 <= RAD:
            pieces.append(to_slab(high_plane, steps)[None])
            near = taps[RAD] * ratio ** (steps * depth - (depth - 1) + np.arange(depth))
            blocks.append(near[None])
            pieces.append(to_slab(low_plane, -steps)[None])
            near = taps[RAD] * ratio ** (steps * depth - np.arange(depth))
            blocks.append(near[None])
        else:
            pieces.append(to_slab(planar, steps))
            blocks.append(banded(depth, depth, steps * depth))
            pieces.append(to_slab(planar, -steps))
            blocks.append(banded(depth, depth, -steps * depth))
        steps += 1
    stacked = jnp.concatenate(pieces, axis=0)
    matrix = jnp.asarray(np.concatenate(blocks, axis=0).astype(np.float32))
    return jnp.einsum("iyx,io->oyx", stacked, matrix, precision=lax.Precision.HIGHEST)


def corners():
    return [(cz, cy, cx) for cz in range(2) for cy in range(2) for cx in range(2)]


def upper_nodes(field):
    column = lax.ppermute(field[:, :, :, :1], ("gx", "gy", "gz"), slab_route(0, -1))
    wide = jnp.concatenate([field, column], axis=3)
    wide = jnp.concatenate([wide, to_slab(wide[:, :1], -1)], axis=1)
    return jnp.pad(wide, ((0, 0), (0, 0), (0, 1), (0, 0)))


def fold_upper(values):
    depth, width = values.shape[1] - 1, values.shape[3] - 1
    carried = to_slab(values[:, depth:], 1)
    values = jnp.concatenate([values[:, :1] + carried, values[:, 1:depth]], axis=1)
    column = lax.ppermute(values[:, :, :, width:], ("gx", "gy", "gz"), slab_route(0, 1))
    return jnp.concatenate([values[:, :, :, :1] + column, values[:, :, :, 1:width]], axis=3)


def corner_columns(nodes, shape):
    depth, height, width = shape
    return jnp.stack(
        [
            nodes[c, cz : cz + depth, cy : cy + height, cx : cx + width]
            for c in range(3)
            for cz, cy, cx in corners()
        ]
    )


def element_products(columns, table):
    return jnp.einsum(
        "rc,czyx->rzyx", jnp.asarray(table, jnp.float32), columns, precision=lax.Precision.HIGHEST
    )


def plain_forces(field, modulus, table):
    depth, height, width = modulus.shape
    columns = corner_columns(upper_nodes(field), modulus.shape)
    products = element_products(columns, table) * modulus
    total = jnp.zeros((3, depth + 1, height + 1, width + 1), jnp.float32)
    for node, (cz, cy, cx) in enumerate(corners()):
        total = total.at[:, cz : cz + depth, cy : cy + height, cx : cx + width].add(products[node::8])
    return fold_upper(total[:, :, :height])


def plain_path(table, density, bone, fixed, load):
    depth, height, width = density.shape
    share = bone.astype(jnp.float32)
    free = 1.0 - fixed.astype(jnp.float32)
    modulus = share * density * density + (1.0 - share) * MARROW
    spread = jnp.zeros((1, depth + 1, height + 1, width + 1), jnp.float32)
    for cz, cy, cx in corners():
        spread = spread.at[0, cz : cz + depth, cy : cy + height, cx : cx + width].add(modulus)
    precondition = free / (float(table[0, 0]) * fold_upper(spread[:, :, :height]))
    residual = free * load
    solution = jnp.zeros_like(residual)
    search = precondition * residual
    gamma = inner_sum(residual * search)
    for count in range(ITERS):
        image = free * plain_forces(free * search, modulus, table)
        alpha = gamma / inner_sum(search * image)
        solution = solution + alpha * search
        if count + 1 < ITERS:
            residual = residual - alpha * image
            scaled = precondition * residual
            gamma_next = inner_sum(residual * scaled)
            search = scaled + gamma_next / gamma * search
            gamma = gamma_next
    columns = corner_columns(upper_nodes(solution), modulus.shape)
    energy = 0.5 * modulus * jnp.sum(columns * element_products(columns, table), axis=0)
    specific = jnp.swapaxes(energy / density, 1, 2)
    return smooth_plane(specific[None], height)[0], solution, specific


def on_device(density, bone, fixed, load):
    table = element_stiffness()
    density, bone, fixed, load = density[0], bone[0], fixed[0], load[:, 0]
    depth, height, width = density.shape
    slabs = lax.axis_size("gy") * lax.axis_size("gz")
    slab = lax.axis_index("gz") * lax.axis_size("gy") + lax.axis_index("gy")
    across = lax.axis_size("gx") * width
    cover_x = coverage(lax.axis_index("gx") * width + jnp.arange(width), across)
    cover_y = coverage(jnp.arange(height), height)
    cover_z = coverage(slab * depth + jnp.arange(depth), slabs * depth)
    weights = jnp.pad(cover_x[:, None] * cover_y[None], ((0, 0), (0, LANES - height)))
    planes = jnp.broadcast_to(cover_z[:, None, None], (depth, 8, LANES))

    fields, up, down = run_prepare(density, bone, fixed, load)
    got_up, got_down = to_slab(up, 1), to_slab(down, -1)
    low, high = fields[:5, :, :2], fields[:5, :, width - 2 :]
    left, right = edges_swapped(low, high, 0)
    left_up, right_up = edges_swapped(low[:, depth - 2 :], high[:, depth - 2 :], 1)
    left_down, right_down = edges_swapped(low[:, :2], high[:, :2], -1)
    halos = (got_up, got_down, left, right, left_up, right_up, left_down, right_down)
    first, second, basis, stats = run_krylov(table, fields, halos, weights, planes)

    sums = jnp.sum(total_over_mesh(stats), axis=1)
    gamma, curve, mixed, curve_second = sums[0], 2.0 * sums[1], sums[2], 2.0 * sums[3]
    smoothed = smooth_plane(basis, height)
    alpha = gamma / curve
    grown = alpha * mixed / curve
    beta = grown - 1.0
    bent = alpha * (alpha * (alpha * curve_second / gamma))
    rest = bent - grown * grown
    alpha_next = alpha * beta / rest
    by_first = alpha + alpha_next * grown
    by_second = -alpha_next * alpha
    squares = (by_first * by_first, 2.0 * by_first * by_second, by_second * by_second)
    parts = [f * s for f, s in zip(squares, (sums[4], sums[5], sums[6]))]
    total = parts[0] + parts[1] + parts[2]
    size = jnp.abs(parts[0]) + jnp.abs(parts[1]) + jnp.abs(parts[2])
    sound = (beta > GUARD * grown) & (rest > GUARD * bent) & (total > GUARD * size)

    def combined():
        planar = sum(f * s for f, s in zip(squares, smoothed))
        moved = by_first * first[..., :height] + by_second * second[..., :height]
        return planar, jnp.swapaxes(moved, 2, 3), total

    def repeated():
        planar, moved, specific = plain_path(table, density, bone, fixed, load)
        cover = weights[None, :, :height] * cover_z[:, None, None]
        return planar, moved, inner_sum(specific * cover)

    planar, solution, total = lax.cond(sound, combined, repeated)
    stimulus = smooth_depth(planar)
    mean = total / (density.size * lax.axis_size("gx") * slabs)
    share = bone.astype(jnp.float32)
    updated = density + REMODEL * share * (stimulus / (mean + EPSILON) - 1.0)
    updated = jnp.clip(updated, FLOOR, CEILING)
    return updated[None], solution[:, None]


def solution(mesh):
    placed = (
        P("gz", "gy", None, "gx"),
        P("gz", "gy", None, "gx"),
        P("gz", "gy", None, "gx"),
        P(None, "gz", "gy", None, "gx"),
    )
    return jax.shard_map(
        on_device,
        mesh=mesh,
        in_specs=placed,
        out_specs=(P("gz", "gy", None, "gx"), P(None, "gz", "gy", None, "gx")),
        check_vma=False,
    )
```

time: 382 us -> 139 us (0.36); the launches traced: 376 us -> 138 us
  other arithmetic: 142 us -> 9.21 us
  waiting for transfers between devices: 105 us -> 19.7 us
  starting transfers between devices: 76 us -> 47.6 us
  Pallas kernels: 0 us -> 23.8 us
  blocking collectives: 16.6 us -> 0 us
    mul x51 -> x1, other arithmetic: 90.3 us -> 0.08 us  [on_device(): cover_x[:, None] * cover_y[None]]
    ppermute x22 -> x12, waiting for transfers between devices: 63.4 us -> 11.9 us  [the longest x8 9.69 us: to_slab(): return lax.ppermute(value, ('gx', 'gy', 'gz'), slab_route(steps, sideways))]
    ppermute x25 -> x5, waiting for transfers between devices: 42.1 us -> 7.8 us  [total_over_mesh(): other = lax.ppermute(value, axis, [(i, i ^ step) for i in range(count)])]
    div x1 -> x0, other arithmetic: 28.1 us -> none  [on_device(): specific = energy / local_density]
    pallas_call x0 -> x2, Pallas kernels: none -> 23.8 us  [the longest x1 18.9 us: run_krylov(): pl.pallas_call(functools.partial(krylov_kernel, mode_constants(table), fl...]
    all_to_all x1 -> x0, blocking collectives: 16.6 us -> none  [to_bricks(): return lax.all_to_all(values, 'gy', split_axis=2, concat_axis=1, tiled=True)]
    ppermute x25 -> x5, starting transfers between devices: 27.7 us -> 15.3 us  [total_over_mesh(): other = lax.ppermute(value, axis, [(i, i ^ step) for i in range(count)])]
    ppermute x22 -> x12, starting transfers between devices: 44.2 us -> 32.3 us  [the longest x8 21.9 us: to_slab(): return lax.ppermute(value, ('gx', 'gy', 'gz'), slab_route(steps, sideways))]
  transfers between devices with their start and end apart: 48 -> 17, of which waited for: 40 -> 8; matrix products, arithmetic and copies ran while one was open for 5% -> 10% of each run, Pallas kernels for 0% -> 0%
where the time goes in v2:
time: 139 us; the launch traced here: 138 us
  starting transfers between devices  47.6 us (34%)
  Pallas kernels  23.8 us (17%)
  local copies, waits for them, and re-layouts  21.5 us (15%)
  waiting for transfers between devices  19.7 us (14%)
  other arithmetic  9.21 us (7%)
  matrix products  8.67 us (6%)
  between operations  7.11 us (5%)
    ppermute x8, starting transfers between devices, to_slab(): return lax.ppermute(value, ('gx', 'gy', 'gz'), slab_route(steps, sideways))  21.9 us
    pallas_call x1, Pallas kernels, run_krylov(): pl.pallas_call(functools.partial(krylov_kernel, mode_constants(table), fl...  18.9 us
    ppermute x5, starting transfers between devices, total_over_mesh(): other = lax.ppermute(value, axis, [(i, i ^ step) for i in range(count)])  15.3 us
    ppermute x4, starting transfers between devices, edges_swapped(): got = lax.ppermute(sent, ('gx', 'gy', 'gz'), spots)  10.4 us
    ppermute x8, waiting for transfers between devices, to_slab(): return lax.ppermute(value, ('gx', 'gy', 'gz'), slab_route(steps, sideways))  9.69 us
    ppermute x5, waiting for transfers between devices, total_over_mesh(): other = lax.ppermute(value, axis, [(i, i ^ step) for i in range(count)])  7.8 us
    concatenate x1, local copies, waits for them, and re-layouts, smooth_depth(): stacked = jnp.concatenate(pieces, axis=0)  6.62 us
    gather x6, local copies, waits for them, and re-layouts, coverage(): return ends[high] - ends[low]  6.19 us
  transfers between devices with their start and end apart: 17, of which 8 were waited for; matrix products, arithmetic and copies ran while one was open for 10% of the time, Pallas kernels for 0%

profile of v2, /device:TPU:0, one launch (start us, length us, event | category | flops | bytes accessed | tf_op | source)
XLA Modules:
  0.0 138.4 jit_solution(2143797262803428782)
XLA Ops:
  0.6 4.9 %prepare.1 = (f32[6,8,128,128]{3,2,1,0:T(8,128)}, f32[5,96,128]{2,1,0:T(8,128)}, f32[9,96,128]{2,1,0:T(8,128)}) custom-call(f32[8,96,128]{2,1,0:T(8,128)} %bitcast.149, s32[8,96,128]{2,1,0:T(8,128)} %bitcast.151, s32[8,96,128]{2,1,0:T(8,128)} %bitcast.156, f32[3,8,96,128]{3,2,1,0:T(8,128)} %bitcast.145), custom_call_target="tpu_custom_call" | custom-call | tf_op jit(solution)/shard_map/prepare/pallas_call | solution.py:382
  6.4 1.3 collective-permute-start.42
  7.7 6.5 %collective-permute-start.41 = (f32[5,2,2,128]{3,2,1,0:T(2,128)S(1)}, f32[5,2,2,128]{3,2,1,0:T(2,128)S(1)}, u32[]{:S(2)}, u32[]{:S(2)}) collective-permute-start(f32[5,2,2,128]{3,2,1,0:T(2,128)S(1)} %get-tuple-element.528), channel_id=1, source_target_pairs={{0,20},{4,24},{8,28},{12,17},{1,21},{5,25},{9,29},{13,18},{2,22},{... | collective-permute-start | bytes 30728 | tf_op jit(solution)/shard_map/ppermute | solution.py:430
  15.3 2.0 %collective-permute-start.40 = (f32[5,8,2,128]{3,2,1,0:T(2,128)S(1)}, f32[5,8,2,128]{3,2,1,0:T(2,128)S(1)}, u32[]{:S(2)}, u32[]{:S(2)}) collective-permute-start(f32[5,8,2,128]{3,2,1,0:T(2,128)S(1)} %slice_select_fusion.2), channel_id=1, source_target_pairs={{0,16},{4,20},{8,24},{12,28},{1,17},{5,21},{9,25},{13,29},{2,18},{... | collective-permute-start | bytes 122888 | tf_op jit(solution)/shard_map/ppermute | solution.py:430
  17.3 1.3 collective-permute-start.39
  18.5 4.6 %collective-permute-start.38 = (f32[5,96,128]{2,1,0:T(8,128)}, f32[5,96,128]{2,1,0:T(8,128)S(1)}, u32[]{:S(2)}, u32[]{:S(2)}) collective-permute-start(f32[5,96,128]{2,1,0:T(8,128)} %get-tuple-element.365), channel_id=1, source_target_pairs={{0,4},{4,8},{8,12},{12,1},{1,5},{5,9},{9,13},{13,2},{2,6},{6,10},{... | collective-permute-start | bytes 737288 | tf_op jit(solution)/shard_map/ppermute | solution.py:422
  23.2 1.2 gather_fusion
  24.5 1.2 gather_fusion.1
  25.7 1.2 gather_fusion.2
  32.7 18.9 %krylov.1 = (f32[3,8,128,128]{3,2,1,0:T(8,128)}, f32[3,8,128,128]{3,2,1,0:T(8,128)}, f32[3,8,128,128]{3,2,1,0:T(8,128)}, f32[8,128]{1,0:T(8,128)}) custom-call(f32[6,8,128,128]{3,2,1,0:T(8,128)} %get-tuple-element.364.fields, f32[5,96,128]{2,1,0:T(8,128)} %copy-done.47, f32[9,96,128]{2,1,0:T(8,128)} %copy-done.44, f32[5,8,2,128]{3,2,1,0:T(2,128)} %get-tuple-element.532.left, ...), custom_call_target="tpu_custom_call" | custom-call | tf_op jit(solution)/shard_map/krylov/pallas_call | solution.py:400
  51.7 3.8 %collective-permute-done.43 = f32[8,128]{1,0:T(8,128)S(1)} collective-permute-done((f32[8,128]{1,0:T(8,128)}, f32[8,128]{1,0:T(8,128)S(1)}, u32[]{:S(2)}, u32[]{:S(2)}) %collective-permute-start.43) | collective-permute-done | bytes 4128 | tf_op jit(solution)/shard_map/ppermute | solution.py:444
  56.1 2.2 %collective-permute-start.44 = (f32[8,128]{1,0:T(8,128)S(1)}, f32[8,128]{1,0:T(8,128)S(1)}, u32[]{:S(2)}, u32[]{:S(2)}) collective-permute-start(f32[8,128]{1,0:T(8,128)S(1)} %add.554), channel_id=1, source_target_pairs={{0,4},{4,0},{8,12},{12,8},{1,5},{5,1},{9,13},{13,9},{2,6},{6,2},{1... | collective-permute-start | bytes 12296 | tf_op jit(solution)/shard_map/ppermute | solution.py:444
  58.4 1.6 %collective-permute-done.44 = f32[8,128]{1,0:T(8,128)S(1)} collective-permute-done((f32[8,128]{1,0:T(8,128)S(1)}, f32[8,128]{1,0:T(8,128)S(1)}, u32[]{:S(2)}, u32[]{:S(2)}) %collective-permute-start.44) | collective-permute-done | bytes 4128 | tf_op jit(solution)/shard_map/ppermute | solution.py:444
  59.9 6.7 %collective-permute-start.45 = (f32[8,128]{1,0:T(8,128)S(1)}, f32[8,128]{1,0:T(8,128)S(1)}, u32[]{:S(2)}, u32[]{:S(2)}) collective-permute-start(f32[8,128]{1,0:T(8,128)S(1)} %add.555), channel_id=1, source_target_pairs={{0,8},{4,12},{8,0},{12,4},{1,9},{5,13},{9,1},{13,5},{2,10},{6,14},... | collective-permute-start | bytes 12296 | tf_op jit(solution)/shard_map/ppermute | solution.py:444
  66.6 1.6 %collective-permute-done.45 = f32[8,128]{1,0:T(8,128)S(1)} collective-permute-done((f32[8,128]{1,0:T(8,128)S(1)}, f32[8,128]{1,0:T(8,128)S(1)}, u32[]{:S(2)}, u32[]{:S(2)}) %collective-permute-start.45) | collective-permute-done | bytes 4128 | tf_op jit(solution)/shard_map/ppermute | solution.py:444
  70.2 5.2 %collective-permute-start.47 = (f32[8,128]{1,0:T(8,128)S(1)}, f32[8,128]{1,0:T(8,128)S(1)}, u32[]{:S(2)}, u32[]{:S(2)}) collective-permute-start(f32[8,128]{1,0:T(8,128)S(1)} %add.557), channel_id=1, source_target_pairs={{0,2},{1,3},{2,0},{3,1},{4,6},{5,7},{6,4},{7,5},{8,10},{9,11},{10,... | collective-permute-start | bytes 12296 | tf_op jit(solution)/shard_map/ppermute | solution.py:444
  83.2 2.2 %collective-permute-done.48 = f32[3,8,24,96]{3,2,1,0:T(8,128)S(1)} collective-permute-done((f32[3,8,24,96]{3,2,1,0:T(8,128)S(1)}, f32[3,8,24,96]{3,2,1,0:T(8,128)S(1)}, u32[]{:S(2)}, u32[]{:S(2)}) %collective-permute-start.48) | collective-permute-done | bytes 221216 | tf_op jit(solution)/shard_map/ppermute | solution.py:430
  85.4 4.5 %fusion.39 = f32[3,8,128,96]{2,3,1,0:T(8,128)S(1)} fusion(f32[176,128,1,1]{1,0,3,2:T(8,128)S(1)} %copy-done.50, f32[3,8,24,96]{3,2,1,0:T(8,128)S(1)} %get-tuple-element.530, f32[3,8,128,96]{3,2,1,0:T(8,128)S(1)} %bitcast.153, f32[3,8,24,96]{3,2,1,0:T(8,128)S(1)} %get-tuple-element.529), kind=kOutput, calls=%fused_computation.166 | convolution fusion | flops 623665152 | bytes 2891776 | tf_op jit(solution)/shard_map/fzxy,xo->fzoy/dot_general | solution.py:486
  90.0 2.2 %convolution_bitcast_fusion.2 = f32[3,8,96,128]{3,2,1,0:T(8,128)} fusion(f32[3,8,128,96]{2,3,1,0:T(8,128)S(1)} %fusion.39, f32[96,96,1,1]{0,1,3,2:T(8,128)S(1)} %copy-done.52), kind=kOutput, calls=%fused_computation.167 | convolution fusion | flops 339738624 | bytes 2396160 | tf_op jit(solution)/shard_map/fzxy,yo->fzox/dot_general | solution.py:487
  92.3 8.4 %conditional.1 = (f32[3,8,96,128]{3,0,2,1:T(4,128)S(1)}, f32[]{:T(128)}, f32[8,96,128]{2,0,1:T(8,128)S(1)}) conditional(s32[]{:T(128)} %convert_element_type.19, (s32[8,96,128]{2,1,0:T(8,128)S(1)}, f32[8,96,128]{2,1,0:T(8,128)S(1)}, s32[8,96,128]{2,1,0:T(8,128)}, f32[3,8,96,128]{3,2,1,0:T(8,128)S(1)}, (), /*index=5*/(), (), f32[176,128]{1,0:T(8,128)S(1)}, ...), branch_computations={%region_1.8_spmd, %region_8.9_spmd} | conditional | flops 2394607104 | bytes 474408416 | solution.py:642
  92.5 3.0 %copy.78 = f32[3,8,128,128]{2,0,3,1:T(4,128)} copy(f32[3,8,128,128]{3,2,1,0:T(8,128)} %get-tuple-element.435) | data formatting | bytes 3145728 | tf_op jit(solution)/shard_map
  95.5 1.8 %copy.79 = f32[3,8,128,128]{2,0,3,1:T(4,128)} copy(f32[3,8,128,128]{3,2,1,0:T(8,128)S(1)} %copy-done.43) | data formatting | bytes 3145728 | tf_op jit(solution)/shard_map
  97.4 2.4 %fusion.32 = f32[3,8,96,128]{3,0,2,1:T(4,128)S(1)} fusion(f32[3,8,128,128]{2,0,3,1:T(4,128)} %copy.79, f32[3,8,128,128]{2,0,3,1:T(4,128)} %copy.78, f32[]{:T(128)} %get-tuple-element.349, f32[]{:T(128)} %get-tuple-element.347), kind=kLoop, calls=%fused_computation.157 | loop fusion | flops 884736 | bytes 3538952 | tf_op jit(solution)/shard_map/cond/branch_1_fun/transpose | solution.py:635
  100.6 3.4 %collective-permute-start.53 = (f32[8,96,128]{2,0,1:T(8,128)S(1)}, f32[8,96,128]{2,0,1:T(8,128)S(1)}, u32[]{:S(2)}, u32[]{:S(2)}) collective-permute-start(f32[8,96,128]{2,0,1:T(8,128)S(1)} %get-tuple-element.439), channel_id=1, source_target_pairs={{0,12},{4,1},{8,5},{12,9},{1,13},{5,2},{9,6},{13,10},{2,14},{6,3},... | collective-permute-start | bytes 1179656 | tf_op jit(solution)/shard_map/ppermute | solution.py:422
  104.0 1.3 collective-permute-start.54
  105.8 1.9 %collective-permute-start.49 = (f32[96,128]{1,0:T(8,128)S(1)}, f32[96,128]{1,0:T(8,128)S(1)}, u32[]{:S(2)}, u32[]{:S(2)}) collective-permute-start(f32[96,128]{1,0:T(8,128)S(1)} %bitcast.160), channel_id=1, source_target_pairs={{0,4},{4,8},{8,12},{12,1},{1,5},{5,9},{9,13},{13,2},{2,6},{6,10},{... | collective-permute-start | bytes 147464 | tf_op jit(solution)/shard_map/ppermute | solution.py:422
  107.6 7.0 %collective-permute-start.51 = (f32[96,128]{1,0:T(8,128)S(1)}, f32[96,128]{1,0:T(8,128)S(1)}, u32[]{:S(2)}, u32[]{:S(2)}) collective-permute-start(f32[96,128]{1,0:T(8,128)S(1)} %bitcast.161), channel_id=1, source_target_pairs={{0,8},{4,12},{8,1},{12,5},{1,9},{5,13},{9,2},{13,6},{2,10},{6,14},... | collective-permute-start | bytes 147464 | tf_op jit(solution)/shard_map/ppermute | solution.py:422
  115.1 1.3 collective-permute-start.50
  116.4 1.3 collective-permute-start.52
  119.5 4.7 %collective-permute-done.50 = f32[96,128]{1,0:T(8,128)S(1)} collective-permute-done((f32[96,128]{1,0:T(8,128)S(1)}, f32[96,128]{1,0:T(8,128)S(1)}, u32[]{:S(2)}, u32[]{:S(2)}) %collective-permute-start.50) | collective-permute-done | bytes 49184 | tf_op jit(solution)/shard_map/ppermute | solution.py:422
  124.2 4.6 %collective-permute-done.52 = f32[96,128]{1,0:T(8,128)S(1)} collective-permute-done((f32[96,128]{1,0:T(8,128)S(1)}, f32[96,128]{1,0:T(8,128)S(1)}, u32[]{:S(2)}, u32[]{:S(2)}) %collective-permute-start.52) | collective-permute-done | bytes 49184 | tf_op jit(solution)/shard_map/ppermute | solution.py:422
  129.8 6.6 %concatenate.118 = f32[28,96,128]{2,0,1:T(8,128)S(1)} concatenate(f32[8,96,128]{2,0,1:T(8,128)S(1)} %get-tuple-element.439, f32[1,96,128]{2,0,1:T(1,128)S(1)} %bitcast.164, f32[1,96,128]{2,0,1:T(1,128)S(1)} %bitcast.166, f32[1,96,128]{2,0,1:T(1,128)S(1)} %bitcast.165, f32[1,96,128]{2,0,1:T(1,128)S(1)} %bitcast.167, f32[8,96,128]{2,0,1:T(8,128)} %copy-done.45, ...), dimensions={0} | concatenate | bytes 2752512 | tf_op jit(solution)/shard_map/concatenate | solution.py:513
  (97 shorter events, 18.1 us)
Async XLA Ops:
  0.6 22.6 %copy-start = (f32[50]{0:T(128)S(1)}, f32[50]{0:T(128)}, u32[]{:S(2)}) copy-start(f32[50]{0:T(128)} %constant.790.clone) | copy-start | bytes 604
  6.4 23.2 %collective-permute-start.42 = (f32[5,2,2,128]{3,2,1,0:T(2,128)S(1)}, f32[5,2,2,128]{3,2,1,0:T(2,128)S(1)}, u32[]{:S(2)}, u32[]{:S(2)}) collective-permute-start(f32[5,2,2,128]{3,2,1,0:T(2,128)S(1)} %get-tuple-element.527), channel_id=1, source_target_pairs={{4,16},{8,20},{12,24},{1,28},{5,17},{9,21},{13,25},{2,29},{6,18},{... | collective-permute-start | bytes 30728 | tf_op jit(solution)/shard_map/ppermute | solution.py:430
  7.7 22.5 %collective-permute-start.41 = (f32[5,2,2,128]{3,2,1,0:T(2,128)S(1)}, f32[5,2,2,128]{3,2,1,0:T(2,128)S(1)}, u32[]{:S(2)}, u32[]{:S(2)}) collective-permute-start(f32[5,2,2,128]{3,2,1,0:T(2,128)S(1)} %get-tuple-element.528), channel_id=1, source_target_pairs={{0,20},{4,24},{8,28},{12,17},{1,21},{5,25},{9,29},{13,18},{2,22},{... | collective-permute-start | bytes 30728 | tf_op jit(solution)/shard_map/ppermute | solution.py:430
  15.3 15.6 %collective-permute-start.40 = (f32[5,8,2,128]{3,2,1,0:T(2,128)S(1)}, f32[5,8,2,128]{3,2,1,0:T(2,128)S(1)}, u32[]{:S(2)}, u32[]{:S(2)}) collective-permute-start(f32[5,8,2,128]{3,2,1,0:T(2,128)S(1)} %slice_select_fusion.2), channel_id=1, source_target_pairs={{0,16},{4,20},{8,24},{12,28},{1,17},{5,21},{9,25},{13,29},{2,18},{... | collective-permute-start | bytes 122888 | tf_op jit(solution)/shard_map/ppermute | solution.py:430
  17.3 14.7 %collective-permute-start.39 = (f32[9,96,128]{2,1,0:T(8,128)}, f32[9,96,128]{2,1,0:T(8,128)S(1)}, u32[]{:S(2)}, u32[]{:S(2)}) collective-permute-start(f32[9,96,128]{2,1,0:T(8,128)} %get-tuple-element.366), channel_id=1, source_target_pairs={{4,0},{8,4},{12,8},{1,12},{5,1},{9,5},{13,9},{2,13},{6,2},{10,6},{... | collective-permute-start | bytes 1327112 | tf_op jit(solution)/shard_map/ppermute | solution.py:422
  18.5 13.0 %collective-permute-start.38 = (f32[5,96,128]{2,1,0:T(8,128)}, f32[5,96,128]{2,1,0:T(8,128)S(1)}, u32[]{:S(2)}, u32[]{:S(2)}) collective-permute-start(f32[5,96,128]{2,1,0:T(8,128)} %get-tuple-element.365), channel_id=1, source_target_pairs={{0,4},{4,8},{8,12},{12,1},{1,5},{5,9},{9,13},{13,2},{2,6},{6,10},{... | collective-permute-start | bytes 737288 | tf_op jit(solution)/shard_map/ppermute | solution.py:422
  29.0 3.7 %copy-start.56 = (f32[8]{0:T(128)}, f32[8]{0:T(128)S(1)}, u32[]{:S(2)}) copy-start(f32[8]{0:T(128)S(1)} %gather_fusion.4) | copy-start | bytes 100
  29.6 3.1 %copy-start.58 = (f32[8]{0:T(128)}, f32[8]{0:T(128)S(1)}, u32[]{:S(2)}) copy-start(f32[8]{0:T(128)S(1)} %gather_fusion.5) | copy-start | bytes 100
  51.6 33.8 %copy-start.42 = (f32[3,8,128,128]{3,2,1,0:T(8,128)S(1)}, f32[3,8,128,128]{3,2,1,0:T(8,128)}, u32[]{:S(2)}) copy-start(f32[3,8,128,128]{3,2,1,0:T(8,128)} %get-tuple-element.368) | copy-start | bytes 4718596
  51.6 33.8 %copy-start.50 = (f32[176,128,1,1]{1,0,3,2:T(8,128)S(1)}, f32[176,128,1,1]{1,0,3,2:T(8,128)}, u32[]{:S(2)}) copy-start(f32[176,128,1,1]{1,0,3,2:T(8,128)} %constant.815) | copy-start | bytes 270340
  51.6 3.9 %collective-permute-start.43 = (f32[8,128]{1,0:T(8,128)}, f32[8,128]{1,0:T(8,128)S(1)}, u32[]{:S(2)}, u32[]{:S(2)}) collective-permute-start(f32[8,128]{1,0:T(8,128)} %get-tuple-element.367), channel_id=1, source_target_pairs={{0,16},{16,0},{1,17},{17,1},{2,18},{18,2},{3,19},{19,3},{4,20},{20... | collective-permute-start | bytes 12296 | tf_op jit(solution)/shard_map/ppermute | solution.py:444
  56.1 3.8 %collective-permute-start.44 = (f32[8,128]{1,0:T(8,128)S(1)}, f32[8,128]{1,0:T(8,128)S(1)}, u32[]{:S(2)}, u32[]{:S(2)}) collective-permute-start(f32[8,128]{1,0:T(8,128)S(1)} %add.554), channel_id=1, source_target_pairs={{0,4},{4,0},{8,12},{12,8},{1,5},{5,1},{9,13},{13,9},{2,6},{6,2},{1... | collective-permute-start | bytes 12296 | tf_op jit(solution)/shard_map/ppermute | solution.py:444
  59.9 8.3 %collective-permute-start.45 = (f32[8,128]{1,0:T(8,128)S(1)}, f32[8,128]{1,0:T(8,128)S(1)}, u32[]{:S(2)}, u32[]{:S(2)}) collective-permute-start(f32[8,128]{1,0:T(8,128)S(1)} %add.555), channel_id=1, source_target_pairs={{0,8},{4,12},{8,0},{12,4},{1,9},{5,13},{9,1},{13,5},{2,10},{6,14},... | collective-permute-start | bytes 12296 | tf_op jit(solution)/shard_map/ppermute | solution.py:444
  68.2 1.9 %collective-permute-start.46 = (f32[8,128]{1,0:T(8,128)S(1)}, f32[8,128]{1,0:T(8,128)S(1)}, u32[]{:S(2)}, u32[]{:S(2)}) collective-permute-start(f32[8,128]{1,0:T(8,128)S(1)} %add.556), channel_id=1, source_target_pairs={{0,1},{1,0},{2,3},{3,2},{4,5},{5,4},{6,7},{7,6},{8,9},{9,8},{10,11... | collective-permute-start | bytes 12296 | tf_op jit(solution)/shard_map/ppermute | solution.py:444
  70.2 6.9 %collective-permute-start.47 = (f32[8,128]{1,0:T(8,128)S(1)}, f32[8,128]{1,0:T(8,128)S(1)}, u32[]{:S(2)}, u32[]{:S(2)}) collective-permute-start(f32[8,128]{1,0:T(8,128)S(1)} %add.557), channel_id=1, source_target_pairs={{0,2},{1,3},{2,0},{3,1},{4,6},{5,7},{6,4},{7,5},{8,10},{9,11},{10,... | collective-permute-start | bytes 12296 | tf_op jit(solution)/shard_map/ppermute | solution.py:444
  76.5 8.9 %collective-permute-start.48 = (f32[3,8,24,96]{3,2,1,0:T(8,128)S(1)}, f32[3,8,24,96]{3,2,1,0:T(8,128)S(1)}, u32[]{:S(2)}, u32[]{:S(2)}) collective-permute-start(f32[3,8,24,96]{3,2,1,0:T(8,128)S(1)} %slice_select_fusion.1), channel_id=1, source_target_pairs={{0,16},{4,20},{8,24},{12,28},{1,17},{5,21},{9,25},{13,29},{2,18},{... | collective-permute-start | bytes 663560 | tf_op jit(solution)/shard_map/ppermute | solution.py:430
  85.4 4.6 %copy-start.52 = (f32[96,96,1,1]{0,1,3,2:T(8,128)S(1)}, f32[96,96,1,1]{0,1,3,2:T(8,128)}, u32[]{:S(2)}) copy-start(f32[96,96,1,1]{0,1,3,2:T(8,128)} %constant.816) | copy-start | bytes 110596
  90.0 2.3 %copy-start.1 = (f32[3,1,8,96,128]{4,3,2,1,0:T(8,128)S(1)}, f32[3,1,8,96,128]{4,3,2,1,0:T(8,128)}, u32[]{:S(2)}) copy-start(f32[3,1,8,96,128]{4,3,2,1,0:T(8,128)} %param.70) | copy-start | bytes 3538948
  90.0 2.3 %copy-start.36 = (f32[1,8,96,128]{3,2,1,0:T(8,128)S(1)}, f32[1,8,96,128]{3,2,1,0:T(8,128)}, u32[]{:S(2)}) copy-start(f32[1,8,96,128]{3,2,1,0:T(8,128)} %param.67) | copy-start | bytes 1179652
  90.0 2.2 %copy-start.38 = (s32[1,8,96,128]{3,2,1,0:T(8,128)S(1)}, s32[1,8,96,128]{3,2,1,0:T(8,128)}, u32[]{:S(2)}) copy-start(s32[1,8,96,128]{3,2,1,0:T(8,128)} %param.68) | copy-start | bytes 1179652
  90.0 2.2 %copy-start.49 = (f32[176,128]{1,0:T(8,128)S(1)}, f32[176,128]{1,0:T(8,128)}, u32[]{:S(2)}) copy-start(f32[176,128]{1,0:T(8,128)} %constant.791.clone) | copy-start | bytes 270340
  92.2 13.1 %copy-start.55 = (f32[8,1,1]{0,1,2:T(1,128)S(1)}, f32[8,1,1]{0,1,2:T(1,128)}, u32[]{:S(2)}) copy-start(f32[8,1,1]{0,1,2:T(1,128)} %constant.817) | copy-start | bytes 100
  92.3 22.4 %copy-start.54 = (f32[8,1,1]{0,1,2:T(1,128)S(1)}, f32[8,1,1]{0,1,2:T(1,128)}, u32[]{:S(2)}) copy-start(f32[8,1,1]{0,1,2:T(1,128)} %constant.818) | copy-start | bytes 100
  92.5 3.0 %copy-start.43 = (f32[3,8,128,128]{3,2,1,0:T(8,128)S(1)}, f32[3,8,128,128]{3,2,1,0:T(8,128)}, u32[]{:S(2)}) copy-start(f32[3,8,128,128]{3,2,1,0:T(8,128)} %get-tuple-element.437) | copy-start | bytes 4718596 | tf_op jit(solution)/shard_map/cond
  97.4 2.4 %copy-start.32 = (f32[3,8,96,128]{3,2,1,0:T(8,128)S(1)}, f32[3,8,96,128]{3,2,1,0:T(8,128)}, u32[]{:S(2)}) copy-start(f32[3,8,96,128]{3,2,1,0:T(8,128)} %get-tuple-element.344) | copy-start | bytes 3538948 | tf_op jit(solution)/shard_map/cond
  100.6 28.2 %collective-permute-start.53 = (f32[8,96,128]{2,0,1:T(8,128)S(1)}, f32[8,96,128]{2,0,1:T(8,128)S(1)}, u32[]{:S(2)}, u32[]{:S(2)}) collective-permute-start(f32[8,96,128]{2,0,1:T(8,128)S(1)} %get-tuple-element.439), channel_id=1, source_target_pairs={{0,12},{4,1},{8,5},{12,9},{1,13},{5,2},{9,6},{13,10},{2,14},{6,3},... | collective-permute-start | bytes 1179656 | tf_op jit(solution)/shard_map/ppermute | solution.py:422
  104.0 24.8 %collective-permute-start.54 = (f32[8,96,128]{2,0,1:T(8,128)S(1)}, f32[8,96,128]{2,0,1:T(8,128)S(1)}, u32[]{:S(2)}, u32[]{:S(2)}) collective-permute-start(f32[8,96,128]{2,0,1:T(8,128)S(1)} %get-tuple-element.439), channel_id=1, source_target_pairs={{12,0},{1,4},{5,8},{9,12},{13,1},{2,5},{6,9},{10,13},{14,2},{3,6},... | collective-permute-start | bytes 1179656 | tf_op jit(solution)/shard_map/ppermute | solution.py:422
  105.8 10.6 %collective-permute-start.49 = (f32[96,128]{1,0:T(8,128)S(1)}, f32[96,128]{1,0:T(8,128)S(1)}, u32[]{:S(2)}, u32[]{:S(2)}) collective-permute-start(f32[96,128]{1,0:T(8,128)S(1)} %bitcast.160), channel_id=1, source_target_pairs={{0,4},{4,8},{8,12},{12,1},{1,5},{5,9},{9,13},{13,2},{2,6},{6,10},{... | collective-permute-start | bytes 147464 | tf_op jit(solution)/shard_map/ppermute | solution.py:422
  107.6 16.5 %collective-permute-start.51 = (f32[96,128]{1,0:T(8,128)S(1)}, f32[96,128]{1,0:T(8,128)S(1)}, u32[]{:S(2)}, u32[]{:S(2)}) collective-permute-start(f32[96,128]{1,0:T(8,128)S(1)} %bitcast.161), channel_id=1, source_target_pairs={{0,8},{4,12},{8,1},{12,5},{1,9},{5,13},{9,2},{13,6},{2,10},{6,14},... | collective-permute-start | bytes 147464 | tf_op jit(solution)/shard_map/ppermute | solution.py:422
  115.1 9.1 %collective-permute-start.50 = (f32[96,128]{1,0:T(8,128)S(1)}, f32[96,128]{1,0:T(8,128)S(1)}, u32[]{:S(2)}, u32[]{:S(2)}) collective-permute-start(f32[96,128]{1,0:T(8,128)S(1)} %bitcast.162), channel_id=1, source_target_pairs={{4,0},{8,4},{12,8},{1,12},{5,1},{9,5},{13,9},{2,13},{6,2},{10,6},{... | collective-permute-start | bytes 147464 | tf_op jit(solution)/shard_map/ppermute | solution.py:422
  116.4 12.4 %collective-permute-start.52 = (f32[96,128]{1,0:T(8,128)S(1)}, f32[96,128]{1,0:T(8,128)S(1)}, u32[]{:S(2)}, u32[]{:S(2)}) collective-permute-start(f32[96,128]{1,0:T(8,128)S(1)} %bitcast.163), channel_id=1, source_target_pairs={{8,0},{12,4},{1,8},{5,12},{9,1},{13,5},{2,9},{6,13},{10,2},{14,6},... | collective-permute-start | bytes 147464 | tf_op jit(solution)/shard_map/ppermute | solution.py:422
  118.9 17.5 %copy-start.53 = (f32[28,8,1]{0,1,2:T(8,128)S(1)}, f32[28,8,1]{0,1,2:T(8,128)}, u32[]{:S(2)}) copy-start(f32[28,8,1]{0,1,2:T(8,128)} %constant.819) | copy-start | bytes 2692
  (7 other events, 7.9 us)

commit v3 on v2

--- a/solution.py
+++ b/solution.py
@@ -8,6 +8,7 @@
 from jax.experimental import pallas as pl
 from jax.experimental.pallas import tpu as pltpu
 from jax.sharding import PartitionSpec as P
+
 
 RAD = 24
 ITERS = 2
@@ -151,42 +152,43 @@
 SLOT = {mode: row for row, members in enumerate(REDUCED) for mode in members}
 
 
-def prepare_kernel(density, bone, fixed, load, fields, up, down):
-    depth, height, width = density.shape
-    zeros = jnp.zeros((LANES - height, width), jnp.float32)
-
-    def layer(z, carry):
-        thick = density[z]
-        share = bone[z].astype(jnp.float32)
-        free = 1.0 - fixed[z].astype(jnp.float32)
-        modulus = share * thick * thick + (1.0 - share) * MARROW
-        values = [modulus] + [free * load[c, z] for c in range(3)] + [free, thick]
-        for slot, value in enumerate(values):
-            square = jnp.concatenate([value, zeros], axis=0)
-            fields[slot, z] = jnp.transpose(square)
-        return carry
-
-    lax.fori_loop(0, depth, layer, 0)
-
-    def one(z):
-        thick = density[z]
-        share = bone[z].astype(jnp.float32)
-        free = 1.0 - fixed[z].astype(jnp.float32)
-        modulus = share * thick * thick + (1.0 - share) * MARROW
-        return modulus, [free * load[c, z] for c in range(3)], free
-
-    up[0] = one(depth - 2)[0]
-    modulus, force, _ = one(depth - 1)
+def raw_layer(density, bone, fixed, load, z):
+    thick = density[z]
+    share = bone[z].astype(jnp.float32)
+    free = 1.0 - fixed[z].astype(jnp.float32)
+    modulus = share * thick * thick + (1.0 - share) * MARROW
+    return modulus, [free * load[c, z] for c in range(3)], free, thick
+
+
+def message_kernel(density, bone, fixed, load, up, down):
+    depth = density.shape[0]
+    raw = (density, bone, fixed, load)
+    up[0] = raw_layer(*raw, depth - 2)[0]
+    modulus, force, _, _ = raw_layer(*raw, depth - 1)
     up[1] = modulus
     for c in range(3):
         up[2 + c] = force[c]
     for z in range(2):
-        modulus, force, free = one(z)
+        modulus, force, free, _ = raw_layer(*raw, z)
         down[z] = modulus
         for c in range(3):
             down[2 + 3 * z + c] = force[c]
         if z == 0:
             down[8] = free
+
+
+def prepare_kernel(density, bone, fixed, load, fields):
+    depth, height, width = density.shape
+    zeros = jnp.zeros((LANES - height, width), jnp.float32)
+
+    def layer(z, carry):
+        modulus, force, free, thick = raw_layer(density, bone, fixed, load, z)
+        for slot, value in enumerate([modulus] + force + [free, thick]):
+            square = jnp.concatenate([value, zeros], axis=0)
+            fields[slot, z] = jnp.transpose(square)
+        return carry
+
+    lax.fori_loop(0, depth, layer, 0)
 
 
 def krylov_kernel(
@@ -376,12 +378,20 @@
         out_stats[pl.ds(s, 1)] = jnp.sum(accumulate[s], axis=0, keepdims=True)
 
 
+def run_messages(density, bone, fixed, load):
+    _, height, width = density.shape
+    return pl.pallas_call(
+        message_kernel,
+        out_shape=[jax.ShapeDtypeStruct((n, height, width), jnp.float32) for n in (5, 9)],
+        name="messages",
+    )(density, bone, fixed, load)
+
+
 def run_prepare(density, bone, fixed, load):
-    depth, height, width = density.shape
-    shapes = ((6, depth, width, LANES), (5, height, width), (9, height, width))
+    depth, _, width = density.shape
     return pl.pallas_call(
         prepare_kernel,
-        out_shape=[jax.ShapeDtypeStruct(s, jnp.float32) for s in shapes],
+        out_shape=jax.ShapeDtypeStruct((6, depth, width, LANES), jnp.float32),
         name="prepare",
     )(density, bone, fixed, load)
 
@@ -468,51 +478,154 @@
     return matrix.astype(np.float32)
 
 
-def coverage(position, length):
-    taps = tap_table()
-    ends = jnp.asarray(np.concatenate([[0.0], np.cumsum(taps)]).astype(np.float32))
-    low = jnp.maximum(-RAD, -position) + RAD
-    high = jnp.minimum(RAD, length - 1 - position) + RAD + 1
-    return ends[high] - ends[low]
-
-
-def smooth_plane(fields, height):
-    width = fields.shape[2]
-    fields = fields[..., :height]
-    from_left, from_right = edges_swapped(fields[:, :, :RAD], fields[:, :, width - RAD :], 0)
-    wide = jnp.concatenate([from_left, fields, from_right], axis=2)
-    along_x = jnp.asarray(banded(width + 2 * RAD, width, RAD))
-    along_y = jnp.asarray(banded(height, height, 0))
-    half = jnp.einsum("fzxy,xo->fzoy", wide, along_x, precision=lax.Precision.HIGHEST)
-    return jnp.einsum("fzxy,yo->fzox", half, along_y, precision=lax.Precision.HIGHEST)
-
-
-def smooth_depth(planar):
+def coverage(length):
+    ends = np.concatenate([[0.0], np.cumsum(tap_table())])
+    position = np.arange(length)
+    low = np.maximum(-RAD, -position) + RAD
+    high = np.minimum(RAD, length - 1 - position) + RAD + 1
+    return (ends[high] - ends[low]).astype(np.float32)
+
+
+def depth_pieces(planar, low_plane, high_plane):
     depth = planar.shape[0]
     taps = tap_table()
     ratio = math.exp(-1.0 / (0.5 * RAD))
     pieces, blocks = [planar], [banded(depth, depth, 0)]
-    decay = (ratio ** np.arange(depth)).astype(np.float64)
-    low_plane = jnp.tensordot(jnp.asarray(decay.astype(np.float32)), planar, 1, precision=lax.Precision.HIGHEST)
-    high_plane = jnp.tensordot(jnp.asarray(decay[::-1].astype(np.float32)), planar, 1, precision=lax.Precision.HIGHEST)
+    near, far = [], []
     steps = 1
     while (steps - 1) * depth + 1 <= RAD:
         if steps * depth + depth - 1 <= RAD:
-            pieces.append(to_slab(high_plane, steps)[None])
-            near = taps[RAD] * ratio ** (steps * depth - (depth - 1) + np.arange(depth))
-            blocks.append(near[None])
-            pieces.append(to_slab(low_plane, -steps)[None])
-            near = taps[RAD] * ratio ** (steps * depth - np.arange(depth))
-            blocks.append(near[None])
+            away = steps * depth + np.arange(depth)
+            near.append((high_plane, steps, taps[RAD] * ratio ** (away - (depth - 1))))
+            away = steps * depth - np.arange(depth)
+            near.append((low_plane, -steps, taps[RAD] * ratio ** away))
         else:
-            pieces.append(to_slab(planar, steps))
-            blocks.append(banded(depth, depth, steps * depth))
-            pieces.append(to_slab(planar, -steps))
-            blocks.append(banded(depth, depth, -steps * depth))
+            far.append((steps, banded(depth, depth, steps * depth)))
+            far.append((-steps, banded(depth, depth, -steps * depth)))
         steps += 1
-    stacked = jnp.concatenate(pieces, axis=0)
-    matrix = jnp.asarray(np.concatenate(blocks, axis=0).astype(np.float32))
-    return jnp.einsum("iyx,io->oyx", stacked, matrix, precision=lax.Precision.HIGHEST)
+    for move, block in far:
+        pieces.append(to_slab(planar, move))
+        blocks.append(block)
+    for plane, move, weight in near:
+        pieces.append(to_slab(plane, move)[None])
+        blocks.append(weight[None].astype(np.float32))
+    return pieces, blocks
+
+
+def depth_decay(depth):
+    return (math.exp(-1.0 / (0.5 * RAD)) ** np.arange(depth)).astype(np.float32)
+
+
+def krylov_coefficients(sums):
+    gamma, curve, mixed, curve_second = sums[0], 2.0 * sums[1], sums[2], 2.0 * sums[3]
+    alpha = gamma / curve
+    grown = alpha * mixed / curve
+    beta = grown - 1.0
+    bent = alpha * (alpha * (alpha * curve_second / gamma))
+    rest = bent - grown * grown
+    alpha_next = alpha * beta / rest
+    by_first = alpha + alpha_next * grown
+    by_second = -alpha_next * alpha
+    squares = [by_first * by_first, 2.0 * by_first * by_second, by_second * by_second]
+    parts = [f * s for f, s in zip(squares, sums[4:7])]
+    total = parts[0] + parts[1] + parts[2]
+    size = jnp.abs(parts[0]) + jnp.abs(parts[1]) + jnp.abs(parts[2])
+    sound = (beta > GUARD * grown) & (rest > GUARD * bent) & (total > GUARD * size)
+    return by_first, by_second, squares, total, jnp.where(sound, 1.0, 0.0)
+
+
+def smooth_kernel(plain, cells, stats, basis, left, right, along_x, along_y, planar, low, high, factors):
+    depth = basis.shape[1]
+    decay = depth_decay(depth)
+    exact = dict(precision=lax.Precision.HIGHEST, preferred_element_type=jnp.float32)
+    tile = stats[...]
+    sums = [jnp.sum(tile[i : i + 1], axis=1, keepdims=True) for i in range(8)]
+    if plain:
+        one = jnp.ones((1, 1), jnp.float32)
+        by_first, by_second, squares, total, sound = one, one, [one], sums[4], one
+    else:
+        by_first, by_second, squares, total, sound = krylov_coefficients(sums)
+    scale = 1.0 / (total / cells + EPSILON)
+    for i, value in enumerate((by_first, by_second, scale, sound)):
+        factors[pl.ds(i, 1)] = jnp.broadcast_to(value, (1, LANES))
+    factors[pl.ds(4, 4)] = jnp.zeros((4, LANES), jnp.float32)
+    for z in range(depth):
+        wide = jnp.concatenate(
+            [sum(f * v[i, z] for i, f in enumerate(squares)) for v in (left, basis, right)], axis=0
+        )
+        half = lax.dot_general(along_x[...], wide, (((1,), (0,)), ((), ())), **exact)
+        plane = lax.dot_general(along_y[...], half, (((1,), (1,)), ((), ())), **exact)
+        planar[z] = plane
+        for ref, weight in ((low, decay[z]), (high, decay[depth - 1 - z])):
+            share = plane * float(weight)
+            ref[...] = share if z == 0 else ref[...] + share
+
+
+def run_smooth(plain, cells, stats, basis, sides, height):
+    depth, width = basis.shape[1:3]
+    along_x = banded(width + 2 * RAD, width, RAD).T
+    along_y = np.zeros((height, LANES), np.float32)
+    along_y[:, :height] = banded(height, height, 0).T
+    shapes = ((depth, height, width), (height, width), (height, width), (8, LANES))
+    return pl.pallas_call(
+        functools.partial(smooth_kernel, plain, float(cells)),
+        out_shape=[jax.ShapeDtypeStruct(s, jnp.float32) for s in shapes],
+        name="smooth",
+    )(stats, basis, *sides, jnp.asarray(along_x), jnp.asarray(along_y))
+
+
+def finish_kernel(blocks, factors, density, bone, *rest):
+    pieces, out = rest[:-1], rest[-1]
+    depth, height, _ = density.shape
+
+    scale = factors[pl.ds(2, 1)]
+
+    def chunk(index, carry):
+        rows = pl.ds(pl.multiple_of(index * 8, 8), 8)
+        totals = [None] * depth
+        for piece, block in zip(pieces, blocks):
+            for i in range(block.shape[0]):
+                value = piece[i, rows]
+                for o in range(depth):
+                    if block[i, o] != 0.0:
+                        term = value * float(block[i, o])
+                        totals[o] = term if totals[o] is None else totals[o] + term
+        for o in range(depth):
+            share = REMODEL * bone[o, rows].astype(jnp.float32)
+            moved = density[o, rows] + share * (totals[o] * scale - 1.0)
+            out[o, rows] = jnp.clip(moved, FLOOR, CEILING)
+        return carry
+
+    lax.fori_loop(0, height // 8, chunk, 0)
+
+
+def run_finish(factors, density, bone, pieces, blocks):
+    return pl.pallas_call(
+        functools.partial(finish_kernel, blocks),
+        out_shape=jax.ShapeDtypeStruct(density.shape, jnp.float32),
+        name="finish",
+    )(factors, density, bone, *pieces)
+
+
+def displacement_kernel(height, factors, first, second, out):
+    by_first, by_second = factors[pl.ds(0, 1)], factors[pl.ds(1, 1)]
+
+    def layer(z, carry):
+        for i in range(3):
+            moved = by_first * first[i, z] + by_second * second[i, z]
+            out[i, z] = jnp.transpose(moved)[:height]
+        return carry
+
+    lax.fori_loop(0, first.shape[1], layer, 0)
+
+
+def run_displacement(factors, first, second, height):
+    depth, width = first.shape[1:3]
+    return pl.pallas_call(
+        functools.partial(displacement_kernel, height),
+        out_shape=jax.ShapeDtypeStruct((3, depth, height, width), jnp.float32),
+        name="displacement",
+    )(factors, first, second)
 
 
 def corners():
@@ -551,43 +664,56 @@
     )
 
 
+def spread_corner(values, corner):
+    return jnp.pad(values, ((0, 0),) + tuple((c, 1 - c) for c in corner))
+
+
 def plain_forces(field, modulus, table):
-    depth, height, width = modulus.shape
+    _, height, _ = modulus.shape
     columns = corner_columns(upper_nodes(field), modulus.shape)
     products = element_products(columns, table) * modulus
-    total = jnp.zeros((3, depth + 1, height + 1, width + 1), jnp.float32)
-    for node, (cz, cy, cx) in enumerate(corners()):
-        total = total.at[:, cz : cz + depth, cy : cy + height, cx : cx + width].add(products[node::8])
+    products = products.reshape((3, 8) + modulus.shape)
+    total = sum(spread_corner(products[:, node], corner) for node, corner in enumerate(corners()))
     return fold_upper(total[:, :, :height])
 
 
 def plain_path(table, density, bone, fixed, load):
-    depth, height, width = density.shape
+    _, height, _ = density.shape
     share = bone.astype(jnp.float32)
     free = 1.0 - fixed.astype(jnp.float32)
     modulus = share * density * density + (1.0 - share) * MARROW
-    spread = jnp.zeros((1, depth + 1, height + 1, width + 1), jnp.float32)
-    for cz, cy, cx in corners():
-        spread = spread.at[0, cz : cz + depth, cy : cy + height, cx : cx + width].add(modulus)
+    spread = sum(spread_corner(modulus[None], corner) for corner in corners())
     precondition = free / (float(table[0, 0]) * fold_upper(spread[:, :, :height]))
     residual = free * load
-    solution = jnp.zeros_like(residual)
     search = precondition * residual
-    gamma = inner_sum(residual * search)
-    for count in range(ITERS):
+    start = (jnp.zeros_like(residual), residual, search, inner_sum(residual * search))
+
+    def iterate(_, state):
+        moved, residual, search, gamma = state
         image = free * plain_forces(free * search, modulus, table)
         alpha = gamma / inner_sum(search * image)
-        solution = solution + alpha * search
-        if count + 1 < ITERS:
-            residual = residual - alpha * image
-            scaled = precondition * residual
-            gamma_next = inner_sum(residual * scaled)
-            search = scaled + gamma_next / gamma * search
-            gamma = gamma_next
-    columns = corner_columns(upper_nodes(solution), modulus.shape)
+        moved = moved + alpha * search
+        residual = residual - alpha * image
+        scaled = precondition * residual
+        gamma_next = inner_sum(residual * scaled)
+        return moved, residual, scaled + gamma_next / gamma * search, gamma_next
+
+    moved = lax.fori_loop(0, ITERS, iterate, start)[0]
+    columns = corner_columns(upper_nodes(moved), modulus.shape)
     energy = 0.5 * modulus * jnp.sum(columns * element_products(columns, table), axis=0)
     specific = jnp.swapaxes(energy / density, 1, 2)
-    return smooth_plane(specific[None], height)[0], solution, specific
+    return jnp.pad(specific, ((0, 0), (0, 0), (0, LANES - height))), moved
+
+
+def side_halos(basis):
+    width = basis.shape[2]
+    return edges_swapped(basis[:, :, :RAD], basis[:, :, width - RAD :], 0)
+
+
+def remodelled(plain, cells, density, bone, stats, basis, sides):
+    planar, low, high, factors = run_smooth(plain, cells, stats, basis, sides, density.shape[1])
+    pieces, blocks = depth_pieces(planar, low, high)
+    return run_finish(factors, density, bone, pieces, blocks), factors
 
 
 def on_device(density, bone, fixed, load):
@@ -597,55 +723,40 @@
     slabs = lax.axis_size("gy") * lax.axis_size("gz")
     slab = lax.axis_index("gz") * lax.axis_size("gy") + lax.axis_index("gy")
     across = lax.axis_size("gx") * width
-    cover_x = coverage(lax.axis_index("gx") * width + jnp.arange(width), across)
-    cover_y = coverage(jnp.arange(height), height)
-    cover_z = coverage(slab * depth + jnp.arange(depth), slabs * depth)
-    weights = jnp.pad(cover_x[:, None] * cover_y[None], ((0, 0), (0, LANES - height)))
+    cells = density.size * lax.axis_size("gx") * slabs
+    cover_x = lax.dynamic_slice(jnp.asarray(coverage(across)), (lax.axis_index("gx") * width,), (width,))
+    cover_y = jnp.asarray(np.pad(coverage(height), (0, LANES - height)))
+    cover_z = lax.dynamic_slice(jnp.asarray(coverage(slabs * depth)), (slab * depth,), (depth,))
+    weights = cover_x[:, None] * cover_y[None]
     planes = jnp.broadcast_to(cover_z[:, None, None], (depth, 8, LANES))
 
-    fields, up, down = run_prepare(density, bone, fixed, load)
-    got_up, got_down = to_slab(up, 1), to_slab(down, -1)
+    up, down = run_messages(density, bone, fixed, load)
+    got_up = to_slab(up, 1)
+    got_down = to_slab(down, -1)
+    fields = run_prepare(density, bone, fixed, load)
     low, high = fields[:5, :, :2], fields[:5, :, width - 2 :]
     left, right = edges_swapped(low, high, 0)
     left_up, right_up = edges_swapped(low[:, depth - 2 :], high[:, depth - 2 :], 1)
     left_down, right_down = edges_swapped(low[:, :2], high[:, :2], -1)
     halos = (got_up, got_down, left, right, left_up, right_up, left_down, right_down)
     first, second, basis, stats = run_krylov(table, fields, halos, weights, planes)
-
-    sums = jnp.sum(total_over_mesh(stats), axis=1)
-    gamma, curve, mixed, curve_second = sums[0], 2.0 * sums[1], sums[2], 2.0 * sums[3]
-    smoothed = smooth_plane(basis, height)
-    alpha = gamma / curve
-    grown = alpha * mixed / curve
-    beta = grown - 1.0
-    bent = alpha * (alpha * (alpha * curve_second / gamma))
-    rest = bent - grown * grown
-    alpha_next = alpha * beta / rest
-    by_first = alpha + alpha_next * grown
-    by_second = -alpha_next * alpha
-    squares = (by_first * by_first, 2.0 * by_first * by_second, by_second * by_second)
-    parts = [f * s for f, s in zip(squares, (sums[4], sums[5], sums[6]))]
-    total = parts[0] + parts[1] + parts[2]
-    size = jnp.abs(parts[0]) + jnp.abs(parts[1]) + jnp.abs(parts[2])
-    sound = (beta > GUARD * grown) & (rest > GUARD * bent) & (total > GUARD * size)
-
-    def combined():
-        planar = sum(f * s for f, s in zip(squares, smoothed))
-        moved = by_first * first[..., :height] + by_second * second[..., :height]
-        return planar, jnp.swapaxes(moved, 2, 3), total
-
-    def repeated():
-        planar, moved, specific = plain_path(table, density, bone, fixed, load)
-        cover = weights[None, :, :height] * cover_z[:, None, None]
-        return planar, moved, inner_sum(specific * cover)
-
-    planar, solution, total = lax.cond(sound, combined, repeated)
-    stimulus = smooth_depth(planar)
-    mean = total / (density.size * lax.axis_size("gx") * slabs)
-    share = bone.astype(jnp.float32)
-    updated = density + REMODEL * share * (stimulus / (mean + EPSILON) - 1.0)
-    updated = jnp.clip(updated, FLOOR, CEILING)
-    return updated[None], solution[:, None]
+    sides = side_halos(basis)
+    stats = total_over_mesh(stats)
+    updated, factors = remodelled(False, cells, density, bone, stats, basis, sides)
+    moved = run_displacement(factors, first, second, height)
+
+    def repeated(state):
+        specific, moved = plain_path(table, density, bone, fixed, load)
+        total = inner_sum(specific * weights[None] * cover_z[:, None, None])
+        row, lane = (lax.broadcasted_iota(jnp.int32, (8, LANES), i) for i in range(2))
+        tile = jnp.where((row == 4) & (lane == 0), total, 0.0)
+        again = specific[None]
+        updated = remodelled(True, cells, density, bone, tile, again, side_halos(again))[0]
+        return True, updated, moved.reshape(-1, width)
+
+    sound = factors[3, 0] > 0.5
+    _, updated, moved = lax.while_loop(lambda state: ~state[0], repeated, (sound, updated, moved.reshape(-1, width)))
+    return updated[None], moved.reshape(3, 1, depth, height, width)
 
 
 def solution(mesh):

time: 139 us -> 129 us (0.928)
  the two profiles are of different devices: /device:TPU:0 before, /device:TPU:5 now
where the time goes in v3:
time: 129 us
  starting transfers between devices  49.8 us (39%)
  Pallas kernels  37.3 us (29%)
  waiting for transfers between devices  27.5 us (21%)
  other arithmetic  7.71 us (6%)
  local copies, waits for them, and re-layouts  5.08 us (4%)
  between operations  1.55 us (1%)
    ppermute x8, starting transfers between devices, to_slab(): return lax.ppermute(value, ('gx', 'gy', 'gz'), slab_route(steps, sideways))  33 us
    pallas_call x1, Pallas kernels, run_krylov(): pl.pallas_call(functools.partial(krylov_kernel, mode_constants(table), fl...  18.9 us
    ppermute x8, waiting for transfers between devices, to_slab(): return lax.ppermute(value, ('gx', 'gy', 'gz'), slab_route(steps, sideways))  14 us
    ppermute x5, waiting for transfers between devices, total_over_mesh(): other = lax.ppermute(value, axis, [(i, i ^ step) for i in range(count)])  13.5 us
    ppermute x4, starting transfers between devices, edges_swapped(): got = lax.ppermute(sent, ('gx', 'gy', 'gz'), spots)  9.28 us
    ppermute x5, starting transfers between devices, total_over_mesh(): other = lax.ppermute(value, axis, [(i, i ^ step) for i in range(count)])  7.52 us
    pallas_call x1, Pallas kernels, run_prepare(): pl.pallas_call(prepare_kernel, out_shape=jax.ShapeDtypeStruct((6, depth,...  4.8 us
    pallas_call x1, Pallas kernels, run_smooth(): pl.pallas_call(functools.partial(smooth_kernel, plain, float(cells)), out...  4.65 us
  transfers between devices with their start and end apart: 17, of which 7 were waited for; matrix products, arithmetic and copies ran while one was open for 6% of the time, Pallas kernels for 5%

profile of v3, /device:TPU:5, one launch (start us, length us, event | category | flops | bytes accessed | tf_op | source)
XLA Modules:
  0.0 128.9 jit_solution(9188271176848921607)
XLA Ops:
  0.7 4.8 %prepare.1.fields = f32[6,8,128,128]{3,2,1,0:T(8,128)} custom-call(f32[8,96,128]{2,1,0:T(8,128)} %bitcast.108, s32[8,96,128]{2,1,0:T(8,128)} %bitcast.115, s32[8,96,128]{2,1,0:T(8,128)} %bitcast.122, f32[3,8,96,128]{3,2,1,0:T(8,128)} %bitcast.126), custom_call_target="tpu_custom_call" | custom-call | tf_op jit(solution)/shard_map/prepare/pallas_call | solution.py:392
  5.5 0.9 slice_select_fusion.3
  6.4 6.7 %collective-permute-start.39 = (f32[5,2,2,128]{3,2,1,0:T(2,128)S(1)}, f32[5,2,2,128]{3,2,1,0:T(2,128)S(1)}, u32[]{:S(2)}, u32[]{:S(2)}) collective-permute-start(f32[5,2,2,128]{3,2,1,0:T(2,128)S(1)} %get-tuple-element.559), channel_id=1, source_target_pairs={{4,16},{8,20},{12,24},{1,28},{5,17},{9,21},{13,25},{2,29},{6,18},{... | collective-permute-start | bytes 30728 | tf_op jit(solution)/shard_map/ppermute | solution.py:440
  13.1 1.9 %collective-permute-start.38 = (f32[5,2,2,128]{3,2,1,0:T(2,128)S(1)}, f32[5,2,2,128]{3,2,1,0:T(2,128)S(1)}, u32[]{:S(2)}, u32[]{:S(2)}) collective-permute-start(f32[5,2,2,128]{3,2,1,0:T(2,128)S(1)} %get-tuple-element.560), channel_id=1, source_target_pairs={{0,20},{4,24},{8,28},{12,17},{1,21},{5,25},{9,29},{13,18},{2,22},{... | collective-permute-start | bytes 30728 | tf_op jit(solution)/shard_map/ppermute | solution.py:440
  15.0 1.0 slice_select_fusion.2
  16.4 2.2 %messages.1 = (f32[5,96,128]{2,1,0:T(8,128)}, f32[9,96,128]{2,1,0:T(8,128)}) custom-call(f32[8,96,128]{2,1,0:T(8,128)S(1)} %bitcast.109, s32[8,96,128]{2,1,0:T(8,128)S(1)} %bitcast.116, s32[8,96,128]{2,1,0:T(8,128)S(1)} %bitcast.123, f32[3,8,96,128]{3,2,1,0:T(8,128)} %bitcast.127), custom_call_target="tpu_custom_call" | custom-call | tf_op jit(solution)/shard_map/messages/pallas_call | solution.py:383
  18.6 6.6 %collective-permute-start.36 = (f32[9,96,128]{2,1,0:T(8,128)}, f32[9,96,128]{2,1,0:T(8,128)S(1)}, u32[]{:S(2)}, u32[]{:S(2)}) collective-permute-start(f32[9,96,128]{2,1,0:T(8,128)} %get-tuple-element.218), channel_id=1, source_target_pairs={{4,0},{8,4},{12,8},{1,12},{5,1},{9,5},{13,9},{2,13},{6,2},{10,6},{... | collective-permute-start | bytes 1327112 | tf_op jit(solution)/shard_map/ppermute | solution.py:432
  26.1 1.9 %collective-permute-start.35 = (f32[5,96,128]{2,1,0:T(8,128)}, f32[5,96,128]{2,1,0:T(8,128)S(1)}, u32[]{:S(2)}, u32[]{:S(2)}) collective-permute-start(f32[5,96,128]{2,1,0:T(8,128)} %get-tuple-element.217), channel_id=1, source_target_pairs={{0,4},{4,8},{8,12},{12,1},{1,5},{5,9},{9,13},{13,2},{2,6},{6,10},{... | collective-permute-start | bytes 737288 | tf_op jit(solution)/shard_map/ppermute | solution.py:432
  29.9 10.3 %collective-permute-done.35.up = f32[5,96,128]{2,1,0:T(8,128)S(1)} collective-permute-done((f32[5,96,128]{2,1,0:T(8,128)}, f32[5,96,128]{2,1,0:T(8,128)S(1)}, u32[]{:S(2)}, u32[]{:S(2)}) %collective-permute-start.35) | collective-permute-done | bytes 245792 | tf_op jit(solution)/shard_map/ppermute | solution.py:432
  41.1 18.9 %krylov.1 = (f32[3,8,128,128]{3,2,1,0:T(8,128)}, f32[3,8,128,128]{3,2,1,0:T(8,128)}, f32[3,8,128,128]{3,2,1,0:T(8,128)}, f32[8,128]{1,0:T(8,128)}) custom-call(f32[6,8,128,128]{3,2,1,0:T(8,128)} %prepare.1.fields, f32[5,96,128]{2,1,0:T(8,128)} %copy-done.39, f32[9,96,128]{2,1,0:T(8,128)} %copy-done.36, f32[5,8,2,128]{3,2,1,0:T(2,128)} %get-tuple-element.564.left, ...), custom_call_target="tpu_custom_call" | custom-call | tf_op jit(solution)/shard_map/krylov/pallas_call | solution.py:410
  60.0 1.1 slice_select_fusion.1
  61.4 1.2 collective-permute-start.40
  62.6 5.9 %collective-permute-done.40 = f32[8,128]{1,0:T(8,128)S(1)} collective-permute-done((f32[8,128]{1,0:T(8,128)}, f32[8,128]{1,0:T(8,128)S(1)}, u32[]{:S(2)}, u32[]{:S(2)}) %collective-permute-start.40) | collective-permute-done | bytes 4128 | tf_op jit(solution)/shard_map/ppermute | solution.py:454
  69.1 2.5 %collective-permute-start.41 = (f32[8,128]{1,0:T(8,128)S(1)}, f32[8,128]{1,0:T(8,128)S(1)}, u32[]{:S(2)}, u32[]{:S(2)}) collective-permute-start(f32[8,128]{1,0:T(8,128)S(1)} %add.292), channel_id=1, source_target_pairs={{0,4},{4,0},{8,12},{12,8},{1,5},{5,1},{9,13},{13,9},{2,6},{6,2},{1... | collective-permute-start | bytes 12296 | tf_op jit(solution)/shard_map/ppermute | solution.py:454
  71.6 1.0 collective-permute-done.41
  72.6 3.4 %collective-permute-done.42 = f32[8,128]{1,0:T(8,128)S(1)} collective-permute-done((f32[8,128]{1,0:T(8,128)S(1)}, f32[8,128]{1,0:T(8,128)S(1)}, u32[]{:S(2)}, u32[]{:S(2)}) %collective-permute-start.42) | collective-permute-done | bytes 4128 | tf_op jit(solution)/shard_map/ppermute | solution.py:454
  75.9 3.9 %collective-permute-start.43 = (f32[8,128]{1,0:T(8,128)S(1)}, f32[8,128]{1,0:T(8,128)S(1)}, u32[]{:S(2)}, u32[]{:S(2)}) collective-permute-start(f32[8,128]{1,0:T(8,128)S(1)} %add.294), channel_id=1, source_target_pairs={{0,1},{1,0},{2,3},{3,2},{4,5},{5,4},{6,7},{7,6},{8,9},{9,8},{10,11... | collective-permute-start | bytes 12296 | tf_op jit(solution)/shard_map/ppermute | solution.py:454
  79.8 0.8 collective-permute-done.43
  80.6 2.5 %collective-permute-done.44 = f32[8,128]{1,0:T(8,128)S(1)} collective-permute-done((f32[8,128]{1,0:T(8,128)S(1)}, f32[8,128]{1,0:T(8,128)S(1)}, u32[]{:S(2)}, u32[]{:S(2)}) %collective-permute-start.44) | collective-permute-done | bytes 4128 | tf_op jit(solution)/shard_map/ppermute | solution.py:454
  83.7 0.9 broadcast_select_fusion.2
  84.5 4.6 %smooth.2 = (f32[8,96,128]{2,1,0:T(8,128)}, f32[96,128]{1,0:T(8,128)}, f32[96,128]{1,0:T(8,128)}, f32[8,128]{1,0:T(8,128)}) custom-call(f32[8,128]{1,0:T(8,128)} %add.296.stats, f32[3,8,128,128]{3,2,1,0:T(8,128)} %get-tuple-element.220.basis, f32[3,8,24,128]{3,2,1,0:T(8,128)} %get-tuple-element.562.left, f32[3,8,24,128]{3,2,1,0:T(8,128)} %get-tuple-element.561.right, ...), custom_call_target="tpu_custom_call" | custom-call | tf_op jit(solution)/shard_map/smooth/pallas_call | solution.py:570
  89.2 3.1 %collective-permute-start.46 = (f32[8,96,128]{2,1,0:T(8,128)}, f32[8,96,128]{2,1,0:T(8,128)S(1)}, u32[]{:S(2)}, u32[]{:S(2)}) collective-permute-start(f32[8,96,128]{2,1,0:T(8,128)} %get-tuple-element.222.rest_0_), channel_id=1, source_target_pairs={{0,12},{4,1},{8,5},{12,9},{1,13},{5,2},{9,6},{13,10},{2,14},{6,3},... | collective-permute-start | bytes 1179656 | tf_op jit(solution)/shard_map/ppermute | solution.py:432
  92.3 3.9 %collective-permute-start.47 = (f32[8,96,128]{2,1,0:T(8,128)}, f32[8,96,128]{2,1,0:T(8,128)S(1)}, u32[]{:S(2)}, u32[]{:S(2)}) collective-permute-start(f32[8,96,128]{2,1,0:T(8,128)} %get-tuple-element.222.rest_0_), channel_id=1, source_target_pairs={{12,0},{1,4},{5,8},{9,12},{13,1},{2,5},{6,9},{10,13},{14,2},{3,6},... | collective-permute-start | bytes 1179656 | tf_op jit(solution)/shard_map/ppermute | solution.py:432
  96.1 2.3 %collective-permute-start.48 = (f32[96,128]{1,0:T(8,128)}, f32[96,128]{1,0:T(8,128)S(1)}, u32[]{:S(2)}, u32[]{:S(2)}) collective-permute-start(f32[96,128]{1,0:T(8,128)} %get-tuple-element.223), channel_id=1, source_target_pairs={{0,4},{4,8},{8,12},{12,1},{1,5},{5,9},{9,13},{13,2},{2,6},{6,10},{... | collective-permute-start | bytes 147464 | tf_op jit(solution)/shard_map/ppermute | solution.py:432
  98.4 3.1 %collective-permute-start.50 = (f32[96,128]{1,0:T(8,128)}, f32[96,128]{1,0:T(8,128)S(1)}, u32[]{:S(2)}, u32[]{:S(2)}) collective-permute-start(f32[96,128]{1,0:T(8,128)} %get-tuple-element.223), channel_id=1, source_target_pairs={{0,8},{4,12},{8,1},{12,5},{1,9},{5,13},{9,2},{13,6},{2,10},{6,14},... | collective-permute-start | bytes 147464 | tf_op jit(solution)/shard_map/ppermute | solution.py:432
  101.6 3.8 %collective-permute-start.49 = (f32[96,128]{1,0:T(8,128)}, f32[96,128]{1,0:T(8,128)S(1)}, u32[]{:S(2)}, u32[]{:S(2)}) collective-permute-start(f32[96,128]{1,0:T(8,128)} %get-tuple-element.224), channel_id=1, source_target_pairs={{4,0},{8,4},{12,8},{1,12},{5,1},{9,5},{13,9},{2,13},{6,2},{10,6},{... | collective-permute-start | bytes 147464 | tf_op jit(solution)/shard_map/ppermute | solution.py:432
  105.4 3.6 %collective-permute-done.48 = f32[96,128]{1,0:T(8,128)S(1)} collective-permute-done((f32[96,128]{1,0:T(8,128)}, f32[96,128]{1,0:T(8,128)S(1)}, u32[]{:S(2)}, u32[]{:S(2)}) %collective-permute-start.48) | collective-permute-done | bytes 49184 | tf_op jit(solution)/shard_map/ppermute | solution.py:432
  109.1 8.2 %collective-permute-start.51 = (f32[96,128]{1,0:T(8,128)}, f32[96,128]{1,0:T(8,128)S(1)}, u32[]{:S(2)}, u32[]{:S(2)}) collective-permute-start(f32[96,128]{1,0:T(8,128)} %get-tuple-element.224), channel_id=1, source_target_pairs={{8,0},{12,4},{1,8},{5,12},{9,1},{13,5},{2,9},{6,13},{10,2},{14,6},... | collective-permute-start | bytes 147464 | tf_op jit(solution)/shard_map/ppermute | solution.py:432
  117.3 2.0 %copy.91 = f32[3,8,96,128]{3,0,2,1:T(4,128)} copy(f32[3,8,96,128]{3,2,1,0:T(8,128)S(1)} %bitcast.128) | data formatting | bytes 2359296
  119.3 1.2 slice.492
  120.5 3.9 %displacement.1 = f32[3,8,96,128]{3,2,1,0:T(8,128)} custom-call(f32[8,128]{1,0:T(8,128)} %get-tuple-element.221.factors, f32[3,8,128,128]{3,2,1,0:T(8,128)} %get-tuple-element.225.first, f32[3,8,128,128]{3,2,1,0:T(8,128)} %get-tuple-element.226.second), custom_call_target="tpu_custom_call" | custom-call | tf_op jit(solution)/shard_map/displacement/pallas_call | solution.py:624
  126.0 2.8 %finish.2 = f32[8,96,128]{2,1,0:T(8,128)} custom-call(f32[8,128]{1,0:T(8,128)} %get-tuple-element.221.factors, f32[8,96,128]{2,1,0:T(8,128)S(1)} %bitcast.110, s32[8,96,128]{2,1,0:T(8,128)S(1)} %bitcast.117, f32[8,96,128]{2,1,0:T(8,128)} %get-tuple-element.222.rest_0_, f32[8,96,128]{2,1,0:T(8,128)} %copy-done.37, f32[8,96,128]{2,1,0:T(8,128)} %copy-done.38, ...), custom_call_target="tpu_custom_call" | custom-call | tf_op jit(solution)/shard_map/finish/pallas_call | solution.py:603
  (61 shorter events, 6.4 us)
Async XLA Ops:
  0.6 15.7 %copy-start.12 = (f32[1,8,96,128]{3,2,1,0:T(8,128)S(1)}, f32[1,8,96,128]{3,2,1,0:T(8,128)}, u32[]{:S(2)}) copy-start(f32[1,8,96,128]{3,2,1,0:T(8,128)} %param.17) | copy-start | bytes 1179652
  0.6 15.7 %copy-start.22 = (s32[1,8,96,128]{3,2,1,0:T(8,128)S(1)}, s32[1,8,96,128]{3,2,1,0:T(8,128)}, u32[]{:S(2)}) copy-start(s32[1,8,96,128]{3,2,1,0:T(8,128)} %param.18) | copy-start | bytes 1179652
  0.7 15.7 %copy-start.24 = (s32[1,8,96,128]{3,2,1,0:T(8,128)S(1)}, s32[1,8,96,128]{3,2,1,0:T(8,128)}, u32[]{:S(2)}) copy-start(s32[1,8,96,128]{3,2,1,0:T(8,128)} %param.19) | copy-start | bytes 1179652
  5.5 19.7 %copy-start.50 = (f32[256]{0:T(256)S(1)}, f32[256]{0:T(256)}, u32[]{:S(2)}) copy-start(f32[256]{0:T(256)} %constant.91.clone) | copy-start | bytes 3076
  5.5 19.8 %copy-start.46 = (f32[128]{0:T(128)S(1)}, f32[128]{0:T(128)}, u32[]{:S(2)}) copy-start(f32[128]{0:T(128)} %constant.92.clone) | copy-start | bytes 1540
  5.5 20.5 %copy-start.51 = (f32[128]{0:T(128)S(1)}, f32[128]{0:T(128)}, u32[]{:S(2)}) copy-start(f32[128]{0:T(128)} %constant.93.clone) | copy-start | bytes 1540
  6.4 21.6 %collective-permute-start.39 = (f32[5,2,2,128]{3,2,1,0:T(2,128)S(1)}, f32[5,2,2,128]{3,2,1,0:T(2,128)S(1)}, u32[]{:S(2)}, u32[]{:S(2)}) collective-permute-start(f32[5,2,2,128]{3,2,1,0:T(2,128)S(1)} %get-tuple-element.559), channel_id=1, source_target_pairs={{4,16},{8,20},{12,24},{1,28},{5,17},{9,21},{13,25},{2,29},{6,18},{... | collective-permute-start | bytes 30728 | tf_op jit(solution)/shard_map/ppermute | solution.py:440
  13.1 15.5 %collective-permute-start.38 = (f32[5,2,2,128]{3,2,1,0:T(2,128)S(1)}, f32[5,2,2,128]{3,2,1,0:T(2,128)S(1)}, u32[]{:S(2)}, u32[]{:S(2)}) collective-permute-start(f32[5,2,2,128]{3,2,1,0:T(2,128)S(1)} %get-tuple-element.560), channel_id=1, source_target_pairs={{0,20},{4,24},{8,28},{12,17},{1,21},{5,25},{9,29},{13,18},{2,22},{... | collective-permute-start | bytes 30728 | tf_op jit(solution)/shard_map/ppermute | solution.py:440
  16.1 13.2 %collective-permute-start.37 = (f32[5,8,2,128]{3,2,1,0:T(2,128)S(1)}, f32[5,8,2,128]{3,2,1,0:T(2,128)S(1)}, u32[]{:S(2)}, u32[]{:S(2)}) collective-permute-start(f32[5,8,2,128]{3,2,1,0:T(2,128)S(1)} %slice_select_fusion.2), channel_id=1, source_target_pairs={{0,16},{4,20},{8,24},{12,28},{1,17},{5,21},{9,25},{13,29},{2,18},{... | collective-permute-start | bytes 122888 | tf_op jit(solution)/shard_map/ppermute | solution.py:440
  18.6 21.7 %collective-permute-start.36 = (f32[9,96,128]{2,1,0:T(8,128)}, f32[9,96,128]{2,1,0:T(8,128)S(1)}, u32[]{:S(2)}, u32[]{:S(2)}) collective-permute-start(f32[9,96,128]{2,1,0:T(8,128)} %get-tuple-element.218), channel_id=1, source_target_pairs={{4,0},{8,4},{12,8},{1,12},{5,1},{9,5},{13,9},{2,13},{6,2},{10,6},{... | collective-permute-start | bytes 1327112 | tf_op jit(solution)/shard_map/ppermute | solution.py:432
  25.3 34.7 %copy-start.48 = (f32[128]{0:T(128)}, f32[128]{0:T(128)S(1)}, u32[]{:S(2)}) copy-start(f32[128]{0:T(128)S(1)} %dynamic_slice.6) | copy-start | bytes 1540
  26.1 33.9 %copy-start.44 = (f32[8]{0:T(128)}, f32[8]{0:T(128)S(1)}, u32[]{:S(2)}) copy-start(f32[8]{0:T(128)S(1)} %dynamic_slice.7) | copy-start | bytes 100
  26.1 14.1 %collective-permute-start.35 = (f32[5,96,128]{2,1,0:T(8,128)}, f32[5,96,128]{2,1,0:T(8,128)S(1)}, u32[]{:S(2)}, u32[]{:S(2)}) collective-permute-start(f32[5,96,128]{2,1,0:T(8,128)} %get-tuple-element.217), channel_id=1, source_target_pairs={{0,4},{4,8},{8,12},{12,1},{1,5},{5,9},{9,13},{13,2},{2,6},{6,10},{... | collective-permute-start | bytes 737288 | tf_op jit(solution)/shard_map/ppermute | solution.py:432
  40.2 0.8 copy-start.39
  40.2 0.8 copy-start.36
  61.1 22.6 %collective-permute-start.45 = (f32[3,8,24,128]{3,2,1,0:T(8,128)S(1)}, f32[3,8,24,128]{3,2,1,0:T(8,128)S(1)}, u32[]{:S(2)}, u32[]{:S(2)}) collective-permute-start(f32[3,8,24,128]{3,2,1,0:T(8,128)S(1)} %slice_select_fusion.1), channel_id=1, source_target_pairs={{0,16},{4,20},{8,24},{12,28},{1,17},{5,21},{9,25},{13,29},{2,18},{... | collective-permute-start | bytes 884744 | tf_op jit(solution)/shard_map/ppermute | solution.py:440
  61.4 7.1 %collective-permute-start.40 = (f32[8,128]{1,0:T(8,128)}, f32[8,128]{1,0:T(8,128)S(1)}, u32[]{:S(2)}, u32[]{:S(2)}) collective-permute-start(f32[8,128]{1,0:T(8,128)} %get-tuple-element.219), channel_id=1, source_target_pairs={{0,16},{16,0},{1,17},{17,1},{2,18},{18,2},{3,19},{19,3},{4,20},{20... | collective-permute-start | bytes 12296 | tf_op jit(solution)/shard_map/ppermute | solution.py:454
  69.1 3.4 %collective-permute-start.41 = (f32[8,128]{1,0:T(8,128)S(1)}, f32[8,128]{1,0:T(8,128)S(1)}, u32[]{:S(2)}, u32[]{:S(2)}) collective-permute-start(f32[8,128]{1,0:T(8,128)S(1)} %add.292), channel_id=1, source_target_pairs={{0,4},{4,0},{8,12},{12,8},{1,5},{5,1},{9,13},{13,9},{2,6},{6,2},{1... | collective-permute-start | bytes 12296 | tf_op jit(solution)/shard_map/ppermute | solution.py:454
  72.6 3.4 %collective-permute-start.42 = (f32[8,128]{1,0:T(8,128)S(1)}, f32[8,128]{1,0:T(8,128)S(1)}, u32[]{:S(2)}, u32[]{:S(2)}) collective-permute-start(f32[8,128]{1,0:T(8,128)S(1)} %add.293), channel_id=1, source_target_pairs={{0,8},{4,12},{8,0},{12,4},{1,9},{5,13},{9,1},{13,5},{2,10},{6,14},... | collective-permute-start | bytes 12296 | tf_op jit(solution)/shard_map/ppermute | solution.py:454
  75.9 4.7 %collective-permute-start.43 = (f32[8,128]{1,0:T(8,128)S(1)}, f32[8,128]{1,0:T(8,128)S(1)}, u32[]{:S(2)}, u32[]{:S(2)}) collective-permute-start(f32[8,128]{1,0:T(8,128)S(1)} %add.294), channel_id=1, source_target_pairs={{0,1},{1,0},{2,3},{3,2},{4,5},{5,4},{6,7},{7,6},{8,9},{9,8},{10,11... | collective-permute-start | bytes 12296 | tf_op jit(solution)/shard_map/ppermute | solution.py:454
  80.6 2.5 %collective-permute-start.44 = (f32[8,128]{1,0:T(8,128)S(1)}, f32[8,128]{1,0:T(8,128)S(1)}, u32[]{:S(2)}, u32[]{:S(2)}) collective-permute-start(f32[8,128]{1,0:T(8,128)S(1)} %add.295), channel_id=1, source_target_pairs={{0,2},{1,3},{2,0},{3,1},{4,6},{5,7},{6,4},{7,5},{8,10},{9,11},{10,... | collective-permute-start | bytes 12296 | tf_op jit(solution)/shard_map/ppermute | solution.py:454
  83.7 33.6 %copy-start.28 = (f32[3,1,8,96,128]{4,3,2,1,0:T(8,128)S(1)}, f32[3,1,8,96,128]{4,3,2,1,0:T(8,128)}, u32[]{:S(2)}) copy-start(f32[3,1,8,96,128]{4,3,2,1,0:T(8,128)} %param.20) | copy-start | bytes 3538948
  89.2 36.0 %collective-permute-start.46 = (f32[8,96,128]{2,1,0:T(8,128)}, f32[8,96,128]{2,1,0:T(8,128)S(1)}, u32[]{:S(2)}, u32[]{:S(2)}) collective-permute-start(f32[8,96,128]{2,1,0:T(8,128)} %get-tuple-element.222.rest_0_), channel_id=1, source_target_pairs={{0,12},{4,1},{8,5},{12,9},{1,13},{5,2},{9,6},{13,10},{2,14},{6,3},... | collective-permute-start | bytes 1179656 | tf_op jit(solution)/shard_map/ppermute | solution.py:432
  92.3 32.9 %collective-permute-start.47 = (f32[8,96,128]{2,1,0:T(8,128)}, f32[8,96,128]{2,1,0:T(8,128)S(1)}, u32[]{:S(2)}, u32[]{:S(2)}) collective-permute-start(f32[8,96,128]{2,1,0:T(8,128)} %get-tuple-element.222.rest_0_), channel_id=1, source_target_pairs={{12,0},{1,4},{5,8},{9,12},{13,1},{2,5},{6,9},{10,13},{14,2},{3,6},... | collective-permute-start | bytes 1179656 | tf_op jit(solution)/shard_map/ppermute | solution.py:432
  96.1 12.9 %collective-permute-start.48 = (f32[96,128]{1,0:T(8,128)}, f32[96,128]{1,0:T(8,128)S(1)}, u32[]{:S(2)}, u32[]{:S(2)}) collective-permute-start(f32[96,128]{1,0:T(8,128)} %get-tuple-element.223), channel_id=1, source_target_pairs={{0,4},{4,8},{8,12},{12,1},{1,5},{5,9},{9,13},{13,2},{2,6},{6,10},{... | collective-permute-start | bytes 147464 | tf_op jit(solution)/shard_map/ppermute | solution.py:432
  98.4 26.7 %collective-permute-start.50 = (f32[96,128]{1,0:T(8,128)}, f32[96,128]{1,0:T(8,128)S(1)}, u32[]{:S(2)}, u32[]{:S(2)}) collective-permute-start(f32[96,128]{1,0:T(8,128)} %get-tuple-element.223), channel_id=1, source_target_pairs={{0,8},{4,12},{8,1},{12,5},{1,9},{5,13},{9,2},{13,6},{2,10},{6,14},... | collective-permute-start | bytes 147464 | tf_op jit(solution)/shard_map/ppermute | solution.py:432
  101.6 23.5 %collective-permute-start.49 = (f32[96,128]{1,0:T(8,128)}, f32[96,128]{1,0:T(8,128)S(1)}, u32[]{:S(2)}, u32[]{:S(2)}) collective-permute-start(f32[96,128]{1,0:T(8,128)} %get-tuple-element.224), channel_id=1, source_target_pairs={{4,0},{8,4},{12,8},{1,12},{5,1},{9,5},{13,9},{2,13},{6,2},{10,6},{... | collective-permute-start | bytes 147464 | tf_op jit(solution)/shard_map/ppermute | solution.py:432
  109.1 15.3 %copy-start.40 = (f32[96,128]{1,0:T(8,128)}, f32[96,128]{1,0:T(8,128)S(1)}, u32[]{:S(2)}) copy-start(f32[96,128]{1,0:T(8,128)S(1)} %collective-permute-done.48) | copy-start | bytes 147460
  109.1 16.0 %collective-permute-start.51 = (f32[96,128]{1,0:T(8,128)}, f32[96,128]{1,0:T(8,128)S(1)}, u32[]{:S(2)}, u32[]{:S(2)}) collective-permute-start(f32[96,128]{1,0:T(8,128)} %get-tuple-element.224), channel_id=1, source_target_pairs={{8,0},{12,4},{1,8},{5,12},{9,1},{13,5},{2,9},{6,13},{10,2},{14,6},... | collective-permute-start | bytes 147464 | tf_op jit(solution)/shard_map/ppermute | solution.py:432
  125.1 0.6 copy-start.43
  125.1 0.7 copy-start.37
  125.2 0.9 copy-start.38
  (2 other events, 1.2 us)

commit v4 on v3

--- a/solution.py
+++ b/solution.py
@@ -160,16 +160,15 @@
     return modulus, [free * load[c, z] for c in range(3)], free, thick
 
 
-def message_kernel(density, bone, fixed, load, up, down):
-    depth = density.shape[0]
-    raw = (density, bone, fixed, load)
-    up[0] = raw_layer(*raw, depth - 2)[0]
-    modulus, force, _, _ = raw_layer(*raw, depth - 1)
+def message_kernel(*refs):
+    lowest, highest, (up, down) = refs[:8:2], refs[1:8:2], refs[8:]
+    up[0] = raw_layer(*highest, 0)[0]
+    modulus, force, _, _ = raw_layer(*highest, 1)
     up[1] = modulus
     for c in range(3):
         up[2 + c] = force[c]
     for z in range(2):
-        modulus, force, free, _ = raw_layer(*raw, z)
+        modulus, force, free, _ = raw_layer(*lowest, z)
         down[z] = modulus
         for c in range(3):
             down[2 + 3 * z + c] = force[c]
@@ -177,26 +176,39 @@
             down[8] = free
 
 
-def prepare_kernel(density, bone, fixed, load, fields):
+def prepare_kernel(swap, place, density, bone, fixed, load, fields, *edges):
     depth, height, width = density.shape
     zeros = jnp.zeros((LANES - height, width), jnp.float32)
-
-    def layer(z, carry):
+    first = place[0] == 0
+    kinds = len(edges) // 3
+    for z in range(depth):
         modulus, force, free, thick = raw_layer(density, bone, fixed, load, z)
         for slot, value in enumerate([modulus] + force + [free, thick]):
-            square = jnp.concatenate([value, zeros], axis=0)
-            fields[slot, z] = jnp.transpose(square)
-        return carry
-
-    lax.fori_loop(0, depth, layer, 0)
+            turned = jnp.transpose(jnp.concatenate([value, zeros], axis=0))
+            fields[slot, z] = turned
+            if slot == 5:
+                continue
+            low, high = turned[:2], turned[width - 2 :]
+            sent = (jnp.where(first, high, low),) if swap else (low, high)
+            for kind in range(kinds):
+                edges[kind][slot, z] = sent[kind]
+                if z >= depth - 2:
+                    edges[kinds + kind][slot, z - (depth - 2)] = sent[kind]
+                if z < 2:
+                    edges[2 * kinds + kind][slot, z] = sent[kind]
 
 
 def krylov_kernel(
-    k, kappa,
-    fields, up, down, left, right, left_up, right_up, left_down, right_down, weights, planes,
-    out_p, out_w, out_g, out_stats,
-    mod, force, free, search, inverse, lower, upper, image, stress, accumulate,
+    k, kappa, across,
+    place, cover_z, fields, up, down, left, right, left_up, right_up, left_down, right_down,
+    cover_x, cover_y,
+    *rest,
 ):
+    out_p, out_w, out_g, out_stats = rest[:4]
+    out_edges, rest = rest[4:-10], rest[-10:]
+    mod, force, free, search, inverse, lower, upper, image, stress, accumulate = rest
+    on_left = jnp.where(place[0] > 0, 1.0, 0.0)
+    on_right = jnp.where(place[0] < across - 1, 1.0, 0.0)
     depth, width = fields.shape[1], fields.shape[2]
     height = up.shape[1]
     first, last = PAD, PAD + width
@@ -223,12 +235,12 @@
             for i in range(3):
                 force[i, z + 1, into] = fields[1 + i, z, rows]
             free[z, into] = fields[4, z, rows]
-        mod[z + 2, pl.ds(first - 2, 2)] = left[0, z]
-        mod[z + 2, pl.ds(last, 2)] = right[0, z]
+        mod[z + 2, pl.ds(first - 2, 2)] = left[0, z] * on_left
+        mod[z + 2, pl.ds(last, 2)] = right[0, z] * on_right
         for i in range(3):
-            force[i, z + 1, pl.ds(first - 2, 2)] = left[1 + i, z]
-            force[i, z + 1, pl.ds(last, 2)] = right[1 + i, z]
-        free[z, pl.ds(last, 2)] = right[4, z]
+            force[i, z + 1, pl.ds(first - 2, 2)] = left[1 + i, z] * on_left
+            force[i, z + 1, pl.ds(last, 2)] = right[1 + i, z] * on_right
+        free[z, pl.ds(last, 2)] = right[4, z] * on_right
         return carry
 
     lax.fori_loop(0, depth, local, 0)
@@ -236,19 +248,25 @@
     for z in range(2):
         mod[z, body] = turned(up[z])
         mod[depth + 2 + z, body] = turned(down[z])
-        for side, low, high in ((first - 2, left_up, left_down), (last, right_up, right_down)):
-            mod[z, pl.ds(side, 2)] = low[0, z]
-            mod[depth + 2 + z, pl.ds(side, 2)] = high[0, z]
+        for side, low, high, there in (
+            (first - 2, left_up, left_down, on_left),
+            (last, right_up, right_down, on_right),
+        ):
+            mod[z, pl.ds(side, 2)] = low[0, z] * there
+            mod[depth + 2 + z, pl.ds(side, 2)] = high[0, z] * there
     for i in range(3):
         force[i, 0, body] = turned(up[2 + i])
-        for side, low, high in ((first - 2, left_up, left_down), (last, right_up, right_down)):
-            force[i, 0, pl.ds(side, 2)] = low[1 + i, 1]
+        for side, low, high, there in (
+            (first - 2, left_up, left_down, on_left),
+            (last, right_up, right_down, on_right),
+        ):
+            force[i, 0, pl.ds(side, 2)] = low[1 + i, 1] * there
             for z in range(2):
-                force[i, depth + 1 + z, pl.ds(side, 2)] = high[1 + i, z]
+                force[i, depth + 1 + z, pl.ds(side, 2)] = high[1 + i, z] * there
         for z in range(2):
             force[i, depth + 1 + z, body] = turned(down[2 + 3 * z + i])
     free[depth, body] = turned(down[8])
-    free[depth, pl.ds(last, 2)] = right_down[4, 0]
+    free[depth, pl.ds(last, 2)] = right_down[4, 0] * on_right
 
     def divide(chunk, carry):
         row = pl.multiple_of(chunk * 8, 8)
@@ -346,7 +364,8 @@
     def energies(chunk, carry):
         row = pl.multiple_of(PAD + chunk * 8, 8)
         rows = pl.ds(pl.multiple_of(chunk * 8, 8), 8)
-        weight = weights[rows]
+        across_rows = pl.ds(pl.multiple_of(place[0] * width + chunk * 8, 8), 8)
+        weight = cover_x[across_rows] * cover_y[...]
         sums = [jnp.zeros((8, LANES), jnp.float32) for _ in range(5)]
         below = layer_modes(image, 0, row)
         for voxel in range(depth):
@@ -358,7 +377,7 @@
             second_work = half * dotted(modes, stresses(modes, k))
             thick = fields[5, voxel, rows]
             flip = jnp.where(thick > 0.0, 1.0 / jnp.where(thick > 0.0, thick, 1.0), 0.0)
-            spread = weight * planes[voxel]
+            spread = weight * cover_z[place[1] * depth + voxel]
             sums[0] = sums[0] + first_work
             sums[1] = sums[1] + second_work
             for i, work in enumerate((first_work, mixed, second_work)):
@@ -374,32 +393,64 @@
         return carry
 
     lax.fori_loop(0, chunks, energies, 0)
+    for i in range(3):
+        for z in range(depth):
+            low, high = out_g[i, z, pl.ds(0, RAD)], out_g[i, z, pl.ds(width - RAD, RAD)]
+            sent = (jnp.where(place[0] == 0, high, low),) if len(out_edges) == 1 else (low, high)
+            for ref, value in zip(out_edges, sent):
+                ref[i, z] = value
     for s in range(8):
         out_stats[pl.ds(s, 1)] = jnp.sum(accumulate[s], axis=0, keepdims=True)
 
 
 def run_messages(density, bone, fixed, load):
-    _, height, width = density.shape
+    depth, height, width = density.shape
+    specs, arrays = [], []
+    for array in (density, bone, fixed, load):
+        lead = array.shape[:-3]
+        for block in (0, depth // 2 - 1):
+            spot = lambda _, block=block, lead=lead: (0,) * len(lead) + (block, 0, 0)
+            specs.append(pl.BlockSpec(lead + (2, height, width), spot))
+            arrays.append(array)
     return pl.pallas_call(
         message_kernel,
+        grid=(1,),
+        in_specs=specs,
+        out_specs=[pl.BlockSpec((n, height, width), lambda _: (0, 0, 0)) for n in (5, 9)],
         out_shape=[jax.ShapeDtypeStruct((n, height, width), jnp.float32) for n in (5, 9)],
         name="messages",
-    )(density, bone, fixed, load)
-
-
-def run_prepare(density, bone, fixed, load):
+    )(*arrays)
+
+
+SCALAR = pl.BlockSpec(memory_space=pltpu.SMEM)
+VECTOR = pl.BlockSpec(memory_space=pltpu.VMEM)
+
+
+def run_prepare(place, density, bone, fixed, load):
     depth, _, width = density.shape
-    return pl.pallas_call(
-        prepare_kernel,
-        out_shape=jax.ShapeDtypeStruct((6, depth, width, LANES), jnp.float32),
+    swap = lax.axis_size("gx") == 2
+    shapes = [(6, depth, width, LANES)]
+    for layers in (depth, 2, 2):
+        shapes += [(5, layers, 2, LANES)] * (1 if swap else 2)
+    fields, *edges = pl.pallas_call(
+        functools.partial(prepare_kernel, swap),
+        in_specs=[SCALAR] + [VECTOR] * 4,
+        out_specs=[VECTOR] * len(shapes),
+        out_shape=[jax.ShapeDtypeStruct(s, jnp.float32) for s in shapes],
         name="prepare",
-    )(density, bone, fixed, load)
-
-
-def run_krylov(table, fields, halos, weights, planes):
+    )(place, density, bone, fixed, load)
+    kinds = len(edges) // 3
+    return fields, [edges[i * kinds : (i + 1) * kinds] for i in range(3)]
+
+
+def run_krylov(table, place, fields, halos):
     depth, width = fields.shape[1], fields.shape[2]
+    height = halos[0].shape[1]
+    nx = lax.axis_size("gx")
+    slabs = lax.axis_size("gy") * lax.axis_size("gz")
     rows = width + 3 * PAD
     shapes = [(3, depth, width, LANES)] * 3 + [(8, LANES)]
+    shapes += [(3, depth, RAD, LANES)] * (1 if nx == 2 else 2)
     layers = [(depth + 4,), (3, depth + 3), (depth + 1,), (3, depth + 3), (depth + 1,)]
     layers += [(3, depth + 1)] * 3
     scratch = [pltpu.VMEM(lead + (rows, LANES), jnp.float32) for lead in layers]
@@ -407,13 +458,17 @@
         pltpu.VMEM((18, depth, width, LANES), jnp.float32),
         pltpu.VMEM((8, 8, LANES), jnp.float32),
     ]
+    cover_x = coverage(nx * width)[:, None]
+    cover_y = np.pad(coverage(height), (0, LANES - height))[None]
     return pl.pallas_call(
-        functools.partial(krylov_kernel, mode_constants(table), float(table[0, 0])),
+        functools.partial(krylov_kernel, mode_constants(table), float(table[0, 0]), nx),
+        in_specs=[SCALAR] * 2 + [VECTOR] * (len(halos) + 3),
+        out_specs=[VECTOR] * len(shapes),
         out_shape=[jax.ShapeDtypeStruct(s, jnp.float32) for s in shapes],
         scratch_shapes=scratch,
         compiler_params=pltpu.CompilerParams(vmem_limit_bytes=56 * 1024 * 1024),
         name="krylov",
-    )(fields, *halos, weights, planes)
+    )(place, jnp.asarray(coverage(slabs * depth)), fields, *halos, jnp.asarray(cover_x), jnp.asarray(cover_y))
 
 
 def slab_route(steps, sideways=0):
@@ -441,6 +496,14 @@
         none = jnp.zeros_like(got)
         return jnp.where(first, none, got), jnp.where(first, got, none)
     return to_slab(high_edge, steps, 1), to_slab(low_edge, steps, -1)
+
+
+def edges_moved(sent, steps):
+    if len(sent) == 1:
+        spots = slab_route(steps, 1) + slab_route(steps, -1)
+        got = lax.ppermute(sent[0], ("gx", "gy", "gz"), spots)
+        return got, got
+    return to_slab(sent[1], steps, 1), to_slab(sent[0], steps, -1)
 
 
 def total_over_mesh(value):
@@ -534,7 +597,11 @@
     return by_first, by_second, squares, total, jnp.where(sound, 1.0, 0.0)
 
 
-def smooth_kernel(plain, cells, stats, basis, left, right, along_x, along_y, planar, low, high, factors):
+def smooth_kernel(
+    plain, cells, nx, place, stats, basis, left, right, along_x, along_y, planar, low, high, factors
+):
+    on_left = jnp.where(place[0] > 0, 1.0, 0.0)
+    on_right = jnp.where(place[0] < nx - 1, 1.0, 0.0)
     depth = basis.shape[1]
     decay = depth_decay(depth)
     exact = dict(precision=lax.Precision.HIGHEST, preferred_element_type=jnp.float32)
@@ -551,7 +618,11 @@
     factors[pl.ds(4, 4)] = jnp.zeros((4, LANES), jnp.float32)
     for z in range(depth):
         wide = jnp.concatenate(
-            [sum(f * v[i, z] for i, f in enumerate(squares)) for v in (left, basis, right)], axis=0
+            [
+                there * sum(f * v[i, z] for i, f in enumerate(squares))
+                for v, there in ((left, on_left), (basis, 1.0), (right, on_right))
+            ],
+            axis=0,
         )
         half = lax.dot_general(along_x[...], wide, (((1,), (0,)), ((), ())), **exact)
         plane = lax.dot_general(along_y[...], half, (((1,), (1,)), ((), ())), **exact)
@@ -561,17 +632,19 @@
             ref[...] = share if z == 0 else ref[...] + share
 
 
-def run_smooth(plain, cells, stats, basis, sides, height):
+def run_smooth(plain, cells, place, stats, basis, sides, height):
     depth, width = basis.shape[1:3]
     along_x = banded(width + 2 * RAD, width, RAD).T
     along_y = np.zeros((height, LANES), np.float32)
     along_y[:, :height] = banded(height, height, 0).T
     shapes = ((depth, height, width), (height, width), (height, width), (8, LANES))
     return pl.pallas_call(
-        functools.partial(smooth_kernel, plain, float(cells)),
+        functools.partial(smooth_kernel, plain, float(cells), lax.axis_size("gx")),
+        in_specs=[SCALAR] + [VECTOR] * 6,
+        out_specs=[VECTOR] * 4,
         out_shape=[jax.ShapeDtypeStruct(s, jnp.float32) for s in shapes],
         name="smooth",
-    )(stats, basis, *sides, jnp.asarray(along_x), jnp.asarray(along_y))
+    )(place, stats, basis, *sides, jnp.asarray(along_x), jnp.asarray(along_y))
 
 
 def finish_kernel(blocks, factors, density, bone, *rest):
@@ -710,8 +783,8 @@
     return edges_swapped(basis[:, :, :RAD], basis[:, :, width - RAD :], 0)
 
 
-def remodelled(plain, cells, density, bone, stats, basis, sides):
-    planar, low, high, factors = run_smooth(plain, cells, stats, basis, sides, density.shape[1])
+def remodelled(plain, cells, place, density, bone, stats, basis, sides):
+    planar, low, high, factors = run_smooth(plain, cells, place, stats, basis, sides, density.shape[1])
     pieces, blocks = depth_pieces(planar, low, high)
     return run_finish(factors, density, bone, pieces, blocks), factors
 
@@ -722,36 +795,36 @@
     depth, height, width = density.shape
     slabs = lax.axis_size("gy") * lax.axis_size("gz")
     slab = lax.axis_index("gz") * lax.axis_size("gy") + lax.axis_index("gy")
-    across = lax.axis_size("gx") * width
-    cells = density.size * lax.axis_size("gx") * slabs
-    cover_x = lax.dynamic_slice(jnp.asarray(coverage(across)), (lax.axis_index("gx") * width,), (width,))
-    cover_y = jnp.asarray(np.pad(coverage(height), (0, LANES - height)))
-    cover_z = lax.dynamic_slice(jnp.asarray(coverage(slabs * depth)), (slab * depth,), (depth,))
-    weights = cover_x[:, None] * cover_y[None]
-    planes = jnp.broadcast_to(cover_z[:, None, None], (depth, 8, LANES))
+    nx = lax.axis_size("gx")
+    cells = density.size * nx * slabs
+    place = jnp.stack([lax.axis_index("gx"), slab]).astype(jnp.int32)
 
     up, down = run_messages(density, bone, fixed, load)
     got_up = to_slab(up, 1)
     got_down = to_slab(down, -1)
-    fields = run_prepare(density, bone, fixed, load)
-    low, high = fields[:5, :, :2], fields[:5, :, width - 2 :]
-    left, right = edges_swapped(low, high, 0)
-    left_up, right_up = edges_swapped(low[:, depth - 2 :], high[:, depth - 2 :], 1)
-    left_down, right_down = edges_swapped(low[:, :2], high[:, :2], -1)
-    halos = (got_up, got_down, left, right, left_up, right_up, left_down, right_down)
-    first, second, basis, stats = run_krylov(table, fields, halos, weights, planes)
-    sides = side_halos(basis)
+    fields, edges = run_prepare(place, density, bone, fixed, load)
+    around = [side for sent, steps in zip(edges, (0, 1, -1)) for side in edges_moved(sent, steps)]
+    first, second, basis, stats, *ends = run_krylov(
+        table, place, fields, (got_up, got_down, *around)
+    )
+    sides = edges_moved(ends, 0)
     stats = total_over_mesh(stats)
-    updated, factors = remodelled(False, cells, density, bone, stats, basis, sides)
+    updated, factors = remodelled(False, cells, place, density, bone, stats, basis, sides)
     moved = run_displacement(factors, first, second, height)
 
     def repeated(state):
         specific, moved = plain_path(table, density, bone, fixed, load)
-        total = inner_sum(specific * weights[None] * cover_z[:, None, None])
+        cover = lambda length, start, count: lax.dynamic_slice(
+            jnp.asarray(coverage(length)), (start,), (count,)
+        )
+        cover_x = cover(nx * width, place[0] * width, width)
+        cover_z = cover(slabs * depth, place[1] * depth, depth)
+        spread = cover_z[:, None, None] * cover_x[:, None] * jnp.asarray(coverage(height))
+        total = inner_sum(specific[..., :height] * spread)
         row, lane = (lax.broadcasted_iota(jnp.int32, (8, LANES), i) for i in range(2))
         tile = jnp.where((row == 4) & (lane == 0), total, 0.0)
         again = specific[None]
-        updated = remodelled(True, cells, density, bone, tile, again, side_halos(again))[0]
+        updated = remodelled(True, cells, place, density, bone, tile, again, side_halos(again))[0]
         return True, updated, moved.reshape(-1, width)
 
     sound = factors[3, 0] > 0.5

time: 129 us -> 117 us (0.907)
  the two profiles are of different devices: /device:TPU:5 before, /device:TPU:9 now
where the time goes in v4:
time: 117 us
  starting transfers between devices  50.4 us (43%)
  Pallas kernels  36.7 us (31%)
  waiting for transfers between devices  21.3 us (18%)
  local copies, waits for them, and re-layouts  5.56 us (5%)
  between operations  1.55 us (1%)
  other arithmetic  1.36 us (1%)
    ppermute x8, starting transfers between devices, to_slab(): return lax.ppermute(value, ('gx', 'gy', 'gz'), slab_route(steps, sideways))  30.6 us
    pallas_call x1, Pallas kernels, run_krylov(): pl.pallas_call(functools.partial(krylov_kernel, mode_constants(table), fl...  19.1 us
    ppermute x5, starting transfers between devices, total_over_mesh(): other = lax.ppermute(value, axis, [(i, i ^ step) for i in range(count)])  11.9 us
    ppermute x5, waiting for transfers between devices, total_over_mesh(): other = lax.ppermute(value, axis, [(i, i ^ step) for i in range(count)])  10 us
    ppermute x4, starting transfers between devices, edges_moved(): got = lax.ppermute(sent[0], ('gx', 'gy', 'gz'), spots)  7.9 us
    ppermute x8, waiting for transfers between devices, to_slab(): return lax.ppermute(value, ('gx', 'gy', 'gz'), slab_route(steps, sideways))  6.2 us
    ppermute x4, waiting for transfers between devices, edges_moved(): got = lax.ppermute(sent[0], ('gx', 'gy', 'gz'), spots)  5.15 us
    pallas_call x1, Pallas kernels, run_smooth(): pl.pallas_call(functools.partial(smooth_kernel, plain, float(cells), lax....  4.66 us
  transfers between devices with their start and end apart: 17, of which 8 were waited for; matrix products, arithmetic and copies ran while one was open for 4% of the time, Pallas kernels for 7%

profile of v4, /device:TPU:9, one launch (start us, length us, event | category | flops | bytes accessed | tf_op | source)
XLA Modules:
  0.0 116.9 jit_solution(15480836322462632802)
XLA Ops:
  0.7 2.3 %messages.1 = (f32[5,96,128]{2,1,0:T(8,128)}, f32[9,96,128]{2,1,0:T(8,128)}) custom-call(f32[8,96,128]{2,1,0:T(8,128)} %bitcast.113, f32[8,96,128]{2,1,0:T(8,128)} %bitcast.114, s32[8,96,128]{2,1,0:T(8,128)} %bitcast.121, s32[8,96,128]{2,1,0:T(8,128)} %bitcast.122, s32[8,96,128]{2,1,0:T(8,128)} %bitcast.129, s32[8,96,128]{2,1,0:T(8,128)} %bitcast.130, ...), custom_call_target="tpu_custom_call" | custom-call | tf_op jit(solution)/shard_map/messages/pallas_call | solution.py:415
  3.0 1.9 %collective-permute-start.36 = (f32[9,96,128]{2,1,0:T(8,128)}, f32[9,96,128]{2,1,0:T(8,128)S(1)}, u32[]{:S(2)}, u32[]{:S(2)}) collective-permute-start(f32[9,96,128]{2,1,0:T(8,128)} %get-tuple-element.244), channel_id=1, source_target_pairs={{4,0},{8,4},{12,8},{1,12},{5,1},{9,5},{13,9},{2,13},{6,2},{10,6},{... | collective-permute-start | bytes 1327112 | tf_op jit(solution)/shard_map/ppermute | solution.py:487
  4.9 3.4 %collective-permute-start.35 = (f32[5,96,128]{2,1,0:T(8,128)}, f32[5,96,128]{2,1,0:T(8,128)S(1)}, u32[]{:S(2)}, u32[]{:S(2)}) collective-permute-start(f32[5,96,128]{2,1,0:T(8,128)} %get-tuple-element.243), channel_id=1, source_target_pairs={{0,4},{4,8},{8,12},{12,1},{1,5},{5,9},{9,13},{13,2},{2,6},{6,10},{... | collective-permute-start | bytes 737288 | tf_op jit(solution)/shard_map/ppermute | solution.py:487
  8.4 3.9 %prepare.1 = (f32[6,8,128,128]{3,2,1,0:T(8,128)}, f32[5,8,2,128]{3,2,1,0:T(2,128)}, f32[5,2,2,128]{3,2,1,0:T(2,128)}, f32[5,2,2,128]{3,2,1,0:T(2,128)}) custom-call(s32[2]{0:T(128)S(1)} %pad_add_fusion.2.place, f32[8,96,128]{2,1,0:T(8,128)S(1)} %bitcast.115, s32[8,96,128]{2,1,0:T(8,128)S(1)} %bitcast.123, s32[8,96,128]{2,1,0:T(8,128)S(1)} %bitcast.131, ...), custom_call_target="tpu_custom_call" | custom-call | tf_op jit(solution)/shard_map/prepare/pallas_call | solution.py:435
  12.2 1.2 %collective-permute-start.37 = (f32[5,8,2,128]{3,2,1,0:T(2,128)}, f32[5,8,2,128]{3,2,1,0:T(2,128)S(1)}, u32[]{:S(2)}, u32[]{:S(2)}) collective-permute-start(f32[5,8,2,128]{3,2,1,0:T(2,128)} %get-tuple-element.245), channel_id=1, source_target_pairs={{0,16},{4,20},{8,24},{12,28},{1,17},{5,21},{9,25},{13,29},{2,18},{... | collective-permute-start | bytes 122888 | tf_op jit(solution)/shard_map/ppermute | solution.py:504
  13.4 3.2 %collective-permute-start.38 = (f32[5,2,2,128]{3,2,1,0:T(2,128)}, f32[5,2,2,128]{3,2,1,0:T(2,128)S(1)}, u32[]{:S(2)}, u32[]{:S(2)}) collective-permute-start(f32[5,2,2,128]{3,2,1,0:T(2,128)} %get-tuple-element.246), channel_id=1, source_target_pairs={{0,20},{4,24},{8,28},{12,17},{1,21},{5,25},{9,29},{13,18},{2,22},{... | collective-permute-start | bytes 30728 | tf_op jit(solution)/shard_map/ppermute | solution.py:504
  16.6 3.2 %collective-permute-start.39 = (f32[5,2,2,128]{3,2,1,0:T(2,128)}, f32[5,2,2,128]{3,2,1,0:T(2,128)S(1)}, u32[]{:S(2)}, u32[]{:S(2)}) collective-permute-start(f32[5,2,2,128]{3,2,1,0:T(2,128)} %get-tuple-element.247), channel_id=1, source_target_pairs={{4,16},{8,20},{12,24},{1,28},{5,17},{9,21},{13,25},{2,29},{6,18},{... | collective-permute-start | bytes 30728 | tf_op jit(solution)/shard_map/ppermute | solution.py:504
  19.8 1.5 %collective-permute-done.38.left_up.right_up = f32[5,2,2,128]{3,2,1,0:T(2,128)S(1)} collective-permute-done((f32[5,2,2,128]{3,2,1,0:T(2,128)}, f32[5,2,2,128]{3,2,1,0:T(2,128)S(1)}, u32[]{:S(2)}, u32[]{:S(2)}) %collective-permute-start.38) | collective-permute-done | bytes 10272 | tf_op jit(solution)/shard_map/ppermute | solution.py:504
  21.3 3.7 %collective-permute-done.39.left_down.right_down = f32[5,2,2,128]{3,2,1,0:T(2,128)S(1)} collective-permute-done((f32[5,2,2,128]{3,2,1,0:T(2,128)}, f32[5,2,2,128]{3,2,1,0:T(2,128)S(1)}, u32[]{:S(2)}, u32[]{:S(2)}) %collective-permute-start.39) | collective-permute-done | bytes 10272 | tf_op jit(solution)/shard_map/ppermute | solution.py:504
  25.9 19.1 %krylov.1 = (f32[3,8,128,128]{3,2,1,0:T(8,128)}, f32[3,8,128,128]{3,2,1,0:T(8,128)}, f32[3,8,128,128]{3,2,1,0:T(8,128)}, f32[8,128]{1,0:T(8,128)}, f32[3,8,24,128]{3,2,1,0:T(8,128)}) custom-call(s32[2]{0:T(128)S(1)} %pad_add_fusion.2.place, f32[128]{0:T(128)} %constant.89.clone.cover_z, f32[6,8,128,128]{3,2,1,0:T(8,128)} %get-tuple-element.242.fields, ...), custom_call_target="tpu_custom_call" | custom-call | tf_op jit(solution)/shard_map/krylov/pallas_call | solution.py:463
  45.2 1.2 %collective-permute-start.40 = (f32[8,128]{1,0:T(8,128)}, f32[8,128]{1,0:T(8,128)S(1)}, u32[]{:S(2)}, u32[]{:S(2)}) collective-permute-start(f32[8,128]{1,0:T(8,128)} %get-tuple-element.248), channel_id=1, source_target_pairs={{0,16},{16,0},{1,17},{17,1},{2,18},{18,2},{3,19},{19,3},{4,20},{20... | collective-permute-start | bytes 12296 | tf_op jit(solution)/shard_map/ppermute | solution.py:517
  46.5 6.2 %collective-permute-done.40 = f32[8,128]{1,0:T(8,128)S(1)} collective-permute-done((f32[8,128]{1,0:T(8,128)}, f32[8,128]{1,0:T(8,128)S(1)}, u32[]{:S(2)}, u32[]{:S(2)}) %collective-permute-start.40) | collective-permute-done | bytes 4128 | tf_op jit(solution)/shard_map/ppermute | solution.py:517
  53.3 1.7 %collective-permute-start.41 = (f32[8,128]{1,0:T(8,128)S(1)}, f32[8,128]{1,0:T(8,128)S(1)}, u32[]{:S(2)}, u32[]{:S(2)}) collective-permute-start(f32[8,128]{1,0:T(8,128)S(1)} %add.290), channel_id=1, source_target_pairs={{0,4},{4,0},{8,12},{12,8},{1,5},{5,1},{9,13},{13,9},{2,6},{6,2},{1... | collective-permute-start | bytes 12296 | tf_op jit(solution)/shard_map/ppermute | solution.py:517
  55.0 1.0 collective-permute-done.41
  56.0 5.2 %collective-permute-start.42 = (f32[8,128]{1,0:T(8,128)S(1)}, f32[8,128]{1,0:T(8,128)S(1)}, u32[]{:S(2)}, u32[]{:S(2)}) collective-permute-start(f32[8,128]{1,0:T(8,128)S(1)} %add.291), channel_id=1, source_target_pairs={{0,8},{4,12},{8,0},{12,4},{1,9},{5,13},{9,1},{13,5},{2,10},{6,14},... | collective-permute-start | bytes 12296 | tf_op jit(solution)/shard_map/ppermute | solution.py:517
  61.2 1.0 collective-permute-done.42
  62.2 2.1 %collective-permute-start.43 = (f32[8,128]{1,0:T(8,128)S(1)}, f32[8,128]{1,0:T(8,128)S(1)}, u32[]{:S(2)}, u32[]{:S(2)}) collective-permute-start(f32[8,128]{1,0:T(8,128)S(1)} %add.292), channel_id=1, source_target_pairs={{0,1},{1,0},{2,3},{3,2},{4,5},{5,4},{6,7},{7,6},{8,9},{9,8},{10,11... | collective-permute-start | bytes 12296 | tf_op jit(solution)/shard_map/ppermute | solution.py:517
  64.3 0.8 collective-permute-done.43
  65.1 1.7 %collective-permute-start.44 = (f32[8,128]{1,0:T(8,128)S(1)}, f32[8,128]{1,0:T(8,128)S(1)}, u32[]{:S(2)}, u32[]{:S(2)}) collective-permute-start(f32[8,128]{1,0:T(8,128)S(1)} %add.293), channel_id=1, source_target_pairs={{0,2},{1,3},{2,0},{3,1},{4,6},{5,7},{6,4},{7,5},{8,10},{9,11},{10,... | collective-permute-start | bytes 12296 | tf_op jit(solution)/shard_map/ppermute | solution.py:517
  66.8 1.0 collective-permute-done.44
  69.1 4.7 %smooth.2 = (f32[8,96,128]{2,1,0:T(8,128)}, f32[96,128]{1,0:T(8,128)}, f32[96,128]{1,0:T(8,128)}, f32[8,128]{1,0:T(8,128)}) custom-call(s32[2]{0:T(128)S(1)} %pad_add_fusion.2.place, f32[8,128]{1,0:T(8,128)} %add.294.stats, f32[3,8,128,128]{3,2,1,0:T(8,128)} %get-tuple-element.249.basis, f32[3,8,24,128]{3,2,1,0:T(8,128)} %copy-done.35, ...), custom_call_target="tpu_custom_call" | custom-call | tf_op jit(solution)/shard_map/smooth/pallas_call | solution.py:641
  73.8 4.2 %collective-permute-start.46 = (f32[8,96,128]{2,1,0:T(8,128)}, f32[8,96,128]{2,1,0:T(8,128)S(1)}, u32[]{:S(2)}, u32[]{:S(2)}) collective-permute-start(f32[8,96,128]{2,1,0:T(8,128)} %get-tuple-element.252.rest_0_), channel_id=1, source_target_pairs={{0,12},{4,1},{8,5},{12,9},{1,13},{5,2},{9,6},{13,10},{2,14},{6,3},... | collective-permute-start | bytes 1179656 | tf_op jit(solution)/shard_map/ppermute | solution.py:487
  78.0 1.9 %collective-permute-start.47 = (f32[8,96,128]{2,1,0:T(8,128)}, f32[8,96,128]{2,1,0:T(8,128)S(1)}, u32[]{:S(2)}, u32[]{:S(2)}) collective-permute-start(f32[8,96,128]{2,1,0:T(8,128)} %get-tuple-element.252.rest_0_), channel_id=1, source_target_pairs={{12,0},{1,4},{5,8},{9,12},{13,1},{2,5},{6,9},{10,13},{14,2},{3,6},... | collective-permute-start | bytes 1179656 | tf_op jit(solution)/shard_map/ppermute | solution.py:487
  79.9 7.3 %collective-permute-start.51 = (f32[96,128]{1,0:T(8,128)}, f32[96,128]{1,0:T(8,128)S(1)}, u32[]{:S(2)}, u32[]{:S(2)}) collective-permute-start(f32[96,128]{1,0:T(8,128)} %get-tuple-element.254), channel_id=1, source_target_pairs={{8,0},{12,4},{1,8},{5,12},{9,1},{13,5},{2,9},{6,13},{10,2},{14,6},... | collective-permute-start | bytes 147464 | tf_op jit(solution)/shard_map/ppermute | solution.py:487
  87.2 1.9 %collective-permute-start.49 = (f32[96,128]{1,0:T(8,128)}, f32[96,128]{1,0:T(8,128)S(1)}, u32[]{:S(2)}, u32[]{:S(2)}) collective-permute-start(f32[96,128]{1,0:T(8,128)} %get-tuple-element.254), channel_id=1, source_target_pairs={{4,0},{8,4},{12,8},{1,12},{5,1},{9,5},{13,9},{2,13},{6,2},{10,6},{... | collective-permute-start | bytes 147464 | tf_op jit(solution)/shard_map/ppermute | solution.py:487
  89.1 3.4 %collective-permute-start.48 = (f32[96,128]{1,0:T(8,128)}, f32[96,128]{1,0:T(8,128)S(1)}, u32[]{:S(2)}, u32[]{:S(2)}) collective-permute-start(f32[96,128]{1,0:T(8,128)} %get-tuple-element.253), channel_id=1, source_target_pairs={{0,4},{4,8},{8,12},{12,1},{1,5},{5,9},{9,13},{13,2},{2,6},{6,10},{... | collective-permute-start | bytes 147464 | tf_op jit(solution)/shard_map/ppermute | solution.py:487
  92.5 6.2 %collective-permute-done.51 = f32[96,128]{1,0:T(8,128)S(1)} collective-permute-done((f32[96,128]{1,0:T(8,128)}, f32[96,128]{1,0:T(8,128)S(1)}, u32[]{:S(2)}, u32[]{:S(2)}) %collective-permute-start.51) | collective-permute-done | bytes 49184 | tf_op jit(solution)/shard_map/ppermute | solution.py:487
  98.6 6.7 %collective-permute-start.50 = (f32[96,128]{1,0:T(8,128)}, f32[96,128]{1,0:T(8,128)S(1)}, u32[]{:S(2)}, u32[]{:S(2)}) collective-permute-start(f32[96,128]{1,0:T(8,128)} %get-tuple-element.253), channel_id=1, source_target_pairs={{0,8},{4,12},{8,1},{12,5},{1,9},{5,13},{9,2},{13,6},{2,10},{6,14},... | collective-permute-start | bytes 147464 | tf_op jit(solution)/shard_map/ppermute | solution.py:487
  105.4 2.0 %copy.94 = f32[3,8,96,128]{3,0,2,1:T(4,128)} copy(f32[3,8,96,128]{3,2,1,0:T(8,128)S(1)} %bitcast.137) | data formatting | bytes 2359296
  107.3 1.2 %slice.457 = f32[1,1]{1,0:T(1,128)} slice(f32[8,128]{1,0:T(8,128)} %get-tuple-element.251.factors), slice={[3:4], [0:1]} | slice | bytes 8 | tf_op jit(solution)/shard_map/slice | solution.py:830
  108.5 3.9 %displacement.1 = f32[3,8,96,128]{3,2,1,0:T(8,128)} custom-call(f32[8,128]{1,0:T(8,128)} %get-tuple-element.251.factors, f32[3,8,128,128]{3,2,1,0:T(8,128)} %get-tuple-element.255.first, f32[3,8,128,128]{3,2,1,0:T(8,128)} %get-tuple-element.256.second), custom_call_target="tpu_custom_call" | custom-call | tf_op jit(solution)/shard_map/displacement/pallas_call | solution.py:697
  114.1 2.8 %finish.2 = f32[8,96,128]{2,1,0:T(8,128)} custom-call(f32[8,128]{1,0:T(8,128)} %get-tuple-element.251.factors, f32[8,96,128]{2,1,0:T(8,128)S(1)} %bitcast.116, s32[8,96,128]{2,1,0:T(8,128)S(1)} %bitcast.124, f32[8,96,128]{2,1,0:T(8,128)} %get-tuple-element.252.rest_0_, f32[8,96,128]{2,1,0:T(8,128)} %copy-done.37, f32[8,96,128]{2,1,0:T(8,128)} %copy-done.38, ...), custom_call_target="tpu_custom_call" | custom-call | tf_op jit(solution)/shard_map/finish/pallas_call | solution.py:676
  (51 shorter events, 4.1 us)
Async XLA Ops:
  0.6 7.7 %copy-start.12 = (f32[1,8,96,128]{3,2,1,0:T(8,128)S(1)}, f32[1,8,96,128]{3,2,1,0:T(8,128)}, u32[]{:S(2)}) copy-start(f32[1,8,96,128]{3,2,1,0:T(8,128)} %param.20) | copy-start | bytes 1179652
  0.6 7.7 %copy-start.21 = (s32[1,8,96,128]{3,2,1,0:T(8,128)S(1)}, s32[1,8,96,128]{3,2,1,0:T(8,128)}, u32[]{:S(2)}) copy-start(s32[1,8,96,128]{3,2,1,0:T(8,128)} %param.21) | copy-start | bytes 1179652
  0.7 7.7 %copy-start.24 = (s32[1,8,96,128]{3,2,1,0:T(8,128)S(1)}, s32[1,8,96,128]{3,2,1,0:T(8,128)}, u32[]{:S(2)}) copy-start(s32[1,8,96,128]{3,2,1,0:T(8,128)} %param.22) | copy-start | bytes 1179652
  3.0 22.0 %collective-permute-start.36 = (f32[9,96,128]{2,1,0:T(8,128)}, f32[9,96,128]{2,1,0:T(8,128)S(1)}, u32[]{:S(2)}, u32[]{:S(2)}) collective-permute-start(f32[9,96,128]{2,1,0:T(8,128)} %get-tuple-element.244), channel_id=1, source_target_pairs={{4,0},{8,4},{12,8},{1,12},{5,1},{9,5},{13,9},{2,13},{6,2},{10,6},{... | collective-permute-start | bytes 1327112 | tf_op jit(solution)/shard_map/ppermute | solution.py:487
  4.9 20.1 %collective-permute-start.35 = (f32[5,96,128]{2,1,0:T(8,128)}, f32[5,96,128]{2,1,0:T(8,128)S(1)}, u32[]{:S(2)}, u32[]{:S(2)}) collective-permute-start(f32[5,96,128]{2,1,0:T(8,128)} %get-tuple-element.243), channel_id=1, source_target_pairs={{0,4},{4,8},{8,12},{12,1},{1,5},{5,9},{9,13},{13,2},{2,6},{6,10},{... | collective-permute-start | bytes 737288 | tf_op jit(solution)/shard_map/ppermute | solution.py:487
  8.3 60.1 %copy-start.47 = (s32[2]{0:T(128)}, s32[2]{0:T(128)S(1)}, u32[]{:S(2)}) copy-start(s32[2]{0:T(128)S(1)} %pad_add_fusion.2.place) | copy-start | bytes 28
  12.2 12.8 %collective-permute-start.37 = (f32[5,8,2,128]{3,2,1,0:T(2,128)}, f32[5,8,2,128]{3,2,1,0:T(2,128)S(1)}, u32[]{:S(2)}, u32[]{:S(2)}) collective-permute-start(f32[5,8,2,128]{3,2,1,0:T(2,128)} %get-tuple-element.245), channel_id=1, source_target_pairs={{0,16},{4,20},{8,24},{12,28},{1,17},{5,21},{9,25},{13,29},{2,18},{... | collective-permute-start | bytes 122888 | tf_op jit(solution)/shard_map/ppermute | solution.py:504
  13.4 7.9 %collective-permute-start.38 = (f32[5,2,2,128]{3,2,1,0:T(2,128)}, f32[5,2,2,128]{3,2,1,0:T(2,128)S(1)}, u32[]{:S(2)}, u32[]{:S(2)}) collective-permute-start(f32[5,2,2,128]{3,2,1,0:T(2,128)} %get-tuple-element.246), channel_id=1, source_target_pairs={{0,20},{4,24},{8,28},{12,17},{1,21},{5,25},{9,29},{13,18},{2,22},{... | collective-permute-start | bytes 30728 | tf_op jit(solution)/shard_map/ppermute | solution.py:504
  16.6 8.4 %collective-permute-start.39 = (f32[5,2,2,128]{3,2,1,0:T(2,128)}, f32[5,2,2,128]{3,2,1,0:T(2,128)S(1)}, u32[]{:S(2)}, u32[]{:S(2)}) collective-permute-start(f32[5,2,2,128]{3,2,1,0:T(2,128)} %get-tuple-element.247), channel_id=1, source_target_pairs={{4,16},{8,20},{12,24},{1,28},{5,17},{9,21},{13,25},{2,29},{6,18},{... | collective-permute-start | bytes 30728 | tf_op jit(solution)/shard_map/ppermute | solution.py:504
  21.3 3.7 %copy-start.45 = (f32[5,2,2,128]{3,2,1,0:T(2,128)}, f32[5,2,2,128]{3,2,1,0:T(2,128)S(1)}, u32[]{:S(2)}) copy-start(f32[5,2,2,128]{3,2,1,0:T(2,128)S(1)} %collective-permute-done.38.left_up.right_up) | copy-start | bytes 30724
  25.0 0.6 copy-start.40
  25.0 0.7 copy-start.39
  25.0 0.8 copy-start.36
  44.9 60.4 %copy-start.26 = (f32[3,1,8,96,128]{4,3,2,1,0:T(8,128)S(1)}, f32[3,1,8,96,128]{4,3,2,1,0:T(8,128)}, u32[]{:S(2)}) copy-start(f32[3,1,8,96,128]{4,3,2,1,0:T(8,128)} %param.23) | copy-start | bytes 3538948
  44.9 23.5 %collective-permute-start.45 = (f32[3,8,24,128]{3,2,1,0:T(8,128)}, f32[3,8,24,128]{3,2,1,0:T(8,128)S(1)}, u32[]{:S(2)}, u32[]{:S(2)}) collective-permute-start(f32[3,8,24,128]{3,2,1,0:T(8,128)} %get-tuple-element.250), channel_id=1, source_target_pairs={{0,16},{4,20},{8,24},{12,28},{1,17},{5,21},{9,25},{13,29},{2,18},{... | collective-permute-start | bytes 884744 | tf_op jit(solution)/shard_map/ppermute | solution.py:504
  45.2 7.4 %collective-permute-start.40 = (f32[8,128]{1,0:T(8,128)}, f32[8,128]{1,0:T(8,128)S(1)}, u32[]{:S(2)}, u32[]{:S(2)}) collective-permute-start(f32[8,128]{1,0:T(8,128)} %get-tuple-element.248), channel_id=1, source_target_pairs={{0,16},{16,0},{1,17},{17,1},{2,18},{18,2},{3,19},{19,3},{4,20},{20... | collective-permute-start | bytes 12296 | tf_op jit(solution)/shard_map/ppermute | solution.py:517
  53.3 2.7 %collective-permute-start.41 = (f32[8,128]{1,0:T(8,128)S(1)}, f32[8,128]{1,0:T(8,128)S(1)}, u32[]{:S(2)}, u32[]{:S(2)}) collective-permute-start(f32[8,128]{1,0:T(8,128)S(1)} %add.290), channel_id=1, source_target_pairs={{0,4},{4,0},{8,12},{12,8},{1,5},{5,1},{9,13},{13,9},{2,6},{6,2},{1... | collective-permute-start | bytes 12296 | tf_op jit(solution)/shard_map/ppermute | solution.py:517
  56.0 6.2 %collective-permute-start.42 = (f32[8,128]{1,0:T(8,128)S(1)}, f32[8,128]{1,0:T(8,128)S(1)}, u32[]{:S(2)}, u32[]{:S(2)}) collective-permute-start(f32[8,128]{1,0:T(8,128)S(1)} %add.291), channel_id=1, source_target_pairs={{0,8},{4,12},{8,0},{12,4},{1,9},{5,13},{9,1},{13,5},{2,10},{6,14},... | collective-permute-start | bytes 12296 | tf_op jit(solution)/shard_map/ppermute | solution.py:517
  62.2 2.9 %collective-permute-start.43 = (f32[8,128]{1,0:T(8,128)S(1)}, f32[8,128]{1,0:T(8,128)S(1)}, u32[]{:S(2)}, u32[]{:S(2)}) collective-permute-start(f32[8,128]{1,0:T(8,128)S(1)} %add.292), channel_id=1, source_target_pairs={{0,1},{1,0},{2,3},{3,2},{4,5},{5,4},{6,7},{7,6},{8,9},{9,8},{10,11... | collective-permute-start | bytes 12296 | tf_op jit(solution)/shard_map/ppermute | solution.py:517
  65.1 2.7 %collective-permute-start.44 = (f32[8,128]{1,0:T(8,128)S(1)}, f32[8,128]{1,0:T(8,128)S(1)}, u32[]{:S(2)}, u32[]{:S(2)}) collective-permute-start(f32[8,128]{1,0:T(8,128)S(1)} %add.293), channel_id=1, source_target_pairs={{0,2},{1,3},{2,0},{3,1},{4,6},{5,7},{6,4},{7,5},{8,10},{9,11},{10,... | collective-permute-start | bytes 12296 | tf_op jit(solution)/shard_map/ppermute | solution.py:517
  68.4 0.7 copy-start.35
  73.8 39.4 %collective-permute-start.46 = (f32[8,96,128]{2,1,0:T(8,128)}, f32[8,96,128]{2,1,0:T(8,128)S(1)}, u32[]{:S(2)}, u32[]{:S(2)}) collective-permute-start(f32[8,96,128]{2,1,0:T(8,128)} %get-tuple-element.252.rest_0_), channel_id=1, source_target_pairs={{0,12},{4,1},{8,5},{12,9},{1,13},{5,2},{9,6},{13,10},{2,14},{6,3},... | collective-permute-start | bytes 1179656 | tf_op jit(solution)/shard_map/ppermute | solution.py:487
  78.0 35.2 %collective-permute-start.47 = (f32[8,96,128]{2,1,0:T(8,128)}, f32[8,96,128]{2,1,0:T(8,128)S(1)}, u32[]{:S(2)}, u32[]{:S(2)}) collective-permute-start(f32[8,96,128]{2,1,0:T(8,128)} %get-tuple-element.252.rest_0_), channel_id=1, source_target_pairs={{12,0},{1,4},{5,8},{9,12},{13,1},{2,5},{6,9},{10,13},{14,2},{3,6},... | collective-permute-start | bytes 1179656 | tf_op jit(solution)/shard_map/ppermute | solution.py:487
  79.9 18.7 %collective-permute-start.51 = (f32[96,128]{1,0:T(8,128)}, f32[96,128]{1,0:T(8,128)S(1)}, u32[]{:S(2)}, u32[]{:S(2)}) collective-permute-start(f32[96,128]{1,0:T(8,128)} %get-tuple-element.254), channel_id=1, source_target_pairs={{8,0},{12,4},{1,8},{5,12},{9,1},{13,5},{2,9},{6,13},{10,2},{14,6},... | collective-permute-start | bytes 147464 | tf_op jit(solution)/shard_map/ppermute | solution.py:487
  87.2 26.0 %collective-permute-start.49 = (f32[96,128]{1,0:T(8,128)}, f32[96,128]{1,0:T(8,128)S(1)}, u32[]{:S(2)}, u32[]{:S(2)}) collective-permute-start(f32[96,128]{1,0:T(8,128)} %get-tuple-element.254), channel_id=1, source_target_pairs={{4,0},{8,4},{12,8},{1,12},{5,1},{9,5},{13,9},{2,13},{6,2},{10,6},{... | collective-permute-start | bytes 147464 | tf_op jit(solution)/shard_map/ppermute | solution.py:487
  89.1 24.0 %collective-permute-start.48 = (f32[96,128]{1,0:T(8,128)}, f32[96,128]{1,0:T(8,128)S(1)}, u32[]{:S(2)}, u32[]{:S(2)}) collective-permute-start(f32[96,128]{1,0:T(8,128)} %get-tuple-element.253), channel_id=1, source_target_pairs={{0,4},{4,8},{8,12},{12,1},{1,5},{5,9},{9,13},{13,2},{2,6},{6,10},{... | collective-permute-start | bytes 147464 | tf_op jit(solution)/shard_map/ppermute | solution.py:487
  98.6 13.8 %copy-start.41 = (f32[96,128]{1,0:T(8,128)}, f32[96,128]{1,0:T(8,128)S(1)}, u32[]{:S(2)}) copy-start(f32[96,128]{1,0:T(8,128)S(1)} %collective-permute-done.51) | copy-start | bytes 147460
  98.6 14.5 %collective-permute-start.50 = (f32[96,128]{1,0:T(8,128)}, f32[96,128]{1,0:T(8,128)S(1)}, u32[]{:S(2)}, u32[]{:S(2)}) collective-permute-start(f32[96,128]{1,0:T(8,128)} %get-tuple-element.253), channel_id=1, source_target_pairs={{0,8},{4,12},{8,1},{12,5},{1,9},{5,13},{9,2},{13,6},{2,10},{6,14},... | collective-permute-start | bytes 147464 | tf_op jit(solution)/shard_map/ppermute | solution.py:487
  113.1 0.6 copy-start.43
  113.2 0.6 copy-start.44
  113.2 0.7 copy-start.37
  113.2 0.9 copy-start.38
  (2 other events, 1.2 us)

commit v5 on v4

--- a/solution.py
+++ b/solution.py
@@ -507,7 +507,7 @@
 
 
 def total_over_mesh(value):
-    for axis in ("gx", "gy", "gz"):
+    for axis in ("gz", "gy", "gx"):
         count = lax.axis_size(axis)
         if count & (count - 1):
             value = lax.psum(value, axis)
@@ -812,8 +812,11 @@
     updated, factors = remodelled(False, cells, place, density, bone, stats, basis, sides)
     moved = run_displacement(factors, first, second, height)
 
+    kept = [v.reshape(-1, width) for v in (density, bone, fixed, load)]
+
     def repeated(state):
-        specific, moved = plain_path(table, density, bone, fixed, load)
+        again = [v.reshape((-1, depth, height, width)) for v in kept]
+        specific, moved = plain_path(table, *(v[0] for v in again[:3]), again[3])
         cover = lambda length, start, count: lax.dynamic_slice(
             jnp.asarray(coverage(length)), (start,), (count,)
         )

time: 117 us -> 113 us (0.966)
  starting transfers between devices: 50.4 us -> 46.6 us
  waiting for transfers between devices: 21.3 us -> 19.2 us
    ppermute x5, starting transfers between devices: 11.9 us -> 7.73 us  [total_over_mesh(): other = lax.ppermute(value, axis, [(i, i ^ step) for i in range(count)])]
    ppermute x5, waiting for transfers between devices: 10 us -> 8.16 us  [total_over_mesh(): other = lax.ppermute(value, axis, [(i, i ^ step) for i in range(count)])]
    unnamed x35 -> x24, local copies, waits for them, and re-layouts: 4.39 us -> 5.23 us
  transfers between devices with their start and end apart: 17 -> 17, of which waited for: 8 -> 8; matrix products, arithmetic and copies ran while one was open for 4% -> 6% of each run, Pallas kernels for 7% -> 7%
where the time goes in v5:
time: 113 us; the launch traced here: 112 us
  starting transfers between devices  46.6 us (41%)
  Pallas kernels  36.9 us (33%)
  waiting for transfers between devices  19.2 us (17%)
  local copies, waits for them, and re-layouts  6.42 us (6%)
  between operations  1.52 us (1%)
  other arithmetic  1.36 us (1%)
    ppermute x8, starting transfers between devices, to_slab(): return lax.ppermute(value, ('gx', 'gy', 'gz'), slab_route(steps, sideways))  31 us
    pallas_call x1, Pallas kernels, run_krylov(): pl.pallas_call(functools.partial(krylov_kernel, mode_constants(table), fl...  19.1 us
    ppermute x5, waiting for transfers between devices, total_over_mesh(): other = lax.ppermute(value, axis, [(i, i ^ step) for i in range(count)])  8.16 us
    ppermute x4, starting transfers between devices, edges_moved(): got = lax.ppermute(sent[0], ('gx', 'gy', 'gz'), spots)  7.85 us
    ppermute x5, starting transfers between devices, total_over_mesh(): other = lax.ppermute(value, axis, [(i, i ^ step) for i in range(count)])  7.73 us
    ppermute x8, waiting for transfers between devices, to_slab(): return lax.ppermute(value, ('gx', 'gy', 'gz'), slab_route(steps, sideways))  5.9 us
    unnamed x24, local copies, waits for them, and re-layouts  5.23 us
    ppermute x4, waiting for transfers between devices, edges_moved(): got = lax.ppermute(sent[0], ('gx', 'gy', 'gz'), spots)  5.15 us
  transfers between devices with their start and end apart: 17, of which 8 were waited for; matrix products, arithmetic and copies ran while one was open for 6% of the time, Pallas kernels for 7%

profile of v5, /device:TPU:9, one launch (start us, length us, event | category | flops | bytes accessed | tf_op | source)
XLA Modules:
  0.0 112.0 jit_solution(6246610694368452322)
XLA Ops:
  0.7 2.3 %messages.1 = (f32[5,96,128]{2,1,0:T(8,128)}, f32[9,96,128]{2,1,0:T(8,128)}) custom-call(f32[8,96,128]{2,1,0:T(8,128)} %bitcast.124, f32[8,96,128]{2,1,0:T(8,128)} %bitcast.125, s32[8,96,128]{2,1,0:T(8,128)} %bitcast.129, s32[8,96,128]{2,1,0:T(8,128)} %bitcast.130, s32[8,96,128]{2,1,0:T(8,128)} %bitcast.137, s32[8,96,128]{2,1,0:T(8,128)} %bitcast.138, ...), custom_call_target="tpu_custom_call" | custom-call | tf_op jit(solution)/shard_map/messages/pallas_call | solution.py:415
  2.9 1.9 %collective-permute-start.36 = (f32[9,96,128]{2,1,0:T(8,128)}, f32[9,96,128]{2,1,0:T(8,128)S(1)}, u32[]{:S(2)}, u32[]{:S(2)}) collective-permute-start(f32[9,96,128]{2,1,0:T(8,128)} %get-tuple-element.254), channel_id=1, source_target_pairs={{4,0},{8,4},{12,8},{1,12},{5,1},{9,5},{13,9},{2,13},{6,2},{10,6},{... | collective-permute-start | bytes 1327112 | tf_op jit(solution)/shard_map/ppermute | solution.py:487
  4.9 3.4 %collective-permute-start.35 = (f32[5,96,128]{2,1,0:T(8,128)}, f32[5,96,128]{2,1,0:T(8,128)S(1)}, u32[]{:S(2)}, u32[]{:S(2)}) collective-permute-start(f32[5,96,128]{2,1,0:T(8,128)} %get-tuple-element.253), channel_id=1, source_target_pairs={{0,4},{4,8},{8,12},{12,1},{1,5},{5,9},{9,13},{13,2},{2,6},{6,10},{... | collective-permute-start | bytes 737288 | tf_op jit(solution)/shard_map/ppermute | solution.py:487
  8.3 4.0 %prepare.1 = (f32[6,8,128,128]{3,2,1,0:T(8,128)}, f32[5,8,2,128]{3,2,1,0:T(2,128)}, f32[5,2,2,128]{3,2,1,0:T(2,128)}, f32[5,2,2,128]{3,2,1,0:T(2,128)}) custom-call(s32[2]{0:T(128)S(1)} %pad_add_fusion.2.place, f32[8,96,128]{2,1,0:T(8,128)S(1)} %bitcast.127, s32[8,96,128]{2,1,0:T(8,128)S(1)} %bitcast.133, s32[8,96,128]{2,1,0:T(8,128)} %bitcast.139, ...), custom_call_target="tpu_custom_call" | custom-call | tf_op jit(solution)/shard_map/prepare/pallas_call | solution.py:435
  12.3 1.2 %collective-permute-start.37 = (f32[5,8,2,128]{3,2,1,0:T(2,128)}, f32[5,8,2,128]{3,2,1,0:T(2,128)S(1)}, u32[]{:S(2)}, u32[]{:S(2)}) collective-permute-start(f32[5,8,2,128]{3,2,1,0:T(2,128)} %get-tuple-element.255), channel_id=1, source_target_pairs={{0,16},{4,20},{8,24},{12,28},{1,17},{5,21},{9,25},{13,29},{2,18},{... | collective-permute-start | bytes 122888 | tf_op jit(solution)/shard_map/ppermute | solution.py:504
  13.5 3.2 %collective-permute-start.38 = (f32[5,2,2,128]{3,2,1,0:T(2,128)}, f32[5,2,2,128]{3,2,1,0:T(2,128)S(1)}, u32[]{:S(2)}, u32[]{:S(2)}) collective-permute-start(f32[5,2,2,128]{3,2,1,0:T(2,128)} %get-tuple-element.256), channel_id=1, source_target_pairs={{0,20},{4,24},{8,28},{12,17},{1,21},{5,25},{9,29},{13,18},{2,22},{... | collective-permute-start | bytes 30728 | tf_op jit(solution)/shard_map/ppermute | solution.py:504
  16.7 3.2 %collective-permute-start.39 = (f32[5,2,2,128]{3,2,1,0:T(2,128)}, f32[5,2,2,128]{3,2,1,0:T(2,128)S(1)}, u32[]{:S(2)}, u32[]{:S(2)}) collective-permute-start(f32[5,2,2,128]{3,2,1,0:T(2,128)} %get-tuple-element.257), channel_id=1, source_target_pairs={{4,16},{8,20},{12,24},{1,28},{5,17},{9,21},{13,25},{2,29},{6,18},{... | collective-permute-start | bytes 30728 | tf_op jit(solution)/shard_map/ppermute | solution.py:504
  19.9 1.5 %collective-permute-done.38.left_up.right_up = f32[5,2,2,128]{3,2,1,0:T(2,128)S(1)} collective-permute-done((f32[5,2,2,128]{3,2,1,0:T(2,128)}, f32[5,2,2,128]{3,2,1,0:T(2,128)S(1)}, u32[]{:S(2)}, u32[]{:S(2)}) %collective-permute-start.38) | collective-permute-done | bytes 10272 | tf_op jit(solution)/shard_map/ppermute | solution.py:504
  21.4 3.7 %collective-permute-done.39.left_down.right_down = f32[5,2,2,128]{3,2,1,0:T(2,128)S(1)} collective-permute-done((f32[5,2,2,128]{3,2,1,0:T(2,128)}, f32[5,2,2,128]{3,2,1,0:T(2,128)S(1)}, u32[]{:S(2)}, u32[]{:S(2)}) %collective-permute-start.39) | collective-permute-done | bytes 10272 | tf_op jit(solution)/shard_map/ppermute | solution.py:504
  25.9 19.1 %krylov.1 = (f32[3,8,128,128]{3,2,1,0:T(8,128)}, f32[3,8,128,128]{3,2,1,0:T(8,128)}, f32[3,8,128,128]{3,2,1,0:T(8,128)}, f32[8,128]{1,0:T(8,128)}, f32[3,8,24,128]{3,2,1,0:T(8,128)}) custom-call(s32[2]{0:T(128)S(1)} %pad_add_fusion.2.place, f32[128]{0:T(128)} %constant.89.clone.cover_z, f32[6,8,128,128]{3,2,1,0:T(8,128)} %get-tuple-element.252.fields, ...), custom_call_target="tpu_custom_call" | custom-call | tf_op jit(solution)/shard_map/krylov/pallas_call | solution.py:463
  45.2 1.5 %collective-permute-start.40 = (f32[8,128]{1,0:T(8,128)}, f32[8,128]{1,0:T(8,128)S(1)}, u32[]{:S(2)}, u32[]{:S(2)}) collective-permute-start(f32[8,128]{1,0:T(8,128)} %get-tuple-element.258), channel_id=1, source_target_pairs={{0,1},{1,0},{2,3},{3,2},{4,5},{5,4},{6,7},{7,6},{8,9},{9,8},{10,11... | collective-permute-start | bytes 12296 | tf_op jit(solution)/shard_map/ppermute | solution.py:517
  46.7 1.0 collective-permute-done.40
  48.4 1.6 %collective-permute-start.41 = (f32[8,128]{1,0:T(8,128)S(1)}, f32[8,128]{1,0:T(8,128)S(1)}, u32[]{:S(2)}, u32[]{:S(2)}) collective-permute-start(f32[8,128]{1,0:T(8,128)S(1)} %add.287), channel_id=1, source_target_pairs={{0,2},{1,3},{2,0},{3,1},{4,6},{5,7},{6,4},{7,5},{8,10},{9,11},{10,... | collective-permute-start | bytes 12296 | tf_op jit(solution)/shard_map/ppermute | solution.py:517
  50.0 1.3 %collective-permute-done.41 = f32[8,128]{1,0:T(8,128)S(1)} collective-permute-done((f32[8,128]{1,0:T(8,128)S(1)}, f32[8,128]{1,0:T(8,128)S(1)}, u32[]{:S(2)}, u32[]{:S(2)}) %collective-permute-start.41) | collective-permute-done | bytes 4128 | tf_op jit(solution)/shard_map/ppermute | solution.py:517
  51.6 2.5 %collective-permute-done.42 = f32[8,128]{1,0:T(8,128)S(1)} collective-permute-done((f32[8,128]{1,0:T(8,128)S(1)}, f32[8,128]{1,0:T(8,128)S(1)}, u32[]{:S(2)}, u32[]{:S(2)}) %collective-permute-start.42) | collective-permute-done | bytes 4128 | tf_op jit(solution)/shard_map/ppermute | solution.py:517
  54.1 4.1 %collective-permute-start.43 = (f32[8,128]{1,0:T(8,128)S(1)}, f32[8,128]{1,0:T(8,128)S(1)}, u32[]{:S(2)}, u32[]{:S(2)}) collective-permute-start(f32[8,128]{1,0:T(8,128)S(1)} %add.289), channel_id=1, source_target_pairs={{0,8},{4,12},{8,0},{12,4},{1,9},{5,13},{9,1},{13,5},{2,10},{6,14},... | collective-permute-start | bytes 12296 | tf_op jit(solution)/shard_map/ppermute | solution.py:517
  58.2 1.0 collective-permute-done.43
  59.4 2.4 %collective-permute-done.44 = f32[8,128]{1,0:T(8,128)S(1)} collective-permute-done((f32[8,128]{1,0:T(8,128)S(1)}, f32[8,128]{1,0:T(8,128)S(1)}, u32[]{:S(2)}, u32[]{:S(2)}) %collective-permute-start.44) | collective-permute-done | bytes 4128 | tf_op jit(solution)/shard_map/ppermute | solution.py:517
  62.4 0.7 copy-done.26
  63.1 4.7 %smooth.2 = (f32[8,96,128]{2,1,0:T(8,128)}, f32[96,128]{1,0:T(8,128)}, f32[96,128]{1,0:T(8,128)}, f32[8,128]{1,0:T(8,128)}) custom-call(s32[2]{0:T(128)S(1)} %pad_add_fusion.2.place, f32[8,128]{1,0:T(8,128)} %add.291.stats, f32[3,8,128,128]{3,2,1,0:T(8,128)} %get-tuple-element.259.basis, f32[3,8,24,128]{3,2,1,0:T(8,128)} %copy-done.26, ...), custom_call_target="tpu_custom_call" | custom-call | tf_op jit(solution)/shard_map/smooth/pallas_call | solution.py:641
  67.8 6.2 %collective-permute-start.46 = (f32[8,96,128]{2,1,0:T(8,128)}, f32[8,96,128]{2,1,0:T(8,128)}, u32[]{:S(2)}, u32[]{:S(2)}) collective-permute-start(f32[8,96,128]{2,1,0:T(8,128)} %get-tuple-element.262.rest_0_), channel_id=1, source_target_pairs={{0,12},{4,1},{8,5},{12,9},{1,13},{5,2},{9,6},{13,10},{2,14},{6,3},... | collective-permute-start | bytes 1179656 | tf_op jit(solution)/shard_map/ppermute | solution.py:487
  74.1 2.8 %collective-permute-start.47 = (f32[8,96,128]{2,1,0:T(8,128)}, f32[8,96,128]{2,1,0:T(8,128)}, u32[]{:S(2)}, u32[]{:S(2)}) collective-permute-start(f32[8,96,128]{2,1,0:T(8,128)} %get-tuple-element.262.rest_0_), channel_id=1, source_target_pairs={{12,0},{1,4},{5,8},{9,12},{13,1},{2,5},{6,9},{10,13},{14,2},{3,6},... | collective-permute-start | bytes 1179656 | tf_op jit(solution)/shard_map/ppermute | solution.py:487
  76.8 7.8 %collective-permute-start.51 = (f32[96,128]{1,0:T(8,128)}, f32[96,128]{1,0:T(8,128)S(1)}, u32[]{:S(2)}, u32[]{:S(2)}) collective-permute-start(f32[96,128]{1,0:T(8,128)} %get-tuple-element.264), channel_id=1, source_target_pairs={{8,0},{12,4},{1,8},{5,12},{9,1},{13,5},{2,9},{6,13},{10,2},{14,6},... | collective-permute-start | bytes 147464 | tf_op jit(solution)/shard_map/ppermute | solution.py:487
  84.6 1.9 %collective-permute-start.49 = (f32[96,128]{1,0:T(8,128)}, f32[96,128]{1,0:T(8,128)}, u32[]{:S(2)}, u32[]{:S(2)}) collective-permute-start(f32[96,128]{1,0:T(8,128)} %get-tuple-element.264), channel_id=1, source_target_pairs={{4,0},{8,4},{12,8},{1,12},{5,1},{9,5},{13,9},{2,13},{6,2},{10,6},{... | collective-permute-start | bytes 147464 | tf_op jit(solution)/shard_map/ppermute | solution.py:487
  86.6 3.4 %collective-permute-start.48 = (f32[96,128]{1,0:T(8,128)}, f32[96,128]{1,0:T(8,128)}, u32[]{:S(2)}, u32[]{:S(2)}) collective-permute-start(f32[96,128]{1,0:T(8,128)} %get-tuple-element.263), channel_id=1, source_target_pairs={{0,4},{4,8},{8,12},{12,1},{1,5},{5,9},{9,13},{13,2},{2,6},{6,10},{... | collective-permute-start | bytes 147464 | tf_op jit(solution)/shard_map/ppermute | solution.py:487
  89.9 5.9 %collective-permute-done.51 = f32[96,128]{1,0:T(8,128)S(1)} collective-permute-done((f32[96,128]{1,0:T(8,128)}, f32[96,128]{1,0:T(8,128)S(1)}, u32[]{:S(2)}, u32[]{:S(2)}) %collective-permute-start.51) | collective-permute-done | bytes 49184 | tf_op jit(solution)/shard_map/ppermute | solution.py:487
  95.8 3.6 %collective-permute-start.50 = (f32[96,128]{1,0:T(8,128)}, f32[96,128]{1,0:T(8,128)}, u32[]{:S(2)}, u32[]{:S(2)}) collective-permute-start(f32[96,128]{1,0:T(8,128)} %get-tuple-element.263), channel_id=1, source_target_pairs={{0,8},{4,12},{8,1},{12,5},{1,9},{5,13},{9,2},{13,6},{2,10},{6,14},... | collective-permute-start | bytes 147464 | tf_op jit(solution)/shard_map/ppermute | solution.py:487
  99.5 2.1 %copy.82 = f32[3,1,8,96,128]{4,0,3,2,1:T(4,128)S(1)} copy(f32[3,1,8,96,128]{4,3,2,1,0:T(8,128)} %param.23) | data formatting | bytes 2359296
  102.0 1.2 %copy.81 = s32[1,8,96,128]{2,3,1,0:T(8,128)S(1)} copy(s32[1,8,96,128]{3,2,1,0:T(8,128)} %param.22) | data formatting | bytes 786432
  103.2 1.2 %slice.457 = f32[1,1]{1,0:T(1,128)} slice(f32[8,128]{1,0:T(8,128)} %get-tuple-element.261.factors), slice={[3:4], [0:1]} | slice | bytes 8 | tf_op jit(solution)/shard_map/slice | solution.py:833
  104.4 3.9 %displacement.1 = f32[3,8,96,128]{3,2,1,0:T(8,128)} custom-call(f32[8,128]{1,0:T(8,128)} %get-tuple-element.261.factors, f32[3,8,128,128]{3,2,1,0:T(8,128)} %get-tuple-element.265.first, f32[3,8,128,128]{3,2,1,0:T(8,128)} %get-tuple-element.266.second), custom_call_target="tpu_custom_call" | custom-call | tf_op jit(solution)/shard_map/displacement/pallas_call | solution.py:697
  109.0 3.0 %finish.2 = f32[8,96,128]{2,1,0:T(8,128)} custom-call(f32[8,128]{1,0:T(8,128)} %get-tuple-element.261.factors, f32[8,96,128]{2,1,0:T(8,128)S(1)} %bitcast.128, s32[8,96,128]{2,1,0:T(8,128)} %bitcast.131, f32[8,96,128]{2,1,0:T(8,128)} %get-tuple-element.262.rest_0_, f32[8,96,128]{2,1,0:T(8,128)} %collective-permute-done.46.rest_1_, ...), custom_call_target="tpu_custom_call" | custom-call | tf_op jit(solution)/shard_map/finish/pallas_call | solution.py:676
  (40 shorter events, 3.4 us)
Async XLA Ops:
  0.6 7.7 %copy-start.20 = (f32[1,8,96,128]{3,2,1,0:T(8,128)S(1)}, f32[1,8,96,128]{3,2,1,0:T(8,128)}, u32[]{:S(2)}) copy-start(f32[1,8,96,128]{3,2,1,0:T(8,128)} %param.20) | copy-start | bytes 1179652
  0.6 7.7 %copy-start.22 = (s32[1,8,96,128]{3,2,1,0:T(8,128)S(1)}, s32[1,8,96,128]{3,2,1,0:T(8,128)}, u32[]{:S(2)}) copy-start(s32[1,8,96,128]{3,2,1,0:T(8,128)} %param.21) | copy-start | bytes 1179652
  2.9 22.1 %collective-permute-start.36 = (f32[9,96,128]{2,1,0:T(8,128)}, f32[9,96,128]{2,1,0:T(8,128)S(1)}, u32[]{:S(2)}, u32[]{:S(2)}) collective-permute-start(f32[9,96,128]{2,1,0:T(8,128)} %get-tuple-element.254), channel_id=1, source_target_pairs={{4,0},{8,4},{12,8},{1,12},{5,1},{9,5},{13,9},{2,13},{6,2},{10,6},{... | collective-permute-start | bytes 1327112 | tf_op jit(solution)/shard_map/ppermute | solution.py:487
  4.9 20.2 %collective-permute-start.35 = (f32[5,96,128]{2,1,0:T(8,128)}, f32[5,96,128]{2,1,0:T(8,128)S(1)}, u32[]{:S(2)}, u32[]{:S(2)}) collective-permute-start(f32[5,96,128]{2,1,0:T(8,128)} %get-tuple-element.253), channel_id=1, source_target_pairs={{0,4},{4,8},{8,12},{12,1},{1,5},{5,9},{9,13},{13,2},{2,6},{6,10},{... | collective-permute-start | bytes 737288 | tf_op jit(solution)/shard_map/ppermute | solution.py:487
  8.3 54.1 %copy-start.33 = (s32[2]{0:T(128)}, s32[2]{0:T(128)S(1)}, u32[]{:S(2)}) copy-start(s32[2]{0:T(128)S(1)} %pad_add_fusion.2.place) | copy-start | bytes 28
  12.3 12.8 %collective-permute-start.37 = (f32[5,8,2,128]{3,2,1,0:T(2,128)}, f32[5,8,2,128]{3,2,1,0:T(2,128)S(1)}, u32[]{:S(2)}, u32[]{:S(2)}) collective-permute-start(f32[5,8,2,128]{3,2,1,0:T(2,128)} %get-tuple-element.255), channel_id=1, source_target_pairs={{0,16},{4,20},{8,24},{12,28},{1,17},{5,21},{9,25},{13,29},{2,18},{... | collective-permute-start | bytes 122888 | tf_op jit(solution)/shard_map/ppermute | solution.py:504
  13.5 7.9 %collective-permute-start.38 = (f32[5,2,2,128]{3,2,1,0:T(2,128)}, f32[5,2,2,128]{3,2,1,0:T(2,128)S(1)}, u32[]{:S(2)}, u32[]{:S(2)}) collective-permute-start(f32[5,2,2,128]{3,2,1,0:T(2,128)} %get-tuple-element.256), channel_id=1, source_target_pairs={{0,20},{4,24},{8,28},{12,17},{1,21},{5,25},{9,29},{13,18},{2,22},{... | collective-permute-start | bytes 30728 | tf_op jit(solution)/shard_map/ppermute | solution.py:504
  16.7 8.4 %collective-permute-start.39 = (f32[5,2,2,128]{3,2,1,0:T(2,128)}, f32[5,2,2,128]{3,2,1,0:T(2,128)S(1)}, u32[]{:S(2)}, u32[]{:S(2)}) collective-permute-start(f32[5,2,2,128]{3,2,1,0:T(2,128)} %get-tuple-element.257), channel_id=1, source_target_pairs={{4,16},{8,20},{12,24},{1,28},{5,17},{9,21},{13,25},{2,29},{6,18},{... | collective-permute-start | bytes 30728 | tf_op jit(solution)/shard_map/ppermute | solution.py:504
  21.4 3.7 %copy-start.31 = (f32[5,2,2,128]{3,2,1,0:T(2,128)}, f32[5,2,2,128]{3,2,1,0:T(2,128)S(1)}, u32[]{:S(2)}) copy-start(f32[5,2,2,128]{3,2,1,0:T(2,128)S(1)} %collective-permute-done.38.left_up.right_up) | copy-start | bytes 30724
  25.0 0.6 copy-start.32
  25.0 0.6 copy-start.29
  25.1 0.7 copy-start.28
  25.1 0.8 copy-start.27
  45.0 17.4 %collective-permute-start.45 = (f32[3,8,24,128]{3,2,1,0:T(8,128)}, f32[3,8,24,128]{3,2,1,0:T(8,128)S(1)}, u32[]{:S(2)}, u32[]{:S(2)}) collective-permute-start(f32[3,8,24,128]{3,2,1,0:T(8,128)} %get-tuple-element.260), channel_id=1, source_target_pairs={{0,16},{4,20},{8,24},{12,28},{1,17},{5,21},{9,25},{13,29},{2,18},{... | collective-permute-start | bytes 884744 | tf_op jit(solution)/shard_map/ppermute | solution.py:504
  45.2 2.5 %collective-permute-start.40 = (f32[8,128]{1,0:T(8,128)}, f32[8,128]{1,0:T(8,128)S(1)}, u32[]{:S(2)}, u32[]{:S(2)}) collective-permute-start(f32[8,128]{1,0:T(8,128)} %get-tuple-element.258), channel_id=1, source_target_pairs={{0,1},{1,0},{2,3},{3,2},{4,5},{5,4},{6,7},{7,6},{8,9},{9,8},{10,11... | collective-permute-start | bytes 12296 | tf_op jit(solution)/shard_map/ppermute | solution.py:517
  48.4 2.9 %collective-permute-start.41 = (f32[8,128]{1,0:T(8,128)S(1)}, f32[8,128]{1,0:T(8,128)S(1)}, u32[]{:S(2)}, u32[]{:S(2)}) collective-permute-start(f32[8,128]{1,0:T(8,128)S(1)} %add.287), channel_id=1, source_target_pairs={{0,2},{1,3},{2,0},{3,1},{4,6},{5,7},{6,4},{7,5},{8,10},{9,11},{10,... | collective-permute-start | bytes 12296 | tf_op jit(solution)/shard_map/ppermute | solution.py:517
  51.3 2.8 %collective-permute-start.42 = (f32[8,128]{1,0:T(8,128)S(1)}, f32[8,128]{1,0:T(8,128)S(1)}, u32[]{:S(2)}, u32[]{:S(2)}) collective-permute-start(f32[8,128]{1,0:T(8,128)S(1)} %add.288), channel_id=1, source_target_pairs={{0,4},{4,0},{8,12},{12,8},{1,5},{5,1},{9,13},{13,9},{2,6},{6,2},{1... | collective-permute-start | bytes 12296 | tf_op jit(solution)/shard_map/ppermute | solution.py:517
  54.1 5.1 %collective-permute-start.43 = (f32[8,128]{1,0:T(8,128)S(1)}, f32[8,128]{1,0:T(8,128)S(1)}, u32[]{:S(2)}, u32[]{:S(2)}) collective-permute-start(f32[8,128]{1,0:T(8,128)S(1)} %add.289), channel_id=1, source_target_pairs={{0,8},{4,12},{8,0},{12,4},{1,9},{5,13},{9,1},{13,5},{2,10},{6,14},... | collective-permute-start | bytes 12296 | tf_op jit(solution)/shard_map/ppermute | solution.py:517
  59.2 2.6 %collective-permute-start.44 = (f32[8,128]{1,0:T(8,128)S(1)}, f32[8,128]{1,0:T(8,128)S(1)}, u32[]{:S(2)}, u32[]{:S(2)}) collective-permute-start(f32[8,128]{1,0:T(8,128)S(1)} %add.290), channel_id=1, source_target_pairs={{0,16},{16,0},{1,17},{17,1},{2,18},{18,2},{3,19},{19,3},{4,20},{20... | collective-permute-start | bytes 12296 | tf_op jit(solution)/shard_map/ppermute | solution.py:517
  62.4 0.7 copy-start.26
  67.8 41.2 %collective-permute-start.46 = (f32[8,96,128]{2,1,0:T(8,128)}, f32[8,96,128]{2,1,0:T(8,128)}, u32[]{:S(2)}, u32[]{:S(2)}) collective-permute-start(f32[8,96,128]{2,1,0:T(8,128)} %get-tuple-element.262.rest_0_), channel_id=1, source_target_pairs={{0,12},{4,1},{8,5},{12,9},{1,13},{5,2},{9,6},{13,10},{2,14},{6,3},... | collective-permute-start | bytes 1179656 | tf_op jit(solution)/shard_map/ppermute | solution.py:487
  74.1 35.0 %collective-permute-start.47 = (f32[8,96,128]{2,1,0:T(8,128)}, f32[8,96,128]{2,1,0:T(8,128)}, u32[]{:S(2)}, u32[]{:S(2)}) collective-permute-start(f32[8,96,128]{2,1,0:T(8,128)} %get-tuple-element.262.rest_0_), channel_id=1, source_target_pairs={{12,0},{1,4},{5,8},{9,12},{13,1},{2,5},{6,9},{10,13},{14,2},{3,6},... | collective-permute-start | bytes 1179656 | tf_op jit(solution)/shard_map/ppermute | solution.py:487
  76.8 19.0 %collective-permute-start.51 = (f32[96,128]{1,0:T(8,128)}, f32[96,128]{1,0:T(8,128)S(1)}, u32[]{:S(2)}, u32[]{:S(2)}) collective-permute-start(f32[96,128]{1,0:T(8,128)} %get-tuple-element.264), channel_id=1, source_target_pairs={{8,0},{12,4},{1,8},{5,12},{9,1},{13,5},{2,9},{6,13},{10,2},{14,6},... | collective-permute-start | bytes 147464 | tf_op jit(solution)/shard_map/ppermute | solution.py:487
  84.6 24.3 %collective-permute-start.49 = (f32[96,128]{1,0:T(8,128)}, f32[96,128]{1,0:T(8,128)}, u32[]{:S(2)}, u32[]{:S(2)}) collective-permute-start(f32[96,128]{1,0:T(8,128)} %get-tuple-element.264), channel_id=1, source_target_pairs={{4,0},{8,4},{12,8},{1,12},{5,1},{9,5},{13,9},{2,13},{6,2},{10,6},{... | collective-permute-start | bytes 147464 | tf_op jit(solution)/shard_map/ppermute | solution.py:487
  86.6 22.4 %collective-permute-start.48 = (f32[96,128]{1,0:T(8,128)}, f32[96,128]{1,0:T(8,128)}, u32[]{:S(2)}, u32[]{:S(2)}) collective-permute-start(f32[96,128]{1,0:T(8,128)} %get-tuple-element.263), channel_id=1, source_target_pairs={{0,4},{4,8},{8,12},{12,1},{1,5},{5,9},{9,13},{13,2},{2,6},{6,10},{... | collective-permute-start | bytes 147464 | tf_op jit(solution)/shard_map/ppermute | solution.py:487
  95.8 5.7 %copy-start.30 = (f32[96,128]{1,0:T(8,128)}, f32[96,128]{1,0:T(8,128)S(1)}, u32[]{:S(2)}) copy-start(f32[96,128]{1,0:T(8,128)S(1)} %collective-permute-done.51) | copy-start | bytes 147460
  95.8 13.2 %collective-permute-start.50 = (f32[96,128]{1,0:T(8,128)}, f32[96,128]{1,0:T(8,128)}, u32[]{:S(2)}, u32[]{:S(2)}) collective-permute-start(f32[96,128]{1,0:T(8,128)} %get-tuple-element.263), channel_id=1, source_target_pairs={{0,8},{4,12},{8,1},{12,5},{1,9},{5,13},{9,2},{13,6},{2,10},{6,14},... | collective-permute-start | bytes 147464 | tf_op jit(solution)/shard_map/ppermute | solution.py:487

commit v6 on v5

--- a/solution.py
+++ b/solution.py
@@ -598,7 +598,7 @@
 
 
 def smooth_kernel(
-    plain, cells, nx, place, stats, basis, left, right, along_x, along_y, planar, low, high, factors
+    plain, cells, nx, place, stats, basis, left, right, along_x, along_y, planar, low, high, factors, verdict
 ):
     on_left = jnp.where(place[0] > 0, 1.0, 0.0)
     on_right = jnp.where(place[0] < nx - 1, 1.0, 0.0)
@@ -616,6 +616,7 @@
     for i, value in enumerate((by_first, by_second, scale, sound)):
         factors[pl.ds(i, 1)] = jnp.broadcast_to(value, (1, LANES))
     factors[pl.ds(4, 4)] = jnp.zeros((4, LANES), jnp.float32)
+    verdict[...] = sound
     for z in range(depth):
         wide = jnp.concatenate(
             [
@@ -637,11 +638,11 @@
     along_x = banded(width + 2 * RAD, width, RAD).T
     along_y = np.zeros((height, LANES), np.float32)
     along_y[:, :height] = banded(height, height, 0).T
-    shapes = ((depth, height, width), (height, width), (height, width), (8, LANES))
+    shapes = ((depth, height, width), (height, width), (height, width), (8, LANES), (1, 1))
     return pl.pallas_call(
         functools.partial(smooth_kernel, plain, float(cells), lax.axis_size("gx")),
         in_specs=[SCALAR] + [VECTOR] * 6,
-        out_specs=[VECTOR] * 4,
+        out_specs=[VECTOR] * 5,
         out_shape=[jax.ShapeDtypeStruct(s, jnp.float32) for s in shapes],
         name="smooth",
     )(place, stats, basis, *sides, jnp.asarray(along_x), jnp.asarray(along_y))
@@ -750,14 +751,12 @@
     return fold_upper(total[:, :, :height])
 
 
-def plain_path(table, density, bone, fixed, load):
+def plain_path(table, fields, height):
+    modulus, *force, free, density = jnp.swapaxes(fields[..., :height], 2, 3)
     _, height, _ = density.shape
-    share = bone.astype(jnp.float32)
-    free = 1.0 - fixed.astype(jnp.float32)
-    modulus = share * density * density + (1.0 - share) * MARROW
     spread = sum(spread_corner(modulus[None], corner) for corner in corners())
     precondition = free / (float(table[0, 0]) * fold_upper(spread[:, :, :height]))
-    residual = free * load
+    residual = jnp.stack(force)
     search = precondition * residual
     start = (jnp.zeros_like(residual), residual, search, inner_sum(residual * search))
 
@@ -784,9 +783,9 @@
 
 
 def remodelled(plain, cells, place, density, bone, stats, basis, sides):
-    planar, low, high, factors = run_smooth(plain, cells, place, stats, basis, sides, density.shape[1])
+    planar, low, high, factors, verdict = run_smooth(plain, cells, place, stats, basis, sides, density.shape[1])
     pieces, blocks = depth_pieces(planar, low, high)
-    return run_finish(factors, density, bone, pieces, blocks), factors
+    return run_finish(factors, density, bone, pieces, blocks), factors, verdict
 
 
 def on_device(density, bone, fixed, load):
@@ -809,14 +808,14 @@
     )
     sides = edges_moved(ends, 0)
     stats = total_over_mesh(stats)
-    updated, factors = remodelled(False, cells, place, density, bone, stats, basis, sides)
+    updated, factors, verdict = remodelled(False, cells, place, density, bone, stats, basis, sides)
     moved = run_displacement(factors, first, second, height)
 
-    kept = [v.reshape(-1, width) for v in (density, bone, fixed, load)]
+    shares = bone.reshape(-1, width)
 
     def repeated(state):
-        again = [v.reshape((-1, depth, height, width)) for v in kept]
-        specific, moved = plain_path(table, *(v[0] for v in again[:3]), again[3])
+        specific, moved = plain_path(table, fields, height)
+        thick = jnp.swapaxes(fields[5, ..., :height], 1, 2)
         cover = lambda length, start, count: lax.dynamic_slice(
             jnp.asarray(coverage(length)), (start,), (count,)
         )
@@ -827,10 +826,12 @@
         row, lane = (lax.broadcasted_iota(jnp.int32, (8, LANES), i) for i in range(2))
         tile = jnp.where((row == 4) & (lane == 0), total, 0.0)
         again = specific[None]
-        updated = remodelled(True, cells, place, density, bone, tile, again, side_halos(again))[0]
+        updated = remodelled(
+            True, cells, place, thick, shares.reshape(bone.shape), tile, again, side_halos(again)
+        )[0]
         return True, updated, moved.reshape(-1, width)
 
-    sound = factors[3, 0] > 0.5
+    sound = verdict.reshape(()) > 0.5
     _, updated, moved = lax.while_loop(lambda state: ~state[0], repeated, (sound, updated, moved.reshape(-1, width)))
     return updated[None], moved.reshape(3, 1, depth, height, width)
 

time: 113 us -> 110 us (0.973)
  local copies, waits for them, and re-layouts: 6.42 us -> 3.86 us
    unnamed x24 -> x17, local copies, waits for them, and re-layouts: 5.23 us -> 3.86 us
    slice x1 -> x0, local copies, waits for them, and re-layouts: 1.19 us -> none  [on_device(): sound = factors[3, 0] > 0.5]
  transfers between devices with their start and end apart: 17 -> 17, of which waited for: 8 -> 8; matrix products, arithmetic and copies ran while one was open for 6% -> 3% of each run, Pallas kernels for 7% -> 7%
where the time goes in v6:
time: 110 us
  starting transfers between devices  46.6 us (42%)
  Pallas kernels  37.1 us (34%)
  waiting for transfers between devices  19.3 us (18%)
  local copies, waits for them, and re-layouts  3.86 us (4%)
  other arithmetic  1.36 us (1%)
  between operations  1.36 us (1%)
    ppermute x8, starting transfers between devices, to_slab(): return lax.ppermute(value, ('gx', 'gy', 'gz'), slab_route(steps, sideways))  31 us
    pallas_call x1, Pallas kernels, run_krylov(): pl.pallas_call(functools.partial(krylov_kernel, mode_constants(table), fl...  19.2 us
    ppermute x5, waiting for transfers between devices, total_over_mesh(): other = lax.ppermute(value, axis, [(i, i ^ step) for i in range(count)])  8.16 us
    ppermute x4, starting transfers between devices, edges_moved(): got = lax.ppermute(sent[0], ('gx', 'gy', 'gz'), spots)  7.85 us
    ppermute x5, starting transfers between devices, total_over_mesh(): other = lax.ppermute(value, axis, [(i, i ^ step) for i in range(count)])  7.73 us
    ppermute x8, waiting for transfers between devices, to_slab(): return lax.ppermute(value, ('gx', 'gy', 'gz'), slab_route(steps, sideways))  6 us
    ppermute x4, waiting for transfers between devices, edges_moved(): got = lax.ppermute(sent[0], ('gx', 'gy', 'gz'), spots)  5.15 us
    pallas_call x1, Pallas kernels, run_smooth(): pl.pallas_call(functools.partial(smooth_kernel, plain, float(cells), lax....  4.62 us
  transfers between devices with their start and end apart: 17, of which 8 were waited for; matrix products, arithmetic and copies ran while one was open for 3% of the time, Pallas kernels for 7%

profile of v6, /device:TPU:9, one launch (start us, length us, event | category | flops | bytes accessed | tf_op | source)
XLA Modules:
  0.0 109.6 jit_solution(13530652337496777557)
XLA Ops:
  0.6 2.3 %messages.1 = (f32[5,96,128]{2,1,0:T(8,128)}, f32[9,96,128]{2,1,0:T(8,128)}) custom-call(f32[8,96,128]{2,1,0:T(8,128)} %bitcast.131, f32[8,96,128]{2,1,0:T(8,128)} %bitcast.132, s32[8,96,128]{2,1,0:T(8,128)} %bitcast.123, s32[8,96,128]{2,1,0:T(8,128)} %bitcast.124, s32[8,96,128]{2,1,0:T(8,128)} %bitcast.135, s32[8,96,128]{2,1,0:T(8,128)} %bitcast.136, ...), custom_call_target="tpu_custom_call" | custom-call | tf_op jit(solution)/shard_map/messages/pallas_call | solution.py:415
  2.9 1.9 %collective-permute-start.36 = (f32[9,96,128]{2,1,0:T(8,128)}, f32[9,96,128]{2,1,0:T(8,128)S(1)}, u32[]{:S(2)}, u32[]{:S(2)}) collective-permute-start(f32[9,96,128]{2,1,0:T(8,128)} %get-tuple-element.235), channel_id=1, source_target_pairs={{4,0},{8,4},{12,8},{1,12},{5,1},{9,5},{13,9},{2,13},{6,2},{10,6},{... | collective-permute-start | bytes 1327112 | tf_op jit(solution)/shard_map/ppermute | solution.py:487
  4.8 3.4 %collective-permute-start.35 = (f32[5,96,128]{2,1,0:T(8,128)}, f32[5,96,128]{2,1,0:T(8,128)S(1)}, u32[]{:S(2)}, u32[]{:S(2)}) collective-permute-start(f32[5,96,128]{2,1,0:T(8,128)} %get-tuple-element.234), channel_id=1, source_target_pairs={{0,4},{4,8},{8,12},{12,1},{1,5},{5,9},{9,13},{13,2},{2,6},{6,10},{... | collective-permute-start | bytes 737288 | tf_op jit(solution)/shard_map/ppermute | solution.py:487
  8.3 4.1 %prepare.1 = (f32[6,8,128,128]{3,2,1,0:T(8,128)}, f32[5,8,2,128]{3,2,1,0:T(2,128)}, f32[5,2,2,128]{3,2,1,0:T(2,128)}, f32[5,2,2,128]{3,2,1,0:T(2,128)}) custom-call(s32[2]{0:T(128)S(1)} %pad_add_fusion.2.place, f32[8,96,128]{2,1,0:T(8,128)} %bitcast.133, s32[8,96,128]{2,1,0:T(8,128)S(1)} %bitcast.125, s32[8,96,128]{2,1,0:T(8,128)} %bitcast.137, ...), custom_call_target="tpu_custom_call" | custom-call | tf_op jit(solution)/shard_map/prepare/pallas_call | solution.py:435
  12.4 1.2 %collective-permute-start.37 = (f32[5,8,2,128]{3,2,1,0:T(2,128)}, f32[5,8,2,128]{3,2,1,0:T(2,128)S(1)}, u32[]{:S(2)}, u32[]{:S(2)}) collective-permute-start(f32[5,8,2,128]{3,2,1,0:T(2,128)} %get-tuple-element.236), channel_id=1, source_target_pairs={{0,16},{4,20},{8,24},{12,28},{1,17},{5,21},{9,25},{13,29},{2,18},{... | collective-permute-start | bytes 122888 | tf_op jit(solution)/shard_map/ppermute | solution.py:504
  13.6 3.2 %collective-permute-start.38 = (f32[5,2,2,128]{3,2,1,0:T(2,128)}, f32[5,2,2,128]{3,2,1,0:T(2,128)S(1)}, u32[]{:S(2)}, u32[]{:S(2)}) collective-permute-start(f32[5,2,2,128]{3,2,1,0:T(2,128)} %get-tuple-element.237), channel_id=1, source_target_pairs={{0,20},{4,24},{8,28},{12,17},{1,21},{5,25},{9,29},{13,18},{2,22},{... | collective-permute-start | bytes 30728 | tf_op jit(solution)/shard_map/ppermute | solution.py:504
  16.7 3.2 %collective-permute-start.39 = (f32[5,2,2,128]{3,2,1,0:T(2,128)}, f32[5,2,2,128]{3,2,1,0:T(2,128)S(1)}, u32[]{:S(2)}, u32[]{:S(2)}) collective-permute-start(f32[5,2,2,128]{3,2,1,0:T(2,128)} %get-tuple-element.238), channel_id=1, source_target_pairs={{4,16},{8,20},{12,24},{1,28},{5,17},{9,21},{13,25},{2,29},{6,18},{... | collective-permute-start | bytes 30728 | tf_op jit(solution)/shard_map/ppermute | solution.py:504
  20.0 1.5 %collective-permute-done.38.left_up.right_up = f32[5,2,2,128]{3,2,1,0:T(2,128)S(1)} collective-permute-done((f32[5,2,2,128]{3,2,1,0:T(2,128)}, f32[5,2,2,128]{3,2,1,0:T(2,128)S(1)}, u32[]{:S(2)}, u32[]{:S(2)}) %collective-permute-start.38) | collective-permute-done | bytes 10272 | tf_op jit(solution)/shard_map/ppermute | solution.py:504
  21.4 3.7 %collective-permute-done.39.left_down.right_down = f32[5,2,2,128]{3,2,1,0:T(2,128)S(1)} collective-permute-done((f32[5,2,2,128]{3,2,1,0:T(2,128)}, f32[5,2,2,128]{3,2,1,0:T(2,128)S(1)}, u32[]{:S(2)}, u32[]{:S(2)}) %collective-permute-start.39) | collective-permute-done | bytes 10272 | tf_op jit(solution)/shard_map/ppermute | solution.py:504
  25.1 0.7 copy-done.26
  25.8 0.8 copy-done.25
  26.6 19.2 %krylov.1 = (f32[3,8,128,128]{3,2,1,0:T(8,128)}, f32[3,8,128,128]{3,2,1,0:T(8,128)}, f32[3,8,128,128]{3,2,1,0:T(8,128)}, f32[8,128]{1,0:T(8,128)}, f32[3,8,24,128]{3,2,1,0:T(8,128)}) custom-call(s32[2]{0:T(128)S(1)} %pad_add_fusion.2.place, f32[128]{0:T(128)} %constant.85.clone.cover_z, f32[6,8,128,128]{3,2,1,0:T(8,128)} %get-tuple-element.425.fields, ...), custom_call_target="tpu_custom_call" | custom-call | tf_op jit(solution)/shard_map/krylov/pallas_call | solution.py:463
  46.1 1.5 %collective-permute-start.40 = (f32[8,128]{1,0:T(8,128)}, f32[8,128]{1,0:T(8,128)S(1)}, u32[]{:S(2)}, u32[]{:S(2)}) collective-permute-start(f32[8,128]{1,0:T(8,128)} %get-tuple-element.239), channel_id=1, source_target_pairs={{0,1},{1,0},{2,3},{3,2},{4,5},{5,4},{6,7},{7,6},{8,9},{9,8},{10,11... | collective-permute-start | bytes 12296 | tf_op jit(solution)/shard_map/ppermute | solution.py:517
  47.6 1.0 collective-permute-done.40
  48.6 0.7 add.275
  49.3 1.5 %collective-permute-start.41 = (f32[8,128]{1,0:T(8,128)S(1)}, f32[8,128]{1,0:T(8,128)S(1)}, u32[]{:S(2)}, u32[]{:S(2)}) collective-permute-start(f32[8,128]{1,0:T(8,128)S(1)} %add.275), channel_id=1, source_target_pairs={{0,2},{1,3},{2,0},{3,1},{4,6},{5,7},{6,4},{7,5},{8,10},{9,11},{10,... | collective-permute-start | bytes 12296 | tf_op jit(solution)/shard_map/ppermute | solution.py:517
  50.7 1.4 %collective-permute-done.41 = f32[8,128]{1,0:T(8,128)S(1)} collective-permute-done((f32[8,128]{1,0:T(8,128)S(1)}, f32[8,128]{1,0:T(8,128)S(1)}, u32[]{:S(2)}, u32[]{:S(2)}) %collective-permute-start.41) | collective-permute-done | bytes 4128 | tf_op jit(solution)/shard_map/ppermute | solution.py:517
  52.6 2.5 %collective-permute-done.42 = f32[8,128]{1,0:T(8,128)S(1)} collective-permute-done((f32[8,128]{1,0:T(8,128)S(1)}, f32[8,128]{1,0:T(8,128)S(1)}, u32[]{:S(2)}, u32[]{:S(2)}) %collective-permute-start.42) | collective-permute-done | bytes 4128 | tf_op jit(solution)/shard_map/ppermute | solution.py:517
  55.0 4.1 %collective-permute-start.43 = (f32[8,128]{1,0:T(8,128)S(1)}, f32[8,128]{1,0:T(8,128)S(1)}, u32[]{:S(2)}, u32[]{:S(2)}) collective-permute-start(f32[8,128]{1,0:T(8,128)S(1)} %add.277), channel_id=1, source_target_pairs={{0,8},{4,12},{8,0},{12,4},{1,9},{5,13},{9,1},{13,5},{2,10},{6,14},... | collective-permute-start | bytes 12296 | tf_op jit(solution)/shard_map/ppermute | solution.py:517
  59.1 1.0 collective-permute-done.43
  60.4 2.3 %collective-permute-done.44 = f32[8,128]{1,0:T(8,128)S(1)} collective-permute-done((f32[8,128]{1,0:T(8,128)S(1)}, f32[8,128]{1,0:T(8,128)S(1)}, u32[]{:S(2)}, u32[]{:S(2)}) %collective-permute-start.44) | collective-permute-done | bytes 4128 | tf_op jit(solution)/shard_map/ppermute | solution.py:517
  63.3 4.6 %smooth.2 = (f32[8,96,128]{2,1,0:T(8,128)}, f32[96,128]{1,0:T(8,128)}, f32[96,128]{1,0:T(8,128)}, f32[8,128]{1,0:T(8,128)}, f32[1,1]{1,0:T(1,128)}) custom-call(s32[2]{0:T(128)S(1)} %pad_add_fusion.2.place, f32[8,128]{1,0:T(8,128)} %add.279.stats, f32[3,8,128,128]{3,2,1,0:T(8,128)} %get-tuple-element.240.basis, ...), custom_call_target="tpu_custom_call" | custom-call | tf_op jit(solution)/shard_map/smooth/pallas_call | solution.py:642
  67.9 6.2 %collective-permute-start.46 = (f32[8,96,128]{2,1,0:T(8,128)}, f32[8,96,128]{2,1,0:T(8,128)}, u32[]{:S(2)}, u32[]{:S(2)}) collective-permute-start(f32[8,96,128]{2,1,0:T(8,128)} %get-tuple-element.244.rest_0_), channel_id=1, source_target_pairs={{0,12},{4,1},{8,5},{12,9},{1,13},{5,2},{9,6},{13,10},{2,14},{6,3},... | collective-permute-start | bytes 1179656 | tf_op jit(solution)/shard_map/ppermute | solution.py:487
  74.1 2.8 %collective-permute-start.47 = (f32[8,96,128]{2,1,0:T(8,128)}, f32[8,96,128]{2,1,0:T(8,128)}, u32[]{:S(2)}, u32[]{:S(2)}) collective-permute-start(f32[8,96,128]{2,1,0:T(8,128)} %get-tuple-element.244.rest_0_), channel_id=1, source_target_pairs={{12,0},{1,4},{5,8},{9,12},{13,1},{2,5},{6,9},{10,13},{14,2},{3,6},... | collective-permute-start | bytes 1179656 | tf_op jit(solution)/shard_map/ppermute | solution.py:487
  76.9 7.8 %collective-permute-start.51 = (f32[96,128]{1,0:T(8,128)}, f32[96,128]{1,0:T(8,128)}, u32[]{:S(2)}, u32[]{:S(2)}) collective-permute-start(f32[96,128]{1,0:T(8,128)} %get-tuple-element.246), channel_id=1, source_target_pairs={{8,0},{12,4},{1,8},{5,12},{9,1},{13,5},{2,9},{6,13},{10,2},{14,6},... | collective-permute-start | bytes 147464 | tf_op jit(solution)/shard_map/ppermute | solution.py:487
  84.7 1.9 %collective-permute-start.49 = (f32[96,128]{1,0:T(8,128)}, f32[96,128]{1,0:T(8,128)}, u32[]{:S(2)}, u32[]{:S(2)}) collective-permute-start(f32[96,128]{1,0:T(8,128)} %get-tuple-element.246), channel_id=1, source_target_pairs={{4,0},{8,4},{12,8},{1,12},{5,1},{9,5},{13,9},{2,13},{6,2},{10,6},{... | collective-permute-start | bytes 147464 | tf_op jit(solution)/shard_map/ppermute | solution.py:487
  86.6 3.4 %collective-permute-start.48 = (f32[96,128]{1,0:T(8,128)}, f32[96,128]{1,0:T(8,128)}, u32[]{:S(2)}, u32[]{:S(2)}) collective-permute-start(f32[96,128]{1,0:T(8,128)} %get-tuple-element.245), channel_id=1, source_target_pairs={{0,4},{4,8},{8,12},{12,1},{1,5},{5,9},{9,13},{13,2},{2,6},{6,10},{... | collective-permute-start | bytes 147464 | tf_op jit(solution)/shard_map/ppermute | solution.py:487
  90.0 6.0 %collective-permute-done.51 = f32[96,128]{1,0:T(8,128)} collective-permute-done((f32[96,128]{1,0:T(8,128)}, f32[96,128]{1,0:T(8,128)}, u32[]{:S(2)}, u32[]{:S(2)}) %collective-permute-start.51) | collective-permute-done | bytes 49184 | tf_op jit(solution)/shard_map/ppermute | solution.py:487
  96.0 3.6 %collective-permute-start.50 = (f32[96,128]{1,0:T(8,128)}, f32[96,128]{1,0:T(8,128)}, u32[]{:S(2)}, u32[]{:S(2)}) collective-permute-start(f32[96,128]{1,0:T(8,128)} %get-tuple-element.245), channel_id=1, source_target_pairs={{0,8},{4,12},{8,1},{12,5},{1,9},{5,13},{9,2},{13,6},{2,10},{6,14},... | collective-permute-start | bytes 147464 | tf_op jit(solution)/shard_map/ppermute | solution.py:487
  99.7 2.4 %copy.67 = f32[6,8,128,128]{2,3,1,0:T(8,128)} copy(f32[6,8,128,128]{3,2,1,0:T(8,128)S(1)} %copy-done.16) | data formatting | bytes 6291456
  102.6 3.9 %displacement.1 = f32[3,8,96,128]{3,2,1,0:T(8,128)} custom-call(f32[8,128]{1,0:T(8,128)} %get-tuple-element.243.factors, f32[3,8,128,128]{3,2,1,0:T(8,128)} %get-tuple-element.247.first, f32[3,8,128,128]{3,2,1,0:T(8,128)} %get-tuple-element.248.second), custom_call_target="tpu_custom_call" | custom-call | tf_op jit(solution)/shard_map/displacement/pallas_call | solution.py:698
  106.6 3.0 %finish.2 = f32[8,96,128]{2,1,0:T(8,128)} custom-call(f32[8,128]{1,0:T(8,128)} %get-tuple-element.243.factors, f32[8,96,128]{2,1,0:T(8,128)} %bitcast.134, s32[8,96,128]{2,1,0:T(8,128)S(1)} %bitcast.126, f32[8,96,128]{2,1,0:T(8,128)} %get-tuple-element.244.rest_0_, f32[8,96,128]{2,1,0:T(8,128)} %collective-permute-done.46.rest_1_, ...), custom_call_target="tpu_custom_call" | custom-call | tf_op jit(solution)/shard_map/finish/pallas_call | solution.py:677
  (32 shorter events, 1.6 us)
Async XLA Ops:
  0.6 7.7 %copy-start.14 = (s32[1,8,96,128]{3,2,1,0:T(8,128)S(1)}, s32[1,8,96,128]{3,2,1,0:T(8,128)}, u32[]{:S(2)}) copy-start(s32[1,8,96,128]{3,2,1,0:T(8,128)} %param.21) | copy-start | bytes 1179652
  2.9 22.2 %collective-permute-start.36 = (f32[9,96,128]{2,1,0:T(8,128)}, f32[9,96,128]{2,1,0:T(8,128)S(1)}, u32[]{:S(2)}, u32[]{:S(2)}) collective-permute-start(f32[9,96,128]{2,1,0:T(8,128)} %get-tuple-element.235), channel_id=1, source_target_pairs={{4,0},{8,4},{12,8},{1,12},{5,1},{9,5},{13,9},{2,13},{6,2},{10,6},{... | collective-permute-start | bytes 1327112 | tf_op jit(solution)/shard_map/ppermute | solution.py:487
  4.8 20.3 %collective-permute-start.35 = (f32[5,96,128]{2,1,0:T(8,128)}, f32[5,96,128]{2,1,0:T(8,128)S(1)}, u32[]{:S(2)}, u32[]{:S(2)}) collective-permute-start(f32[5,96,128]{2,1,0:T(8,128)} %get-tuple-element.234), channel_id=1, source_target_pairs={{0,4},{4,8},{8,12},{12,1},{1,5},{5,9},{9,13},{13,2},{2,6},{6,10},{... | collective-permute-start | bytes 737288 | tf_op jit(solution)/shard_map/ppermute | solution.py:487
  8.3 55.0 %copy-start.30 = (s32[2]{0:T(128)}, s32[2]{0:T(128)S(1)}, u32[]{:S(2)}) copy-start(s32[2]{0:T(128)S(1)} %pad_add_fusion.2.place) | copy-start | bytes 28
  12.4 12.8 %collective-permute-start.37 = (f32[5,8,2,128]{3,2,1,0:T(2,128)}, f32[5,8,2,128]{3,2,1,0:T(2,128)S(1)}, u32[]{:S(2)}, u32[]{:S(2)}) collective-permute-start(f32[5,8,2,128]{3,2,1,0:T(2,128)} %get-tuple-element.236), channel_id=1, source_target_pairs={{0,16},{4,20},{8,24},{12,28},{1,17},{5,21},{9,25},{13,29},{2,18},{... | collective-permute-start | bytes 122888 | tf_op jit(solution)/shard_map/ppermute | solution.py:504
  13.6 7.9 %collective-permute-start.38 = (f32[5,2,2,128]{3,2,1,0:T(2,128)}, f32[5,2,2,128]{3,2,1,0:T(2,128)S(1)}, u32[]{:S(2)}, u32[]{:S(2)}) collective-permute-start(f32[5,2,2,128]{3,2,1,0:T(2,128)} %get-tuple-element.237), channel_id=1, source_target_pairs={{0,20},{4,24},{8,28},{12,17},{1,21},{5,25},{9,29},{13,18},{2,22},{... | collective-permute-start | bytes 30728 | tf_op jit(solution)/shard_map/ppermute | solution.py:504
  16.7 8.4 %collective-permute-start.39 = (f32[5,2,2,128]{3,2,1,0:T(2,128)}, f32[5,2,2,128]{3,2,1,0:T(2,128)S(1)}, u32[]{:S(2)}, u32[]{:S(2)}) collective-permute-start(f32[5,2,2,128]{3,2,1,0:T(2,128)} %get-tuple-element.238), channel_id=1, source_target_pairs={{4,16},{8,20},{12,24},{1,28},{5,17},{9,21},{13,25},{2,29},{6,18},{... | collective-permute-start | bytes 30728 | tf_op jit(solution)/shard_map/ppermute | solution.py:504
  21.4 5.1 %copy-start.28 = (f32[5,2,2,128]{3,2,1,0:T(2,128)}, f32[5,2,2,128]{3,2,1,0:T(2,128)S(1)}, u32[]{:S(2)}) copy-start(f32[5,2,2,128]{3,2,1,0:T(2,128)S(1)} %collective-permute-done.38.left_up.right_up) | copy-start | bytes 30724
  25.1 1.5 %copy-start.29 = (f32[5,2,2,128]{3,2,1,0:T(2,128)}, f32[5,2,2,128]{3,2,1,0:T(2,128)S(1)}, u32[]{:S(2)}) copy-start(f32[5,2,2,128]{3,2,1,0:T(2,128)S(1)} %collective-permute-done.39.left_down.right_down) | copy-start | bytes 30724
  25.1 1.5 %copy-start.27 = (f32[5,8,2,128]{3,2,1,0:T(2,128)}, f32[5,8,2,128]{3,2,1,0:T(2,128)S(1)}, u32[]{:S(2)}) copy-start(f32[5,8,2,128]{3,2,1,0:T(2,128)S(1)} %collective-permute-done.37.left.right) | copy-start | bytes 122884
  25.1 0.7 copy-start.26
  25.8 0.8 copy-start.25
  26.6 73.1 %copy-start.16 = (f32[6,8,128,128]{3,2,1,0:T(8,128)S(1)}, f32[6,8,128,128]{3,2,1,0:T(8,128)}, u32[]{:S(2)}) copy-start(f32[6,8,128,128]{3,2,1,0:T(8,128)} %get-tuple-element.425.fields) | copy-start | bytes 9437188
  45.8 17.4 %collective-permute-start.45 = (f32[3,8,24,128]{3,2,1,0:T(8,128)}, f32[3,8,24,128]{3,2,1,0:T(8,128)}, u32[]{:S(2)}, u32[]{:S(2)}) collective-permute-start(f32[3,8,24,128]{3,2,1,0:T(8,128)} %get-tuple-element.241), channel_id=1, source_target_pairs={{0,16},{4,20},{8,24},{12,28},{1,17},{5,21},{9,25},{13,29},{2,18},{... | collective-permute-start | bytes 884744 | tf_op jit(solution)/shard_map/ppermute | solution.py:504
  46.1 2.5 %collective-permute-start.40 = (f32[8,128]{1,0:T(8,128)}, f32[8,128]{1,0:T(8,128)S(1)}, u32[]{:S(2)}, u32[]{:S(2)}) collective-permute-start(f32[8,128]{1,0:T(8,128)} %get-tuple-element.239), channel_id=1, source_target_pairs={{0,1},{1,0},{2,3},{3,2},{4,5},{5,4},{6,7},{7,6},{8,9},{9,8},{10,11... | collective-permute-start | bytes 12296 | tf_op jit(solution)/shard_map/ppermute | solution.py:517
  49.3 2.9 %collective-permute-start.41 = (f32[8,128]{1,0:T(8,128)S(1)}, f32[8,128]{1,0:T(8,128)S(1)}, u32[]{:S(2)}, u32[]{:S(2)}) collective-permute-start(f32[8,128]{1,0:T(8,128)S(1)} %add.275), channel_id=1, source_target_pairs={{0,2},{1,3},{2,0},{3,1},{4,6},{5,7},{6,4},{7,5},{8,10},{9,11},{10,... | collective-permute-start | bytes 12296 | tf_op jit(solution)/shard_map/ppermute | solution.py:517
  52.1 2.9 %collective-permute-start.42 = (f32[8,128]{1,0:T(8,128)S(1)}, f32[8,128]{1,0:T(8,128)S(1)}, u32[]{:S(2)}, u32[]{:S(2)}) collective-permute-start(f32[8,128]{1,0:T(8,128)S(1)} %add.276), channel_id=1, source_target_pairs={{0,4},{4,0},{8,12},{12,8},{1,5},{5,1},{9,13},{13,9},{2,6},{6,2},{1... | collective-permute-start | bytes 12296 | tf_op jit(solution)/shard_map/ppermute | solution.py:517
  55.0 5.1 %collective-permute-start.43 = (f32[8,128]{1,0:T(8,128)S(1)}, f32[8,128]{1,0:T(8,128)S(1)}, u32[]{:S(2)}, u32[]{:S(2)}) collective-permute-start(f32[8,128]{1,0:T(8,128)S(1)} %add.277), channel_id=1, source_target_pairs={{0,8},{4,12},{8,0},{12,4},{1,9},{5,13},{9,1},{13,5},{2,10},{6,14},... | collective-permute-start | bytes 12296 | tf_op jit(solution)/shard_map/ppermute | solution.py:517
  60.1 2.5 %collective-permute-start.44 = (f32[8,128]{1,0:T(8,128)S(1)}, f32[8,128]{1,0:T(8,128)S(1)}, u32[]{:S(2)}, u32[]{:S(2)}) collective-permute-start(f32[8,128]{1,0:T(8,128)S(1)} %add.278), channel_id=1, source_target_pairs={{0,16},{16,0},{1,17},{17,1},{2,18},{18,2},{3,19},{19,3},{4,20},{20... | collective-permute-start | bytes 12296 | tf_op jit(solution)/shard_map/ppermute | solution.py:517
  67.9 38.7 %collective-permute-start.46 = (f32[8,96,128]{2,1,0:T(8,128)}, f32[8,96,128]{2,1,0:T(8,128)}, u32[]{:S(2)}, u32[]{:S(2)}) collective-permute-start(f32[8,96,128]{2,1,0:T(8,128)} %get-tuple-element.244.rest_0_), channel_id=1, source_target_pairs={{0,12},{4,1},{8,5},{12,9},{1,13},{5,2},{9,6},{13,10},{2,14},{6,3},... | collective-permute-start | bytes 1179656 | tf_op jit(solution)/shard_map/ppermute | solution.py:487
  74.1 32.5 %collective-permute-start.47 = (f32[8,96,128]{2,1,0:T(8,128)}, f32[8,96,128]{2,1,0:T(8,128)}, u32[]{:S(2)}, u32[]{:S(2)}) collective-permute-start(f32[8,96,128]{2,1,0:T(8,128)} %get-tuple-element.244.rest_0_), channel_id=1, source_target_pairs={{12,0},{1,4},{5,8},{9,12},{13,1},{2,5},{6,9},{10,13},{14,2},{3,6},... | collective-permute-start | bytes 1179656 | tf_op jit(solution)/shard_map/ppermute | solution.py:487
  76.9 19.1 %collective-permute-start.51 = (f32[96,128]{1,0:T(8,128)}, f32[96,128]{1,0:T(8,128)}, u32[]{:S(2)}, u32[]{:S(2)}) collective-permute-start(f32[96,128]{1,0:T(8,128)} %get-tuple-element.246), channel_id=1, source_target_pairs={{8,0},{12,4},{1,8},{5,12},{9,1},{13,5},{2,9},{6,13},{10,2},{14,6},... | collective-permute-start | bytes 147464 | tf_op jit(solution)/shard_map/ppermute | solution.py:487
  84.7 21.9 %collective-permute-start.49 = (f32[96,128]{1,0:T(8,128)}, f32[96,128]{1,0:T(8,128)}, u32[]{:S(2)}, u32[]{:S(2)}) collective-permute-start(f32[96,128]{1,0:T(8,128)} %get-tuple-element.246), channel_id=1, source_target_pairs={{4,0},{8,4},{12,8},{1,12},{5,1},{9,5},{13,9},{2,13},{6,2},{10,6},{... | collective-permute-start | bytes 147464 | tf_op jit(solution)/shard_map/ppermute | solution.py:487
  86.6 19.9 %collective-permute-start.48 = (f32[96,128]{1,0:T(8,128)}, f32[96,128]{1,0:T(8,128)}, u32[]{:S(2)}, u32[]{:S(2)}) collective-permute-start(f32[96,128]{1,0:T(8,128)} %get-tuple-element.245), channel_id=1, source_target_pairs={{0,4},{4,8},{8,12},{12,1},{1,5},{5,9},{9,13},{13,2},{2,6},{6,10},{... | collective-permute-start | bytes 147464 | tf_op jit(solution)/shard_map/ppermute | solution.py:487
  96.0 10.6 %collective-permute-start.50 = (f32[96,128]{1,0:T(8,128)}, f32[96,128]{1,0:T(8,128)}, u32[]{:S(2)}, u32[]{:S(2)}) collective-permute-start(f32[96,128]{1,0:T(8,128)} %get-tuple-element.245), channel_id=1, source_target_pairs={{0,8},{4,12},{8,1},{12,5},{1,9},{5,13},{9,2},{13,6},{2,10},{6,14},... | collective-permute-start | bytes 147464 | tf_op jit(solution)/shard_map/ppermute | solution.py:487

commit v7 on v6

--- a/solution.py
+++ b/solution.py
@@ -597,6 +597,18 @@
     return by_first, by_second, squares, total, jnp.where(sound, 1.0, 0.0)
 
 
+def split(value):
+    high = value.astype(jnp.bfloat16)
+    return high, (value - high.astype(jnp.float32)).astype(jnp.bfloat16)
+
+
+def split_dot(a, b, side):
+    dot = lambda p, q: lax.dot_general(
+        p, q, (((1,), (side,)), ((), ())), preferred_element_type=jnp.float32
+    )
+    return dot(a[0], b[0]) + (dot(a[0], b[1]) + dot(a[1], b[0]))
+
+
 def smooth_kernel(
     plain, cells, nx, place, stats, basis, left, right, along_x, along_y, planar, low, high, factors, verdict
 ):
@@ -604,7 +616,7 @@
     on_right = jnp.where(place[0] < nx - 1, 1.0, 0.0)
     depth = basis.shape[1]
     decay = depth_decay(depth)
-    exact = dict(precision=lax.Precision.HIGHEST, preferred_element_type=jnp.float32)
+    matrix_x, matrix_y = split(along_x[...]), split(along_y[...])
     tile = stats[...]
     sums = [jnp.sum(tile[i : i + 1], axis=1, keepdims=True) for i in range(8)]
     if plain:
@@ -625,8 +637,8 @@
             ],
             axis=0,
         )
-        half = lax.dot_general(along_x[...], wide, (((1,), (0,)), ((), ())), **exact)
-        plane = lax.dot_general(along_y[...], half, (((1,), (1,)), ((), ())), **exact)
+        half = split_dot(matrix_x, split(wide), 0)
+        plane = split_dot(matrix_y, split(half), 1)
         planar[z] = plane
         for ref, weight in ((low, decay[z]), (high, decay[depth - 1 - z])):
             share = plane * float(weight)

time: 110 us -> 109 us (level)
  no operation moved by 1% of the time
where the time goes in v7:
time: 109 us
  starting transfers between devices  46.6 us (43%)
  Pallas kernels  36.2 us (33%)
  waiting for transfers between devices  19.3 us (18%)
  local copies, waits for them, and re-layouts  3.86 us (4%)
  other arithmetic  1.36 us (1%)
  between operations  1.36 us (1%)
    ppermute x8, starting transfers between devices, to_slab(): return lax.ppermute(value, ('gx', 'gy', 'gz'), slab_route(steps, sideways))  31 us
    pallas_call x1, Pallas kernels, run_krylov(): pl.pallas_call(functools.partial(krylov_kernel, mode_constants(table), fl...  19.2 us
    ppermute x5, waiting for transfers between devices, total_over_mesh(): other = lax.ppermute(value, axis, [(i, i ^ step) for i in range(count)])  8.16 us
    ppermute x4, starting transfers between devices, edges_moved(): got = lax.ppermute(sent[0], ('gx', 'gy', 'gz'), spots)  7.85 us
    ppermute x5, starting transfers between devices, total_over_mesh(): other = lax.ppermute(value, axis, [(i, i ^ step) for i in range(count)])  7.73 us
    ppermute x8, waiting for transfers between devices, to_slab(): return lax.ppermute(value, ('gx', 'gy', 'gz'), slab_route(steps, sideways))  6 us
    ppermute x4, waiting for transfers between devices, edges_moved(): got = lax.ppermute(sent[0], ('gx', 'gy', 'gz'), spots)  5.15 us
    pallas_call x1, Pallas kernels, run_prepare(): pl.pallas_call(functools.partial(prepare_kernel, swap), in_specs=[SCALAR]...  4.07 us
  transfers between devices with their start and end apart: 17, of which 8 were waited for; matrix products, arithmetic and copies ran while one was open for 3% of the time, Pallas kernels for 7%

profile of v7, /device:TPU:9, one launch (start us, length us, event | category | flops | bytes accessed | tf_op | source)
XLA Modules:
  0.0 108.6 jit_solution(10444919734169662438)
XLA Ops:
  0.6 2.3 %messages.1 = (f32[5,96,128]{2,1,0:T(8,128)}, f32[9,96,128]{2,1,0:T(8,128)}) custom-call(f32[8,96,128]{2,1,0:T(8,128)} %bitcast.131, f32[8,96,128]{2,1,0:T(8,128)} %bitcast.132, s32[8,96,128]{2,1,0:T(8,128)} %bitcast.123, s32[8,96,128]{2,1,0:T(8,128)} %bitcast.124, s32[8,96,128]{2,1,0:T(8,128)} %bitcast.135, s32[8,96,128]{2,1,0:T(8,128)} %bitcast.136, ...), custom_call_target="tpu_custom_call" | custom-call | tf_op jit(solution)/shard_map/messages/pallas_call | solution.py:415
  2.9 1.9 %collective-permute-start.36 = (f32[9,96,128]{2,1,0:T(8,128)}, f32[9,96,128]{2,1,0:T(8,128)S(1)}, u32[]{:S(2)}, u32[]{:S(2)}) collective-permute-start(f32[9,96,128]{2,1,0:T(8,128)} %get-tuple-element.235), channel_id=1, source_target_pairs={{4,0},{8,4},{12,8},{1,12},{5,1},{9,5},{13,9},{2,13},{6,2},{10,6},{... | collective-permute-start | bytes 1327112 | tf_op jit(solution)/shard_map/ppermute | solution.py:487
  4.8 3.4 %collective-permute-start.35 = (f32[5,96,128]{2,1,0:T(8,128)}, f32[5,96,128]{2,1,0:T(8,128)S(1)}, u32[]{:S(2)}, u32[]{:S(2)}) collective-permute-start(f32[5,96,128]{2,1,0:T(8,128)} %get-tuple-element.234), channel_id=1, source_target_pairs={{0,4},{4,8},{8,12},{12,1},{1,5},{5,9},{9,13},{13,2},{2,6},{6,10},{... | collective-permute-start | bytes 737288 | tf_op jit(solution)/shard_map/ppermute | solution.py:487
  8.3 4.1 %prepare.1 = (f32[6,8,128,128]{3,2,1,0:T(8,128)}, f32[5,8,2,128]{3,2,1,0:T(2,128)}, f32[5,2,2,128]{3,2,1,0:T(2,128)}, f32[5,2,2,128]{3,2,1,0:T(2,128)}) custom-call(s32[2]{0:T(128)S(1)} %pad_add_fusion.2.place, f32[8,96,128]{2,1,0:T(8,128)} %bitcast.133, s32[8,96,128]{2,1,0:T(8,128)S(1)} %bitcast.125, s32[8,96,128]{2,1,0:T(8,128)} %bitcast.137, ...), custom_call_target="tpu_custom_call" | custom-call | tf_op jit(solution)/shard_map/prepare/pallas_call | solution.py:435
  12.4 1.2 %collective-permute-start.37 = (f32[5,8,2,128]{3,2,1,0:T(2,128)}, f32[5,8,2,128]{3,2,1,0:T(2,128)S(1)}, u32[]{:S(2)}, u32[]{:S(2)}) collective-permute-start(f32[5,8,2,128]{3,2,1,0:T(2,128)} %get-tuple-element.236), channel_id=1, source_target_pairs={{0,16},{4,20},{8,24},{12,28},{1,17},{5,21},{9,25},{13,29},{2,18},{... | collective-permute-start | bytes 122888 | tf_op jit(solution)/shard_map/ppermute | solution.py:504
  13.6 3.2 %collective-permute-start.38 = (f32[5,2,2,128]{3,2,1,0:T(2,128)}, f32[5,2,2,128]{3,2,1,0:T(2,128)S(1)}, u32[]{:S(2)}, u32[]{:S(2)}) collective-permute-start(f32[5,2,2,128]{3,2,1,0:T(2,128)} %get-tuple-element.237), channel_id=1, source_target_pairs={{0,20},{4,24},{8,28},{12,17},{1,21},{5,25},{9,29},{13,18},{2,22},{... | collective-permute-start | bytes 30728 | tf_op jit(solution)/shard_map/ppermute | solution.py:504
  16.7 3.2 %collective-permute-start.39 = (f32[5,2,2,128]{3,2,1,0:T(2,128)}, f32[5,2,2,128]{3,2,1,0:T(2,128)S(1)}, u32[]{:S(2)}, u32[]{:S(2)}) collective-permute-start(f32[5,2,2,128]{3,2,1,0:T(2,128)} %get-tuple-element.238), channel_id=1, source_target_pairs={{4,16},{8,20},{12,24},{1,28},{5,17},{9,21},{13,25},{2,29},{6,18},{... | collective-permute-start | bytes 30728 | tf_op jit(solution)/shard_map/ppermute | solution.py:504
  20.0 1.5 %collective-permute-done.38.left_up.right_up = f32[5,2,2,128]{3,2,1,0:T(2,128)S(1)} collective-permute-done((f32[5,2,2,128]{3,2,1,0:T(2,128)}, f32[5,2,2,128]{3,2,1,0:T(2,128)S(1)}, u32[]{:S(2)}, u32[]{:S(2)}) %collective-permute-start.38) | collective-permute-done | bytes 10272 | tf_op jit(solution)/shard_map/ppermute | solution.py:504
  21.4 3.7 %collective-permute-done.39.left_down.right_down = f32[5,2,2,128]{3,2,1,0:T(2,128)S(1)} collective-permute-done((f32[5,2,2,128]{3,2,1,0:T(2,128)}, f32[5,2,2,128]{3,2,1,0:T(2,128)S(1)}, u32[]{:S(2)}, u32[]{:S(2)}) %collective-permute-start.39) | collective-permute-done | bytes 10272 | tf_op jit(solution)/shard_map/ppermute | solution.py:504
  25.1 0.7 copy-done.26
  25.8 0.8 copy-done.25
  26.6 19.2 %krylov.1 = (f32[3,8,128,128]{3,2,1,0:T(8,128)}, f32[3,8,128,128]{3,2,1,0:T(8,128)}, f32[3,8,128,128]{3,2,1,0:T(8,128)}, f32[8,128]{1,0:T(8,128)}, f32[3,8,24,128]{3,2,1,0:T(8,128)}) custom-call(s32[2]{0:T(128)S(1)} %pad_add_fusion.2.place, f32[128]{0:T(128)} %constant.85.clone.cover_z, f32[6,8,128,128]{3,2,1,0:T(8,128)} %get-tuple-element.425.fields, ...), custom_call_target="tpu_custom_call" | custom-call | tf_op jit(solution)/shard_map/krylov/pallas_call | solution.py:463
  46.1 1.5 %collective-permute-start.40 = (f32[8,128]{1,0:T(8,128)}, f32[8,128]{1,0:T(8,128)S(1)}, u32[]{:S(2)}, u32[]{:S(2)}) collective-permute-start(f32[8,128]{1,0:T(8,128)} %get-tuple-element.239), channel_id=1, source_target_pairs={{0,1},{1,0},{2,3},{3,2},{4,5},{5,4},{6,7},{7,6},{8,9},{9,8},{10,11... | collective-permute-start | bytes 12296 | tf_op jit(solution)/shard_map/ppermute | solution.py:517
  47.6 1.0 collective-permute-done.40
  48.6 0.7 add.275
  49.3 1.5 %collective-permute-start.41 = (f32[8,128]{1,0:T(8,128)S(1)}, f32[8,128]{1,0:T(8,128)S(1)}, u32[]{:S(2)}, u32[]{:S(2)}) collective-permute-start(f32[8,128]{1,0:T(8,128)S(1)} %add.275), channel_id=1, source_target_pairs={{0,2},{1,3},{2,0},{3,1},{4,6},{5,7},{6,4},{7,5},{8,10},{9,11},{10,... | collective-permute-start | bytes 12296 | tf_op jit(solution)/shard_map/ppermute | solution.py:517
  50.7 1.4 %collective-permute-done.41 = f32[8,128]{1,0:T(8,128)S(1)} collective-permute-done((f32[8,128]{1,0:T(8,128)S(1)}, f32[8,128]{1,0:T(8,128)S(1)}, u32[]{:S(2)}, u32[]{:S(2)}) %collective-permute-start.41) | collective-permute-done | bytes 4128 | tf_op jit(solution)/shard_map/ppermute | solution.py:517
  52.6 2.5 %collective-permute-done.42 = f32[8,128]{1,0:T(8,128)S(1)} collective-permute-done((f32[8,128]{1,0:T(8,128)S(1)}, f32[8,128]{1,0:T(8,128)S(1)}, u32[]{:S(2)}, u32[]{:S(2)}) %collective-permute-start.42) | collective-permute-done | bytes 4128 | tf_op jit(solution)/shard_map/ppermute | solution.py:517
  55.0 4.1 %collective-permute-start.43 = (f32[8,128]{1,0:T(8,128)S(1)}, f32[8,128]{1,0:T(8,128)S(1)}, u32[]{:S(2)}, u32[]{:S(2)}) collective-permute-start(f32[8,128]{1,0:T(8,128)S(1)} %add.277), channel_id=1, source_target_pairs={{0,8},{4,12},{8,0},{12,4},{1,9},{5,13},{9,1},{13,5},{2,10},{6,14},... | collective-permute-start | bytes 12296 | tf_op jit(solution)/shard_map/ppermute | solution.py:517
  59.1 1.0 collective-permute-done.43
  60.4 2.3 %collective-permute-done.44 = f32[8,128]{1,0:T(8,128)S(1)} collective-permute-done((f32[8,128]{1,0:T(8,128)S(1)}, f32[8,128]{1,0:T(8,128)S(1)}, u32[]{:S(2)}, u32[]{:S(2)}) %collective-permute-start.44) | collective-permute-done | bytes 4128 | tf_op jit(solution)/shard_map/ppermute | solution.py:517
  63.3 3.7 %smooth.2 = (f32[8,96,128]{2,1,0:T(8,128)}, f32[96,128]{1,0:T(8,128)}, f32[96,128]{1,0:T(8,128)}, f32[8,128]{1,0:T(8,128)}, f32[1,1]{1,0:T(1,128)}) custom-call(s32[2]{0:T(128)S(1)} %pad_add_fusion.2.place, f32[8,128]{1,0:T(8,128)} %add.279.stats, f32[3,8,128,128]{3,2,1,0:T(8,128)} %get-tuple-element.240.basis, ...), custom_call_target="tpu_custom_call" | custom-call | tf_op jit(solution)/shard_map/smooth/pallas_call | solution.py:654
  66.9 6.2 %collective-permute-start.46 = (f32[8,96,128]{2,1,0:T(8,128)}, f32[8,96,128]{2,1,0:T(8,128)}, u32[]{:S(2)}, u32[]{:S(2)}) collective-permute-start(f32[8,96,128]{2,1,0:T(8,128)} %get-tuple-element.244.rest_0_), channel_id=1, source_target_pairs={{0,12},{4,1},{8,5},{12,9},{1,13},{5,2},{9,6},{13,10},{2,14},{6,3},... | collective-permute-start | bytes 1179656 | tf_op jit(solution)/shard_map/ppermute | solution.py:487
  73.2 2.8 %collective-permute-start.47 = (f32[8,96,128]{2,1,0:T(8,128)}, f32[8,96,128]{2,1,0:T(8,128)}, u32[]{:S(2)}, u32[]{:S(2)}) collective-permute-start(f32[8,96,128]{2,1,0:T(8,128)} %get-tuple-element.244.rest_0_), channel_id=1, source_target_pairs={{12,0},{1,4},{5,8},{9,12},{13,1},{2,5},{6,9},{10,13},{14,2},{3,6},... | collective-permute-start | bytes 1179656 | tf_op jit(solution)/shard_map/ppermute | solution.py:487
  76.0 7.8 %collective-permute-start.51 = (f32[96,128]{1,0:T(8,128)}, f32[96,128]{1,0:T(8,128)}, u32[]{:S(2)}, u32[]{:S(2)}) collective-permute-start(f32[96,128]{1,0:T(8,128)} %get-tuple-element.246), channel_id=1, source_target_pairs={{8,0},{12,4},{1,8},{5,12},{9,1},{13,5},{2,9},{6,13},{10,2},{14,6},... | collective-permute-start | bytes 147464 | tf_op jit(solution)/shard_map/ppermute | solution.py:487
  83.8 1.9 %collective-permute-start.49 = (f32[96,128]{1,0:T(8,128)}, f32[96,128]{1,0:T(8,128)}, u32[]{:S(2)}, u32[]{:S(2)}) collective-permute-start(f32[96,128]{1,0:T(8,128)} %get-tuple-element.246), channel_id=1, source_target_pairs={{4,0},{8,4},{12,8},{1,12},{5,1},{9,5},{13,9},{2,13},{6,2},{10,6},{... | collective-permute-start | bytes 147464 | tf_op jit(solution)/shard_map/ppermute | solution.py:487
  85.7 3.4 %collective-permute-start.48 = (f32[96,128]{1,0:T(8,128)}, f32[96,128]{1,0:T(8,128)}, u32[]{:S(2)}, u32[]{:S(2)}) collective-permute-start(f32[96,128]{1,0:T(8,128)} %get-tuple-element.245), channel_id=1, source_target_pairs={{0,4},{4,8},{8,12},{12,1},{1,5},{5,9},{9,13},{13,2},{2,6},{6,10},{... | collective-permute-start | bytes 147464 | tf_op jit(solution)/shard_map/ppermute | solution.py:487
  89.1 6.0 %collective-permute-done.51 = f32[96,128]{1,0:T(8,128)} collective-permute-done((f32[96,128]{1,0:T(8,128)}, f32[96,128]{1,0:T(8,128)}, u32[]{:S(2)}, u32[]{:S(2)}) %collective-permute-start.51) | collective-permute-done | bytes 49184 | tf_op jit(solution)/shard_map/ppermute | solution.py:487
  95.1 3.6 %collective-permute-start.50 = (f32[96,128]{1,0:T(8,128)}, f32[96,128]{1,0:T(8,128)}, u32[]{:S(2)}, u32[]{:S(2)}) collective-permute-start(f32[96,128]{1,0:T(8,128)} %get-tuple-element.245), channel_id=1, source_target_pairs={{0,8},{4,12},{8,1},{12,5},{1,9},{5,13},{9,2},{13,6},{2,10},{6,14},... | collective-permute-start | bytes 147464 | tf_op jit(solution)/shard_map/ppermute | solution.py:487
  98.7 2.4 %copy.67 = f32[6,8,128,128]{2,3,1,0:T(8,128)} copy(f32[6,8,128,128]{3,2,1,0:T(8,128)S(1)} %copy-done.16) | data formatting | bytes 6291456
  101.7 3.9 %displacement.1 = f32[3,8,96,128]{3,2,1,0:T(8,128)} custom-call(f32[8,128]{1,0:T(8,128)} %get-tuple-element.243.factors, f32[3,8,128,128]{3,2,1,0:T(8,128)} %get-tuple-element.247.first, f32[3,8,128,128]{3,2,1,0:T(8,128)} %get-tuple-element.248.second), custom_call_target="tpu_custom_call" | custom-call | tf_op jit(solution)/shard_map/displacement/pallas_call | solution.py:710
  105.7 3.0 %finish.2 = f32[8,96,128]{2,1,0:T(8,128)} custom-call(f32[8,128]{1,0:T(8,128)} %get-tuple-element.243.factors, f32[8,96,128]{2,1,0:T(8,128)} %bitcast.134, s32[8,96,128]{2,1,0:T(8,128)S(1)} %bitcast.126, f32[8,96,128]{2,1,0:T(8,128)} %get-tuple-element.244.rest_0_, f32[8,96,128]{2,1,0:T(8,128)} %collective-permute-done.46.rest_1_, ...), custom_call_target="tpu_custom_call" | custom-call | tf_op jit(solution)/shard_map/finish/pallas_call | solution.py:689
  (32 shorter events, 1.6 us)
Async XLA Ops:
  0.6 7.7 %copy-start.14 = (s32[1,8,96,128]{3,2,1,0:T(8,128)S(1)}, s32[1,8,96,128]{3,2,1,0:T(8,128)}, u32[]{:S(2)}) copy-start(s32[1,8,96,128]{3,2,1,0:T(8,128)} %param.21) | copy-start | bytes 1179652
  2.9 22.2 %collective-permute-start.36 = (f32[9,96,128]{2,1,0:T(8,128)}, f32[9,96,128]{2,1,0:T(8,128)S(1)}, u32[]{:S(2)}, u32[]{:S(2)}) collective-permute-start(f32[9,96,128]{2,1,0:T(8,128)} %get-tuple-element.235), channel_id=1, source_target_pairs={{4,0},{8,4},{12,8},{1,12},{5,1},{9,5},{13,9},{2,13},{6,2},{10,6},{... | collective-permute-start | bytes 1327112 | tf_op jit(solution)/shard_map/ppermute | solution.py:487
  4.8 20.3 %collective-permute-start.35 = (f32[5,96,128]{2,1,0:T(8,128)}, f32[5,96,128]{2,1,0:T(8,128)S(1)}, u32[]{:S(2)}, u32[]{:S(2)}) collective-permute-start(f32[5,96,128]{2,1,0:T(8,128)} %get-tuple-element.234), channel_id=1, source_target_pairs={{0,4},{4,8},{8,12},{12,1},{1,5},{5,9},{9,13},{13,2},{2,6},{6,10},{... | collective-permute-start | bytes 737288 | tf_op jit(solution)/shard_map/ppermute | solution.py:487
  8.3 55.0 %copy-start.30 = (s32[2]{0:T(128)}, s32[2]{0:T(128)S(1)}, u32[]{:S(2)}) copy-start(s32[2]{0:T(128)S(1)} %pad_add_fusion.2.place) | copy-start | bytes 28
  12.4 12.8 %collective-permute-start.37 = (f32[5,8,2,128]{3,2,1,0:T(2,128)}, f32[5,8,2,128]{3,2,1,0:T(2,128)S(1)}, u32[]{:S(2)}, u32[]{:S(2)}) collective-permute-start(f32[5,8,2,128]{3,2,1,0:T(2,128)} %get-tuple-element.236), channel_id=1, source_target_pairs={{0,16},{4,20},{8,24},{12,28},{1,17},{5,21},{9,25},{13,29},{2,18},{... | collective-permute-start | bytes 122888 | tf_op jit(solution)/shard_map/ppermute | solution.py:504
  13.6 7.9 %collective-permute-start.38 = (f32[5,2,2,128]{3,2,1,0:T(2,128)}, f32[5,2,2,128]{3,2,1,0:T(2,128)S(1)}, u32[]{:S(2)}, u32[]{:S(2)}) collective-permute-start(f32[5,2,2,128]{3,2,1,0:T(2,128)} %get-tuple-element.237), channel_id=1, source_target_pairs={{0,20},{4,24},{8,28},{12,17},{1,21},{5,25},{9,29},{13,18},{2,22},{... | collective-permute-start | bytes 30728 | tf_op jit(solution)/shard_map/ppermute | solution.py:504
  16.7 8.4 %collective-permute-start.39 = (f32[5,2,2,128]{3,2,1,0:T(2,128)}, f32[5,2,2,128]{3,2,1,0:T(2,128)S(1)}, u32[]{:S(2)}, u32[]{:S(2)}) collective-permute-start(f32[5,2,2,128]{3,2,1,0:T(2,128)} %get-tuple-element.238), channel_id=1, source_target_pairs={{4,16},{8,20},{12,24},{1,28},{5,17},{9,21},{13,25},{2,29},{6,18},{... | collective-permute-start | bytes 30728 | tf_op jit(solution)/shard_map/ppermute | solution.py:504
  21.4 5.1 %copy-start.28 = (f32[5,2,2,128]{3,2,1,0:T(2,128)}, f32[5,2,2,128]{3,2,1,0:T(2,128)S(1)}, u32[]{:S(2)}) copy-start(f32[5,2,2,128]{3,2,1,0:T(2,128)S(1)} %collective-permute-done.38.left_up.right_up) | copy-start | bytes 30724
  25.1 1.5 %copy-start.29 = (f32[5,2,2,128]{3,2,1,0:T(2,128)}, f32[5,2,2,128]{3,2,1,0:T(2,128)S(1)}, u32[]{:S(2)}) copy-start(f32[5,2,2,128]{3,2,1,0:T(2,128)S(1)} %collective-permute-done.39.left_down.right_down) | copy-start | bytes 30724
  25.1 1.5 %copy-start.27 = (f32[5,8,2,128]{3,2,1,0:T(2,128)}, f32[5,8,2,128]{3,2,1,0:T(2,128)S(1)}, u32[]{:S(2)}) copy-start(f32[5,8,2,128]{3,2,1,0:T(2,128)S(1)} %collective-permute-done.37.left.right) | copy-start | bytes 122884
  25.1 0.7 copy-start.26
  25.8 0.8 copy-start.25
  26.6 72.1 %copy-start.16 = (f32[6,8,128,128]{3,2,1,0:T(8,128)S(1)}, f32[6,8,128,128]{3,2,1,0:T(8,128)}, u32[]{:S(2)}) copy-start(f32[6,8,128,128]{3,2,1,0:T(8,128)} %get-tuple-element.425.fields) | copy-start | bytes 9437188
  45.8 17.4 %collective-permute-start.45 = (f32[3,8,24,128]{3,2,1,0:T(8,128)}, f32[3,8,24,128]{3,2,1,0:T(8,128)}, u32[]{:S(2)}, u32[]{:S(2)}) collective-permute-start(f32[3,8,24,128]{3,2,1,0:T(8,128)} %get-tuple-element.241), channel_id=1, source_target_pairs={{0,16},{4,20},{8,24},{12,28},{1,17},{5,21},{9,25},{13,29},{2,18},{... | collective-permute-start | bytes 884744 | tf_op jit(solution)/shard_map/ppermute | solution.py:504
  46.1 2.5 %collective-permute-start.40 = (f32[8,128]{1,0:T(8,128)}, f32[8,128]{1,0:T(8,128)S(1)}, u32[]{:S(2)}, u32[]{:S(2)}) collective-permute-start(f32[8,128]{1,0:T(8,128)} %get-tuple-element.239), channel_id=1, source_target_pairs={{0,1},{1,0},{2,3},{3,2},{4,5},{5,4},{6,7},{7,6},{8,9},{9,8},{10,11... | collective-permute-start | bytes 12296 | tf_op jit(solution)/shard_map/ppermute | solution.py:517
  49.3 2.9 %collective-permute-start.41 = (f32[8,128]{1,0:T(8,128)S(1)}, f32[8,128]{1,0:T(8,128)S(1)}, u32[]{:S(2)}, u32[]{:S(2)}) collective-permute-start(f32[8,128]{1,0:T(8,128)S(1)} %add.275), channel_id=1, source_target_pairs={{0,2},{1,3},{2,0},{3,1},{4,6},{5,7},{6,4},{7,5},{8,10},{9,11},{10,... | collective-permute-start | bytes 12296 | tf_op jit(solution)/shard_map/ppermute | solution.py:517
  52.1 2.9 %collective-permute-start.42 = (f32[8,128]{1,0:T(8,128)S(1)}, f32[8,128]{1,0:T(8,128)S(1)}, u32[]{:S(2)}, u32[]{:S(2)}) collective-permute-start(f32[8,128]{1,0:T(8,128)S(1)} %add.276), channel_id=1, source_target_pairs={{0,4},{4,0},{8,12},{12,8},{1,5},{5,1},{9,13},{13,9},{2,6},{6,2},{1... | collective-permute-start | bytes 12296 | tf_op jit(solution)/shard_map/ppermute | solution.py:517
  55.0 5.1 %collective-permute-start.43 = (f32[8,128]{1,0:T(8,128)S(1)}, f32[8,128]{1,0:T(8,128)S(1)}, u32[]{:S(2)}, u32[]{:S(2)}) collective-permute-start(f32[8,128]{1,0:T(8,128)S(1)} %add.277), channel_id=1, source_target_pairs={{0,8},{4,12},{8,0},{12,4},{1,9},{5,13},{9,1},{13,5},{2,10},{6,14},... | collective-permute-start | bytes 12296 | tf_op jit(solution)/shard_map/ppermute | solution.py:517
  60.1 2.5 %collective-permute-start.44 = (f32[8,128]{1,0:T(8,128)S(1)}, f32[8,128]{1,0:T(8,128)S(1)}, u32[]{:S(2)}, u32[]{:S(2)}) collective-permute-start(f32[8,128]{1,0:T(8,128)S(1)} %add.278), channel_id=1, source_target_pairs={{0,16},{16,0},{1,17},{17,1},{2,18},{18,2},{3,19},{19,3},{4,20},{20... | collective-permute-start | bytes 12296 | tf_op jit(solution)/shard_map/ppermute | solution.py:517
  66.9 38.7 %collective-permute-start.46 = (f32[8,96,128]{2,1,0:T(8,128)}, f32[8,96,128]{2,1,0:T(8,128)}, u32[]{:S(2)}, u32[]{:S(2)}) collective-permute-start(f32[8,96,128]{2,1,0:T(8,128)} %get-tuple-element.244.rest_0_), channel_id=1, source_target_pairs={{0,12},{4,1},{8,5},{12,9},{1,13},{5,2},{9,6},{13,10},{2,14},{6,3},... | collective-permute-start | bytes 1179656 | tf_op jit(solution)/shard_map/ppermute | solution.py:487
  73.2 32.5 %collective-permute-start.47 = (f32[8,96,128]{2,1,0:T(8,128)}, f32[8,96,128]{2,1,0:T(8,128)}, u32[]{:S(2)}, u32[]{:S(2)}) collective-permute-start(f32[8,96,128]{2,1,0:T(8,128)} %get-tuple-element.244.rest_0_), channel_id=1, source_target_pairs={{12,0},{1,4},{5,8},{9,12},{13,1},{2,5},{6,9},{10,13},{14,2},{3,6},... | collective-permute-start | bytes 1179656 | tf_op jit(solution)/shard_map/ppermute | solution.py:487
  76.0 19.1 %collective-permute-start.51 = (f32[96,128]{1,0:T(8,128)}, f32[96,128]{1,0:T(8,128)}, u32[]{:S(2)}, u32[]{:S(2)}) collective-permute-start(f32[96,128]{1,0:T(8,128)} %get-tuple-element.246), channel_id=1, source_target_pairs={{8,0},{12,4},{1,8},{5,12},{9,1},{13,5},{2,9},{6,13},{10,2},{14,6},... | collective-permute-start | bytes 147464 | tf_op jit(solution)/shard_map/ppermute | solution.py:487
  83.8 21.8 %collective-permute-start.49 = (f32[96,128]{1,0:T(8,128)}, f32[96,128]{1,0:T(8,128)}, u32[]{:S(2)}, u32[]{:S(2)}) collective-permute-start(f32[96,128]{1,0:T(8,128)} %get-tuple-element.246), channel_id=1, source_target_pairs={{4,0},{8,4},{12,8},{1,12},{5,1},{9,5},{13,9},{2,13},{6,2},{10,6},{... | collective-permute-start | bytes 147464 | tf_op jit(solution)/shard_map/ppermute | solution.py:487
  85.7 19.9 %collective-permute-start.48 = (f32[96,128]{1,0:T(8,128)}, f32[96,128]{1,0:T(8,128)}, u32[]{:S(2)}, u32[]{:S(2)}) collective-permute-start(f32[96,128]{1,0:T(8,128)} %get-tuple-element.245), channel_id=1, source_target_pairs={{0,4},{4,8},{8,12},{12,1},{1,5},{5,9},{9,13},{13,2},{2,6},{6,10},{... | collective-permute-start | bytes 147464 | tf_op jit(solution)/shard_map/ppermute | solution.py:487
  95.1 10.6 %collective-permute-start.50 = (f32[96,128]{1,0:T(8,128)}, f32[96,128]{1,0:T(8,128)}, u32[]{:S(2)}, u32[]{:S(2)}) collective-permute-start(f32[96,128]{1,0:T(8,128)} %get-tuple-element.245), channel_id=1, source_target_pairs={{0,8},{4,12},{8,1},{12,5},{1,9},{5,13},{9,2},{13,6},{2,10},{6,14},... | collective-permute-start | bytes 147464 | tf_op jit(solution)/shard_map/ppermute | solution.py:487
